TPU v7x, 32 devices: a whole 2x2x4 slice. The times are simulated.
32 devices in a mesh: groups: 2 (over y), ep: 4 (over z), side: 2 (over core), head: 2 (over x).
Axes of the slice: x: 2, y: 2, z: 4, core: 2. Of those that a mesh axis runs over, the one named last changes fastest.
Arguments:
- hidden: bfloat16 [64, 2048], P(('groups', 'ep')), parts along dimension 0, may hold values from -6 to 6
- query: bfloat16 [64, 4, 1024], P(('groups', 'ep'), 'head', 'side'), parts along dimension 0, may hold values from -6 to 6
- new_key: bfloat16 [64, 512], P(('groups', 'ep'), 'head'), parts along dimension 0, may hold values from -220 to 220
- new_value: bfloat16 [64, 512], P(('groups', 'ep'), 'head'), parts along dimension 0, may hold values from -6 to 6
- cache_keys: bfloat16 [64, 128, 512], P(('groups', 'ep'), None, 'head'), parts along dimension 0, may hold values from -220 to 220
- cache_values: bfloat16 [64, 128, 512], P(('groups', 'ep'), None, 'head'), parts along dimension 0, may hold values from -6 to 6
- lengths: int32 [64], P(('groups', 'ep')), parts along dimension 0, may hold values from 1 to 128, 1024 in all
- out_weight: bfloat16 [4, 1024, 2048], P('head', 'side'), may hold values from -0.14 to 0.14
- norm_gain: float32 [2048], replicated, may hold values from 0.5 to 1.5
- expert_ids: int32 [64, 8], P(('groups', 'ep')), parts along dimension 0, may hold values from 0 to 63, all different within a row; in each aligned block of 8 rows (0 to 7, 8 to 15, ...) at most 2 rows name the same one
- route_weights: float32 [64, 8], P(('groups', 'ep')), parts along dimension 0, may hold values from 0.25 to 1
- gate_weight: bfloat16 [64, 2048, 768], P(('ep', 'side'), None, 'head'), may hold values from -0.125 to 0.125
- up_weight: bfloat16 [64, 2048, 768], P(('ep', 'side'), None, 'head'), may hold values from -0.125 to 0.125
- down_weight: bfloat16 [64, 768, 2048], P(('ep', 'side'), 'head'), may hold values from -0.21875 to 0.21875
Outputs:
- after_attention: float32 [64, 2048], P(('groups', 'ep'), 'head'), parts along dimension 0
- expert_sum: bfloat16 [64, 2048], P(('groups', 'ep'), 'head'), parts along dimension 0
There are 2 independent parts, one for each index of `groups`. A program takes and returns all parts, laid end to end along the dimension named above; an argument that names none is the same for every part. Nothing has to cross between parts.
Inputs may be any that keep to these rules, and one draw needn't show every extreme that they name: `expert_ids`: each row names 8 different experts; among the 8 aligned rows of one index of ep no expert is named more than 2 times, and some expert reaches 2.
All inputs are finite; a program needn't handle non-finite values. No bound on the sum of `lengths` on one device may be relied on, other than what follows from the above.
Results may differ from a plain program's by a relative error of at most 0.024.
Values may be sent and summed in bfloat16 or wider, within the bound.
No kernel may reach another device: no remote copies, remote signals or barrier semaphores. Data moves between devices by JAX's collectives and lax.ppermute only.
A program may use at most 128 MiB of HBM per device.

v0:
```python
import math

import jax
import jax.numpy as jnp
from jax import lax
from jax.sharding import PartitionSpec as P

HD = 128
EXPERTS = 64
CAP = 2


def expert_apply(arrived, gate_local, up_local, down_local):
    expert_count, source_count, slot_count, feature_count = arrived.shape
    stacked = arrived.reshape(expert_count, source_count * slot_count, feature_count)
    gate = jnp.einsum("lnd,ldf->lnf", stacked, gate_local, preferred_element_type=jnp.float32)
    upper = jnp.einsum("lnd,ldf->lnf", stacked, up_local, preferred_element_type=jnp.float32)
    inner = (jax.nn.silu(gate) * upper).astype(jnp.bfloat16)
    result = jnp.einsum("lnf,lfd->lnd", inner, down_local, preferred_element_type=jnp.float32)
    return result.reshape(expert_count, source_count, slot_count, down_local.shape[2])


def on_device(
    hidden,
    query,
    new_key,
    new_value,
    cache_keys,
    cache_values,
    lengths,
    out_weight,
    norm_gain,
    expert_ids,
    route_weights,
    gate_weight,
    up_weight,
    down_weight,
):
    ep_count = lax.axis_size("ep")
    side_count = lax.axis_size("side")
    head_count = lax.axis_size("head")
    side_index = lax.axis_index("side")
    head_index = lax.axis_index("head")
    rows_here = hidden.shape[0]
    context = cache_keys.shape[1]
    kv_local = new_key.shape[1] // HD
    scale = 1.0 / math.sqrt(HD)
    queries = query.reshape(rows_here, kv_local, -1, HD)
    cached_keys = cache_keys.reshape(rows_here, context, kv_local, HD)
    cached_values = cache_values.reshape(rows_here, context, kv_local, HD)
    fresh_key = new_key.reshape(rows_here, kv_local, HD)
    fresh_value = new_value.reshape(rows_here, kv_local, HD)
    scores = (
        jnp.einsum("rgnd,rcgd->rgnc", queries, cached_keys, preferred_element_type=jnp.float32)
        * scale
    )
    fresh = (
        jnp.einsum("rgnd,rgd->rgn", queries, fresh_key, preferred_element_type=jnp.float32) * scale
    )
    usable = jnp.arange(context, dtype=jnp.int32)[None, :] < lengths[:, None]
    scores = jnp.where(usable[:, None, None, :], scores, jnp.float32(-1e30))
    highest = jnp.maximum(jnp.max(scores, -1), fresh)
    weights = jnp.where(
        usable[:, None, None, :], jnp.exp(scores - highest[..., None]), jnp.float32(0.0)
    )
    own_weight = jnp.exp(fresh - highest)
    denominator = jnp.sum(weights, -1) + own_weight
    mixed = jnp.einsum(
        "rgnc,rcgd->rgnd",
        weights.astype(jnp.bfloat16),
        cached_values,
        preferred_element_type=jnp.float32,
    )
    own_low = own_weight.astype(jnp.bfloat16).astype(jnp.float32)
    mixed = mixed + own_low[..., None] * fresh_value.astype(jnp.float32)[:, :, None, :]
    attended = (mixed / denominator[..., None]).astype(jnp.bfloat16).reshape(rows_here, -1)
    partial_value = jnp.dot(
        attended, out_weight.reshape(-1, out_weight.shape[2]), preferred_element_type=jnp.float32
    )
    projected = lax.psum(partial_value.astype(jnp.bfloat16), ("side", "head")).astype(jnp.float32)
    stream = hidden.astype(jnp.float32) + projected
    slice_width = stream.shape[1] // head_count
    after_attention = lax.dynamic_slice_in_dim(stream, head_index * slice_width, slice_width, 1)
    normed = (
        stream * lax.rsqrt(jnp.mean(stream * stream, -1, keepdims=True) + 1e-06) * norm_gain
    ).astype(jnp.bfloat16)
    local_count = gate_weight.shape[0]
    top_k = expert_ids.shape[1]
    capacity = CAP
    slots_total = local_count * ep_count * capacity
    flat_ids = expert_ids.reshape(-1)
    one_hot = (flat_ids[:, None] == jnp.arange(EXPERTS, dtype=jnp.int32)[None, :]).astype(jnp.int32)
    earlier = jnp.cumsum(one_hot, 0) - one_hot
    slot_index = jnp.sum(earlier * one_hot, 1)
    owner_block = flat_ids // local_count
    target_ep = owner_block // side_count
    target_side = owner_block % side_count
    local_slot = flat_ids % local_count
    position = (local_slot * ep_count + target_ep) * capacity + slot_index
    on_side = target_side == side_index
    chosen = (position[:, None] == jnp.arange(slots_total, dtype=jnp.int32)[None, :]) & on_side[
        :, None
    ]
    chosen = chosen.reshape(rows_here, top_k, slots_total)
    selector = jnp.sum(chosen.astype(jnp.int32), 1).astype(jnp.bfloat16)
    share = route_weights / jnp.sum(route_weights, 1, keepdims=True)
    combiner = jnp.sum(jnp.where(chosen, share[:, :, None], jnp.float32(0.0)), 1)
    outgoing = jnp.einsum("rf,rd->fd", selector, normed, preferred_element_type=jnp.float32).astype(
        jnp.bfloat16
    )
    outgoing = outgoing.reshape(local_count, ep_count, capacity, normed.shape[1])
    produced = expert_apply(
        lax.all_to_all(outgoing, "ep", split_axis=1, concat_axis=1, tiled=True),
        gate_weight,
        up_weight,
        down_weight,
    )
    reduced = lax.psum_scatter(
        produced.astype(jnp.bfloat16), "head", scatter_dimension=3, tiled=True
    )
    returned = lax.all_to_all(reduced, "ep", split_axis=1, concat_axis=1, tiled=True)
    side_share = jnp.dot(
        combiner,
        returned.reshape(slots_total, slice_width).astype(jnp.float32),
        precision=lax.Precision.HIGHEST,
    )
    expert_sum = lax.psum(side_share, "side").astype(jnp.bfloat16)
    return (after_attention, expert_sum)


def solution(mesh):
    placed = (
        P(("groups", "ep"), None),
        P(("groups", "ep"), "head", "side"),
        P(("groups", "ep"), "head"),
        P(("groups", "ep"), "head"),
        P(("groups", "ep"), None, "head"),
        P(("groups", "ep"), None, "head"),
        P(("groups", "ep")),
        P("head", "side", None),
        P(),
        P(("groups", "ep"), None),
        P(("groups", "ep"), None),
        P(("ep", "side"), None, "head"),
        P(("ep", "side"), None, "head"),
        P(("ep", "side"), "head", None),
    )
    return jax.shard_map(
        on_device,
        mesh=mesh,
        in_specs=placed,
        out_specs=(P(("groups", "ep"), "head"), P(("groups", "ep"), "head")),
        check_vma=False,
    )
```

profile of v0, /device:TPU:0, one launch (start us, length us, event | category | flops | bytes accessed | tf_op | source)
XLA Modules:
  0.0 187.5 jit_solution(13907719717470037876)
XLA Ops:
  7.2 0.0 copy-start
  7.2 0.0 reduce-scatter.4.cloned.1.call-start
  7.2 0.8 eq.42
  8.0 0.7 fusion.30
  8.8 0.7 iota_compare_fusion.2
  9.5 0.7 bitcast_convert_fusion
  10.2 0.7 reshape.168
  10.9 0.8 fusion.24
  11.7 0.0 copy-done
  11.7 0.5 fusion.39
  12.2 0.2 fusion.18
  12.4 1.4 fusion.3
  13.8 2.8 %convolution_convert_fusion.2 = bf16[8,2048]{1,0:T(8,128)(2,1)S(1)} fusion(bf16[8,1024]{1,0:T(8,128)(2,1)S(1)} %reshape.172, bf16[1024,2048]{1,0:T(8,128)(2,1)} %bitcast.40), kind=kOutput, calls=%fused_computation.2 | convolution fusion | flops 33570816 | bytes 4243456 | tf_op jit(solution)/shard_map/dot_general | solution.py:77
  16.7 14.3 %psum.14 = bf16[8,2048]{1,0:T(8,128)(2,1)S(1)} all-reduce(bf16[8,2048]{1,0:T(8,128)(2,1)S(1)} %convolution_convert_fusion.2), channel_id=1, replica_groups=mesh['groups'=2,'ep'=4,'side'=2,'head'=2] {'side','head'}, use_global_device_ids=true, to_apply=%region_2.3 | all-reduce | flops 16384 | bytes 65536 | tf_op jit(solution)/shard_map/psum | solution.py:80
  31.0 0.1 fusion.16
  31.0 0.1 reduce_window_sum.11
  31.1 0.2 select_reduce_fusion.1
  31.3 0.1 reduce_sum.58
  31.4 0.7 fusion.29
  32.1 0.9 multiply_reduce_fusion
  33.0 0.1 convert_reduce_fusion
  33.1 1.1 convolution_convert_fusion.1
  34.2 0.2 reshape.174
  34.4 0.2 copy.35
  34.6 13.5 %all_to_all.10 = bf16[8,4,2,2048]{3,2,0,1:T(2,128)(2,1)S(1)} all-to-all(bf16[8,4,2,2048]{3,2,0,1:T(2,128)(2,1)S(1)} %copy.35), channel_id=1, replica_groups=mesh['groups'=2,'ep'=4,'side'=2,'head'=2] {'ep'}, dimensions={1} | all-to-all | bytes 524288 | tf_op jit(solution)/shard_map/all_to_all | solution.py:113
  48.1 0.2 copy.36
  48.3 0.1 reshape.175
  48.4 6.3 %fusion.40 = f32[8,8,384]{2,1,0:T(8,128)S(1)} fusion(bf16[8,8,2048]{2,1,0:T(8,128)(2,1)S(1)} %reshape.175, bf16[8,2048,384]{2,1,0:T(8,128)(2,1)} %param.25), kind=kOutput, calls=%fused_computation.74 | convolution fusion | flops 100663296 | bytes 12943360 | tf_op jit(solution)/shard_map/lnd,ldf->lnf/dot_general | solution.py:16
  54.7 11.5 %convolution_convert_fusion = bf16[8,8,2048]{2,1,0:T(8,128)(2,1)S(1)} fusion(bf16[8,384,2048]{2,1,0:T(8,128)(2,1)} %param.27, bf16[8,8,2048]{2,1,0:T(8,128)(2,1)S(1)} %reshape.175, bf16[8,2048,384]{2,1,0:T(8,128)(2,1)} %param.26, f32[8,8,384]{2,1,0:T(8,128)S(1)} %fusion.40), kind=kOutput, calls=%fused_computation | convolution fusion | flops 201605120 | bytes 25788416 | tf_op jit(solution)/shard_map/lnf,lfd->lnd/dot_general | solution.py:19
  66.2 0.2 convert_element_type.75
  66.4 20.9 %copy.41 = bf16[8,4,2,2048]{2,1,0,3:T(4,128)(2,1)} copy(bf16[8,4,2,2048]{3,2,1,0:T(2,128)(2,1)S(1)} %convert_element_type.75) | data formatting | bytes 524288
  87.3 0.0 copy-start.2
  87.3 0.0 copy-start.1
  87.3 31.8 %reshape.180 = bf16[2048,64]{1,0:T(8,128)(2,1)} reshape(bf16[2048,8,4,2]{3,2,1,0:T(4,128)(2,1)} %bitcast.38) | data formatting | bytes 524288
  119.1 0.0 reduce-scatter.4.cloned.1.call-update
  119.2 0.0 copy-done.2
  119.2 0.1 reduce_sum.59
  119.3 0.1 broadcast_divide_fusion
  119.4 13.7 %reduce-scatter.4.cloned.1.call-done = bf16[1024,64]{1,0:T(8,128)(2,1)} async-done(((bf16[2048,64]{1,0:T(8,128)(2,1)}), bf16[1024,64]{1,0:T(8,128)(2,1)}) %reduce-scatter.4.cloned.1.call-update) | async-done | bytes 131088
  133.1 19.7 %reshape.181 = bf16[1024,8,4,2]{3,2,1,0:T(4,128)(2,1)} reshape(bf16[1024,64]{1,0:T(8,128)(2,1)} %reduce-scatter.4.cloned.1.call-done) | data formatting | bytes 262144
  152.8 12.9 %copy.37 = bf16[8,4,2,1024]{3,2,0,1:T(2,128)(2,1)} copy(bf16[8,4,2,1024]{2,1,0,3:T(4,128)(2,1)} %bitcast.39) | data formatting | bytes 262144 | tf_op jit(solution)/shard_map/reduce_scatter | solution.py:118
  165.7 4.6 %all-to-all-start.1 = ((bf16[8,4,2,1024]{3,2,0,1:T(2,128)(2,1)}), bf16[8,4,2,1024]{3,2,0,1:T(2,128)(2,1)S(1)}, u32[]{:S(2)}, u32[]{:S(2)}) async-start(bf16[8,4,2,1024]{3,2,0,1:T(2,128)(2,1)} %copy.37), calls=%async_computation.1 | async-start | bytes 262144 | tf_op jit(solution)/shard_map/all_to_all | solution.py:121
  170.3 0.6 constant_dynamic-slice_fusion
  170.9 0.1 select_reduce_fusion
  171.0 5.4 %all-to-all-done.1 = bf16[8,4,2,1024]{3,2,0,1:T(2,128)(2,1)S(1)} async-done(((bf16[8,4,2,1024]{3,2,0,1:T(2,128)(2,1)}), bf16[8,4,2,1024]{3,2,0,1:T(2,128)(2,1)S(1)}, u32[]{:S(2)}, u32[]{:S(2)}) %all-to-all-start.1) | async-done | bytes 131104 | tf_op jit(solution)/shard_map/all_to_all | solution.py:121
  176.4 0.1 copy.38
  176.5 0.1 reshape.176
  176.5 0.2 fusion.41
  176.7 4.0 %psum.15 = bf16[8,1024]{1,0:T(8,128)(2,1)} all-reduce(f32[8,1024]{1,0:T(8,128)S(1)} %fusion.41), channel_id=1, replica_groups=mesh['groups'=2,'ep'=4,'side'=2,'head'=2] {'side'}, use_global_device_ids=true, to_apply=%region_10.11 | all-reduce | flops 8192 | bytes 49152 | tf_op jit(solution)/shard_map/psum | solution.py:127
  180.7 0.0 copy-done.1
  (5 shorter events, 0.1 us)
Async XLA Ops:
  7.2 4.6 %copy-start = (bf16[8,128,256]{2,1,0:T(8,128)(2,1)S(1)}, bf16[8,128,256]{2,1,0:T(8,128)(2,1)}, u32[]{:S(2)}) copy-start(bf16[8,128,256]{2,1,0:T(8,128)(2,1)} %param.18) | copy-start | bytes 1572868
  7.2 125.9 %reduce-scatter.4.cloned.1.call-start = ((), (), s32[]{:S(2)}) async-start(), calls=%async_computation.3 | async-start | bytes 786432
  87.3 31.9 %copy-start.2 = (f32[8,8]{1,0:T(8,128)S(1)}, f32[8,8]{1,0:T(8,128)}, u32[]{:S(2)}) copy-start(f32[8,8]{1,0:T(8,128)} %param.24) | copy-start | bytes 772
  87.3 93.4 %copy-start.1 = (bf16[8,128,256]{2,1,0:T(8,128)(2,1)S(1)}, bf16[8,128,256]{2,1,0:T(8,128)(2,1)}, u32[]{:S(2)}) copy-start(bf16[8,128,256]{2,1,0:T(8,128)(2,1)} %param.18) | copy-start | bytes 1572868
  165.7 10.7 %all-to-all-start.1 = ((bf16[8,4,2,1024]{3,2,0,1:T(2,128)(2,1)}), bf16[8,4,2,1024]{3,2,0,1:T(2,128)(2,1)S(1)}, u32[]{:S(2)}, u32[]{:S(2)}) async-start(bf16[8,4,2,1024]{3,2,0,1:T(2,128)(2,1)} %copy.37), calls=%async_computation.1 | async-start | bytes 262144 | tf_op jit(solution)/shard_map/all_to_all | solution.py:121
Sparse Core Ops, SparseCore 0:
  119.3 13.7 reduce-scatter.3
where the time goes:
time: 189 us; the launch traced here: 188 us
  local copies, waits for them, and re-layouts  88.6 us (47%)
  blocking collectives  31.8 us (17%)
  matrix products  24.5 us (13%)
  waiting for transfers between devices  19.1 us (10%)
  between operations  14.2 us (8%)
  other arithmetic  4.69 us (2%)
  starting transfers between devices  4.64 us (2%)
    unnamed x9, local copies, waits for them, and re-layouts  72.4 us
    psum x1, blocking collectives, on_device(): lax.psum(partial_value.astype(jnp.bfloat16), ('side', 'head'))  14.3 us
    unnamed x2, waiting for transfers between devices  13.8 us
    all_to_all x1, blocking collectives, on_device(): lax.all_to_all(outgoing, 'ep', split_axis=1, concat_axis=1, tiled=True)  13.5 us
    reduce_scatter x1, local copies, waits for them, and re-layouts, on_device(): lax.psum_scatter(produced.astype(jnp.bfloat16), 'head', scatter_dimension...  12.9 us
    dot_general x1, matrix products, expert_apply(): jnp.einsum('lnf,lfd->lnd', inner, down_local, preferred_element_type=jnp....  11.5 us
    dot_general x1, matrix products, expert_apply(): jnp.einsum('lnd,ldf->lnf', stacked, gate_local, preferred_element_type=jn...  6.31 us
    all_to_all x1, waiting for transfers between devices, on_device(): lax.all_to_all(reduced, 'ep', split_axis=1, concat_axis=1, tiled=True)  5.35 us
  transfers between devices with their start and end apart: 2, of which 2 were waited for; matrix products, arithmetic and copies ran while one was open for 0% of the time, Pallas kernels for 0%

commit v1 on v0

v1 whole, which is shorter than its diff:
```python
import math

import jax
import jax.numpy as jnp
from jax import lax
from jax.sharding import PartitionSpec as P

HD = 128
BF = jnp.bfloat16
F32 = jnp.float32


def partners(count):
    steps = []
    k = 1
    while k < count:
        steps.append(k)
        k *= 2
    return steps


def swap(x, axis, k):
    count = lax.axis_size(axis)
    return lax.ppermute(x, axis, [(i, i ^ k) for i in range(count)])


def sum_over(x, axis):
    for k in partners(lax.axis_size(axis)):
        low = x.astype(BF)
        x = low.astype(F32) + swap(low, axis, k).astype(F32)
    return x


def on_device(
    hidden,
    query,
    new_key,
    new_value,
    cache_keys,
    cache_values,
    lengths,
    out_weight,
    norm_gain,
    expert_ids,
    route_weights,
    gate_weight,
    up_weight,
    down_weight,
):
    ep_count = lax.axis_size("ep")
    side_count = lax.axis_size("side")
    head_count = lax.axis_size("head")
    rows_here = hidden.shape[0]
    context = cache_keys.shape[1]
    kv_local = new_key.shape[1] // HD
    scale = 1.0 / math.sqrt(HD)
    queries = query.reshape(rows_here, kv_local, -1, HD)
    cached_keys = cache_keys.reshape(rows_here, context, kv_local, HD)
    cached_values = cache_values.reshape(rows_here, context, kv_local, HD)
    fresh_key = new_key.reshape(rows_here, kv_local, HD)
    fresh_value = new_value.reshape(rows_here, kv_local, HD)
    scores = (
        jnp.einsum("rgnd,rcgd->rgnc", queries, cached_keys, preferred_element_type=F32) * scale
    )
    fresh = jnp.einsum("rgnd,rgd->rgn", queries, fresh_key, preferred_element_type=F32) * scale
    usable = jnp.arange(context, dtype=jnp.int32)[None, :] < lengths[:, None]
    scores = jnp.where(usable[:, None, None, :], scores, F32(-1e30))
    highest = jnp.maximum(jnp.max(scores, -1), fresh)
    weights = jnp.where(usable[:, None, None, :], jnp.exp(scores - highest[..., None]), F32(0.0))
    own_weight = jnp.exp(fresh - highest)
    denominator = jnp.sum(weights, -1) + own_weight
    mixed = jnp.einsum(
        "rgnc,rcgd->rgnd", weights.astype(BF), cached_values, preferred_element_type=F32
    )
    own_low = own_weight.astype(BF).astype(F32)
    mixed = mixed + own_low[..., None] * fresh_value.astype(F32)[:, :, None, :]
    attended = (mixed / denominator[..., None]).astype(BF).reshape(rows_here, -1)
    partial_value = jnp.dot(
        attended, out_weight.reshape(-1, out_weight.shape[2]), preferred_element_type=F32
    )
    projected = sum_over(sum_over(partial_value, "side"), "head")
    stream = hidden.astype(F32) + projected
    width = stream.shape[1] // head_count
    head_index = lax.axis_index("head")
    after_attention = lax.dynamic_slice_in_dim(stream, head_index * width, width, 1)
    normed = (
        stream * lax.rsqrt(jnp.mean(stream * stream, -1, keepdims=True) + 1e-06) * norm_gain
    ).astype(BF)

    local_count = gate_weight.shape[0]
    experts = local_count * ep_count * side_count
    share = route_weights / jnp.sum(route_weights, 1, keepdims=True)
    named = expert_ids[:, :, None] == jnp.arange(experts, dtype=jnp.int32)[None, None, :]
    coefficient = jnp.sum(jnp.where(named, share[:, :, None], F32(0.0)), 1)
    high = coefficient.astype(BF)
    low = (coefficient - high.astype(F32)).astype(BF)
    packed = jnp.concatenate([normed, high, low], 1)
    for k in partners(ep_count):
        packed = jnp.concatenate([packed, swap(packed, "ep", k)], 0)
    depth = normed.shape[1]
    gathered = packed[:, :depth]
    coefficient = packed[:, depth : depth + experts].astype(F32) + packed[:, depth + experts :].astype(F32)
    first = (lax.axis_index("ep") * side_count + lax.axis_index("side")) * local_count
    coefficient = lax.dynamic_slice_in_dim(coefficient, first, local_count, 1)
    gate = jnp.einsum("nd,ldf->lnf", gathered, gate_weight, preferred_element_type=F32)
    upper = jnp.einsum("nd,ldf->lnf", gathered, up_weight, preferred_element_type=F32)
    inner = (jax.nn.silu(gate) * upper * coefficient.T[:, :, None]).astype(BF)
    result = jnp.einsum("lnf,lfd->nd", inner, down_weight, preferred_element_type=F32)
    parts = head_count
    for k in reversed(partners(head_count)):
        half = result.shape[1] // 2
        upper_half = (head_index & k) != 0
        mine = jnp.where(upper_half, result[:, half:], result[:, :half])
        other = jnp.where(upper_half, result[:, :half], result[:, half:])
        result = mine.astype(F32) + swap(other.astype(BF), "head", k).astype(F32)
    for k in reversed(partners(ep_count)):
        half = result.shape[0] // 2
        result = result[:half] + swap(result[half:].astype(BF), "ep", k).astype(F32)
    expert_sum = sum_over(result, "side").astype(BF)
    return (after_attention, expert_sum)


def solution(mesh):
    placed = (
        P(("groups", "ep"), None),
        P(("groups", "ep"), "head", "side"),
        P(("groups", "ep"), "head"),
        P(("groups", "ep"), "head"),
        P(("groups", "ep"), None, "head"),
        P(("groups", "ep"), None, "head"),
        P(("groups", "ep")),
        P("head", "side", None),
        P(),
        P(("groups", "ep"), None),
        P(("groups", "ep"), None),
        P(("ep", "side"), None, "head"),
        P(("ep", "side"), None, "head"),
        P(("ep", "side"), "head", None),
    )
    return jax.shard_map(
        on_device,
        mesh=mesh,
        in_specs=placed,
        out_specs=(P(("groups", "ep"), "head"), P(("groups", "ep"), "head")),
        check_vma=False,
    )
```

time: 189 us -> 62.3 us (0.33)
  local copies, waits for them, and re-layouts: 88.6 us -> 1.56 us
  blocking collectives: 31.8 us -> 0 us
  between operations: 14.2 us -> 0.76 us
  starting transfers between devices: 4.64 us -> 15.1 us
  waiting for transfers between devices: 19.1 us -> 12.9 us
    unnamed x9 -> x2, local copies, waits for them, and re-layouts: 72.4 us -> 0.01 us
    psum x2 -> x0, blocking collectives: 18.3 us -> none  [the longest x1 14.3 us: on_device(): lax.psum(partial_value.astype(jnp.bfloat16), ('side', 'head'))]
    ppermute x0 -> x8, starting transfers between devices: none -> 15.1 us  [swap(): return lax.ppermute(x, axis, [(i, i ^ k) for i in range(count)])]
    unnamed x2 -> x0, waiting for transfers between devices: 13.8 us -> none
    all_to_all x1 -> x0, blocking collectives: 13.5 us -> none  [on_device(): lax.all_to_all(outgoing, 'ep', split_axis=1, concat_axis=1, tiled=True)]
    ppermute x0 -> x8, waiting for transfers between devices: none -> 12.9 us  [swap(): return lax.ppermute(x, axis, [(i, i ^ k) for i in range(count)])]
    reduce_scatter x1 -> x0, local copies, waits for them, and re-layouts: 12.9 us -> none  [on_device(): lax.psum_scatter(produced.astype(jnp.bfloat16), 'head', scatter_dimension...]
    all_to_all x1 -> x0, waiting for transfers between devices: 5.35 us -> none  [on_device(): lax.all_to_all(reduced, 'ep', split_axis=1, concat_axis=1, tiled=True)]
  transfers between devices with their start and end apart: 2 -> 8, of which waited for: 2 -> 7; matrix products, arithmetic and copies ran while one was open for 0% -> 5% of each run, Pallas kernels for 0% -> 0%
where the time goes in v1:
time: 62.3 us; the launch traced here: 61.7 us
  matrix products  24.9 us (40%)
  starting transfers between devices  15.1 us (24%)
  waiting for transfers between devices  12.9 us (21%)
  other arithmetic  6.48 us (10%)
  local copies, waits for them, and re-layouts  1.56 us (3%)
  between operations  0.76 us (1%)
    ppermute x8, starting transfers between devices, swap(): return lax.ppermute(x, axis, [(i, i ^ k) for i in range(count)])  15.1 us
    ppermute x8, waiting for transfers between devices, swap(): return lax.ppermute(x, axis, [(i, i ^ k) for i in range(count)])  12.9 us
    dot_general x1, matrix products, on_device(): jnp.einsum('lnf,lfd->nd', inner, down_weight, preferred_element_type=F32)  12.6 us
    dot_general x1, matrix products, on_device(): jnp.einsum('nd,ldf->lnf', gathered, gate_weight, preferred_element_type=F32)  6.81 us
    dot_general x1, matrix products, on_device(): jnp.dot(attended, out_weight.reshape(-1, out_weight.shape[2]), preferred_...  2.84 us
    dot_general x1, matrix products, on_device(): jnp.einsum('rgnc,rcgd->rgnd', weights.astype(BF), cached_values, preferre...  1.35 us
  transfers between devices with their start and end apart: 8, of which 7 were waited for; matrix products, arithmetic and copies ran while one was open for 5% of the time, Pallas kernels for 0%

profile of v1, /device:TPU:0, one launch (start us, length us, event | category | flops | bytes accessed | tf_op | source)
XLA Modules:
  0.0 61.7 jit_solution(6337488867857813845)
XLA Ops:
  0.6 0.0 copy-start
  0.6 0.8 %iota_compare_fusion.1 = pred[8,128]{1,0:T(8,128)(4,1)S(1)} fusion(s32[8]{0:T(128)} %param.20), kind=kLoop, calls=%fused_computation.58 | loop fusion | flops 1024 | bytes 1056 | tf_op jit(solution)/shard_map/lt | solution.py:66
  1.4 0.7 %bitcast_convert_fusion = f32[8,2,128]{2,0,1:T(8,128)S(1)} fusion(bf16[8,256]{1,0:T(8,128)(2,1)} %param.17), kind=kLoop, calls=%fused_computation.55 | loop fusion | flops 2048 | bytes 12288 | tf_op jit(solution)/shard_map/convert_element_type | solution.py:76
  2.1 0.7 %reshape.63 = bf16[8,2,4,128]{3,2,1,0:T(4,128)(2,1)S(1)} reshape(bf16[8,2,512]{2,1,0:T(2,128)(2,1)} %param.15) | data formatting | bytes 32768 | tf_op jit(solution)/shard_map/reshape | solution.py:57
  2.9 0.8 %fusion.24 = f32[8,2,1,4]{3,2,1,0:T(1,128)S(1)} fusion(bf16[8,2,4,128]{3,2,1,0:T(4,128)(2,1)S(1)} %reshape.63, bf16[8,2,128,1]{2,0,1,3:T(8,128)(2,1)} %bitcast.56), kind=kOutput, calls=%fused_computation.52 | convolution fusion | flops 16384 | bytes 20736 | tf_op jit(solution)/shard_map/rgnd,rgd->rgn/dot_general | solution.py:65
  3.7 0.0 copy-done
  3.7 0.5 fusion.29
  4.2 0.2 fusion.18
  4.4 1.4 %fusion.5 = bf16[8,2,4,128]{3,2,1,0:T(4,128)(2,1)S(1)} fusion(f32[8,2,4,128]{3,2,1,0:T(4,128)S(1)} %get-tuple-element.9, f32[8,2,4]{2,1,0:T(2,128)S(1)} %get-tuple-element.7, f32[8,2,128]{2,1,0:T(2,128)S(1)} %copy.22, f32[8,2,4]{2,1,0:T(2,128)S(1)} %get-tuple-element.6, f32[8,2,4]{2,1,0:T(2,128)S(1)} %multiply_maximum_fusion, ...), kind=kOutput, calls=%fused_computation.11 | convolution fusion | flops 2154496 | bytes 583424 | tf_op jit(solution)/shard_map/rgnc,rcgd->rgnd/dot_general | solution.py:72
  5.8 2.8 %convolution_convert_fusion = bf16[8,2048]{1,0:T(8,128)(2,1)S(1)} fusion(bf16[8,1024]{1,0:T(8,128)(2,1)S(1)} %reshape.67, bf16[1024,2048]{1,0:T(8,128)(2,1)} %bitcast.53), kind=kOutput, calls=%fused_computation.1 | convolution fusion | flops 33570816 | bytes 4243456 | tf_op jit(solution)/shard_map/dot_general | solution.py:78
  8.6 0.5 collective-permute-start
  9.1 0.8 %reduce_sum.38 = f32[8]{0:T(128)S(1)} reduce(f32[8,8]{1,0:T(8,128)} %param.24, f32[]{:T(128)} %constant.9.clone.1), dimensions={1}, to_apply=%region_3.4 | reduce | flops 56 | bytes 292 | tf_op jit(solution)/shard_map/reduce_sum | solution.py:92
  9.9 0.8 %broadcast_divide_fusion = f32[8,8]{1,0:T(8,128)S(1)} fusion(f32[8,8]{1,0:T(8,128)} %param.24, f32[8]{0:T(128)S(1)} %reduce_sum.38), kind=kLoop, calls=%fused_computation.59 | loop fusion | flops 64 | bytes 544 | tf_op jit(solution)/shard_map/div | solution.py:92
  10.7 0.8 %select_reduce_fusion = f32[8,64]{1,0:T(8,128)S(1)} fusion(f32[8,8]{1,0:T(8,128)S(1)} %broadcast_divide_fusion, s32[8,8]{1,0:T(8,128)} %param.23), kind=kLoop, calls=%fused_computation.38 | loop fusion | flops 11776 | bytes 2560 | tf_op jit(solution)/shard_map/reduce_sum | solution.py:94
  11.5 0.0 collective-permute-done
  11.5 2.5 %collective-permute-start.1 = (bf16[8,2048]{1,0:T(8,128)(2,1)S(1)}, bf16[8,2048]{1,0:T(8,128)(2,1)S(1)}, u32[]{:S(2)}, u32[]{:S(2)}) collective-permute-start(bf16[8,2048]{1,0:T(8,128)(2,1)S(1)} %add_convert_fusion), channel_id=1, source_target_pairs={{0,1},{1,0},{2,3},{3,2},{4,5},{5,4},{6,7},{7,6},{8,9},{9,8},{10,11... | collective-permute-start | bytes 98312 | tf_op jit(solution)/shard_map/ppermute | solution.py:24
  14.0 2.1 %collective-permute-done.1 = bf16[8,2048]{1,0:T(8,128)(2,1)S(1)} collective-permute-done((bf16[8,2048]{1,0:T(8,128)(2,1)S(1)}, bf16[8,2048]{1,0:T(8,128)(2,1)S(1)}, u32[]{:S(2)}, u32[]{:S(2)}) %collective-permute-start.1) | collective-permute-done | bytes 32800 | tf_op jit(solution)/shard_map/ppermute | solution.py:24
  16.1 0.9 %multiply_reduce_fusion = (f32[8]{0:T(128)S(1)}, f32[8,2048]{1,0:T(8,128)S(1)}) fusion(bf16[8,2048]{1,0:T(8,128)(2,1)S(1)} %collective-permute-done.1, bf16[8,2048]{1,0:T(8,128)(2,1)S(1)} %add_convert_fusion, bf16[8,2048]{1,0:T(8,128)(2,1)} %param.14), kind=kLoop, calls=%fused_computation.31 | loop fusion | flops 114680 | bytes 163872 | tf_op jit(solution)/shard_map/reduce_sum | solution.py:87
  17.0 0.8 %multiply_convert_fusion = bf16[8,2048]{1,0:T(8,128)(2,1)S(1)} fusion(f32[8,2048]{1,0:T(8,128)S(1)} %get-tuple-element.5, f32[2048]{0:T(1024)} %param.22, f32[8]{0:T(128)S(1)} %add_rsqrt_fusion), kind=kLoop, calls=%fused_computation.30 | loop fusion | flops 49152 | bytes 106528 | tf_op jit(solution)/shard_map/convert_element_type | solution.py:88
  17.8 0.1 concatenate.10
  17.9 1.9 %collective-permute-start.2 = (bf16[8,2176]{1,0:T(8,128)(2,1)S(1)}, bf16[8,2176]{1,0:T(8,128)(2,1)S(1)}, u32[]{:S(2)}, u32[]{:S(2)}) collective-permute-start(bf16[8,2176]{1,0:T(8,128)(2,1)S(1)} %concatenate.10), channel_id=1, source_target_pairs={{0,4},{4,0},{8,12},{12,8},{1,5},{5,1},{9,13},{13,9},{2,6},{6,2},{1... | collective-permute-start | bytes 104456 | tf_op jit(solution)/shard_map/ppermute | solution.py:24
  19.8 2.0 %collective-permute-done.2 = bf16[8,2176]{1,0:T(8,128)(2,1)S(1)} collective-permute-done((bf16[8,2176]{1,0:T(8,128)(2,1)S(1)}, bf16[8,2176]{1,0:T(8,128)(2,1)S(1)}, u32[]{:S(2)}, u32[]{:S(2)}) %collective-permute-start.2) | collective-permute-done | bytes 34848 | tf_op jit(solution)/shard_map/ppermute | solution.py:24
  21.8 3.0 %collective-permute-start.3 = (bf16[16,2176]{1,0:T(8,128)(2,1)S(1)}, bf16[16,2176]{1,0:T(8,128)(2,1)S(1)}, u32[]{:S(2)}, u32[]{:S(2)}) collective-permute-start(bf16[16,2176]{1,0:T(8,128)(2,1)S(1)} %pad_maximum_fusion.1), channel_id=1, source_target_pairs={{0,8},{4,12},{8,0},{12,4},{1,9},{5,13},{9,1},{13,5},{2,10},{6,14},... | collective-permute-start | bytes 208904 | tf_op jit(solution)/shard_map/ppermute | solution.py:24
  24.8 2.3 %collective-permute-done.3 = bf16[16,2176]{1,0:T(8,128)(2,1)S(1)} collective-permute-done((bf16[16,2176]{1,0:T(8,128)(2,1)S(1)}, bf16[16,2176]{1,0:T(8,128)(2,1)S(1)}, u32[]{:S(2)}, u32[]{:S(2)}) %collective-permute-start.3) | collective-permute-done | bytes 69664 | tf_op jit(solution)/shard_map/ppermute | solution.py:24
  27.0 0.1 add_bitcast_fusion
  27.1 0.1 copy.23
  27.2 6.8 %convolution_bitcast_fusion.2 = f32[8,32,384]{2,1,0:T(8,128)S(1)} fusion(bf16[8,2048,384]{2,1,0:T(8,128)(2,1)} %param.25, bf16[32,2176]{1,0:T(8,128)(2,1)S(1)} %pad_maximum_fusion), kind=kOutput, calls=%fused_computation.3 | convolution fusion | flops 402653184 | bytes 13107200 | tf_op jit(solution)/shard_map/nd,ldf->lnf/dot_general | solution.py:105
  34.0 12.6 %convolution_bitcast_fusion = f32[32,2048]{1,0:T(8,128)S(1)} fusion(bf16[8,384,2048]{2,1,0:T(8,128)(2,1)} %param.27, bf16[8,2048,384]{2,1,0:T(8,128)(2,1)} %param.26, f32[8,32,384]{2,1,0:T(8,128)S(1)} %convolution_bitcast_fusion.2, f32[8,32]{1,0:T(8,128)S(1)} %copy.23, bf16[32,2176]{1,0:T(8,128)(2,1)S(1)} %pad_maximum_fusion), kind=kOutput, calls=%fused_computation | convolution fusion | flops 805994496 | bytes 25956352 | tf_op jit(solution)/shard_map/lnf,lfd->nd/dot_general | solution.py:108
  46.7 1.9 %collective-permute-start.4 = (bf16[32,1024]{1,0:T(8,128)(2,1)S(1)}, bf16[32,1024]{1,0:T(8,128)(2,1)S(1)}, u32[]{:S(2)}, u32[]{:S(2)}) collective-permute-start(bf16[32,1024]{1,0:T(8,128)(2,1)S(1)} %select_convert_fusion), channel_id=1, source_target_pairs={{0,1},{1,0},{2,3},{3,2},{4,5},{5,4},{6,7},{7,6},{8,9},{9,8},{10,11... | collective-permute-start | bytes 196616 | tf_op jit(solution)/shard_map/ppermute | solution.py:24
  48.6 2.4 %collective-permute-done.4 = bf16[32,1024]{1,0:T(8,128)(2,1)S(1)} collective-permute-done((bf16[32,1024]{1,0:T(8,128)(2,1)S(1)}, bf16[32,1024]{1,0:T(8,128)(2,1)S(1)}, u32[]{:S(2)}, u32[]{:S(2)}) %collective-permute-start.4) | collective-permute-done | bytes 65568 | tf_op jit(solution)/shard_map/ppermute | solution.py:24
  51.0 3.1 %collective-permute-start.5 = (bf16[16,1024]{1,0:T(8,128)(2,1)S(1)}, bf16[16,1024]{1,0:T(8,128)(2,1)S(1)}, u32[]{:S(2)}, u32[]{:S(2)}) collective-permute-start(bf16[16,1024]{1,0:T(8,128)(2,1)S(1)} %slice.61), channel_id=1, source_target_pairs={{0,8},{4,12},{8,0},{12,4},{1,9},{5,13},{9,1},{13,5},{2,10},{6,14},... | collective-permute-start | bytes 98312 | tf_op jit(solution)/shard_map/ppermute | solution.py:24
  54.1 1.9 %collective-permute-done.5 = bf16[16,1024]{1,0:T(8,128)(2,1)S(1)} collective-permute-done((bf16[16,1024]{1,0:T(8,128)(2,1)S(1)}, bf16[16,1024]{1,0:T(8,128)(2,1)S(1)}, u32[]{:S(2)}, u32[]{:S(2)}) %collective-permute-start.5) | collective-permute-done | bytes 32800 | tf_op jit(solution)/shard_map/ppermute | solution.py:24
  56.0 2.2 %collective-permute-start.6 = (bf16[8,1024]{1,0:T(8,128)(2,1)S(1)}, bf16[8,1024]{1,0:T(8,128)(2,1)S(1)}, u32[]{:S(2)}, u32[]{:S(2)}) collective-permute-start(bf16[8,1024]{1,0:T(8,128)(2,1)S(1)} %slice.62), channel_id=1, source_target_pairs={{0,4},{4,0},{8,12},{12,8},{1,5},{5,1},{9,13},{13,9},{2,6},{6,2},{1... | collective-permute-start | bytes 49160 | tf_op jit(solution)/shard_map/ppermute | solution.py:24
  58.2 1.7 %collective-permute-done.6 = bf16[8,1024]{1,0:T(8,128)(2,1)S(1)} collective-permute-done((bf16[8,1024]{1,0:T(8,128)(2,1)S(1)}, bf16[8,1024]{1,0:T(8,128)(2,1)S(1)}, u32[]{:S(2)}, u32[]{:S(2)}) %collective-permute-start.6) | collective-permute-done | bytes 16416 | tf_op jit(solution)/shard_map/ppermute | solution.py:24
  59.9 0.0 collective-permute-start.7
  60.0 0.6 %constant_dynamic-slice_fusion = f32[8,1024]{1,0:T(8,128)} fusion(f32[8,2048]{1,0:T(8,128)S(1)} %get-tuple-element.5, s32[]{:T(128)S(6)} %select_n.31), kind=kLoop, calls=%fused_computation.60 | loop fusion | bytes 65540 | tf_op jit(solution)/shard_map/dynamic_slice | solution.py:85
  60.6 0.5 collective-permute-done.7
  61.1 0.6 add_convert_fusion.1
  (15 shorter events, 0.2 us)
Async XLA Ops:
  0.6 3.1 %copy-start = (bf16[8,128,256]{2,1,0:T(8,128)(2,1)S(1)}, bf16[8,128,256]{2,1,0:T(8,128)(2,1)}, u32[]{:S(2)}) copy-start(bf16[8,128,256]{2,1,0:T(8,128)(2,1)} %param.18) | copy-start | bytes 1572868
  8.6 2.9 %collective-permute-start = (bf16[8,2048]{1,0:T(8,128)(2,1)S(1)}, bf16[8,2048]{1,0:T(8,128)(2,1)S(1)}, u32[]{:S(2)}, u32[]{:S(2)}) collective-permute-start(bf16[8,2048]{1,0:T(8,128)(2,1)S(1)} %convolution_convert_fusion), channel_id=1, source_target_pairs={{0,2},{2,0},{1,3},{3,1},{4,6},{6,4},{5,7},{7,5},{8,10},{10,8},{9,1... | collective-permute-start | bytes 98312 | tf_op jit(solution)/shard_map/ppermute | solution.py:24
  11.5 4.6 %collective-permute-start.1 = (bf16[8,2048]{1,0:T(8,128)(2,1)S(1)}, bf16[8,2048]{1,0:T(8,128)(2,1)S(1)}, u32[]{:S(2)}, u32[]{:S(2)}) collective-permute-start(bf16[8,2048]{1,0:T(8,128)(2,1)S(1)} %add_convert_fusion), channel_id=1, source_target_pairs={{0,1},{1,0},{2,3},{3,2},{4,5},{5,4},{6,7},{7,6},{8,9},{9,8},{10,11... | collective-permute-start | bytes 98312 | tf_op jit(solution)/shard_map/ppermute | solution.py:24
  17.9 3.9 %collective-permute-start.2 = (bf16[8,2176]{1,0:T(8,128)(2,1)S(1)}, bf16[8,2176]{1,0:T(8,128)(2,1)S(1)}, u32[]{:S(2)}, u32[]{:S(2)}) collective-permute-start(bf16[8,2176]{1,0:T(8,128)(2,1)S(1)} %concatenate.10), channel_id=1, source_target_pairs={{0,4},{4,0},{8,12},{12,8},{1,5},{5,1},{9,13},{13,9},{2,6},{6,2},{1... | collective-permute-start | bytes 104456 | tf_op jit(solution)/shard_map/ppermute | solution.py:24
  21.8 5.2 %collective-permute-start.3 = (bf16[16,2176]{1,0:T(8,128)(2,1)S(1)}, bf16[16,2176]{1,0:T(8,128)(2,1)S(1)}, u32[]{:S(2)}, u32[]{:S(2)}) collective-permute-start(bf16[16,2176]{1,0:T(8,128)(2,1)S(1)} %pad_maximum_fusion.1), channel_id=1, source_target_pairs={{0,8},{4,12},{8,0},{12,4},{1,9},{5,13},{9,1},{13,5},{2,10},{6,14},... | collective-permute-start | bytes 208904 | tf_op jit(solution)/shard_map/ppermute | solution.py:24
  46.7 4.3 %collective-permute-start.4 = (bf16[32,1024]{1,0:T(8,128)(2,1)S(1)}, bf16[32,1024]{1,0:T(8,128)(2,1)S(1)}, u32[]{:S(2)}, u32[]{:S(2)}) collective-permute-start(bf16[32,1024]{1,0:T(8,128)(2,1)S(1)} %select_convert_fusion), channel_id=1, source_target_pairs={{0,1},{1,0},{2,3},{3,2},{4,5},{5,4},{6,7},{7,6},{8,9},{9,8},{10,11... | collective-permute-start | bytes 196616 | tf_op jit(solution)/shard_map/ppermute | solution.py:24
  51.0 4.9 %collective-permute-start.5 = (bf16[16,1024]{1,0:T(8,128)(2,1)S(1)}, bf16[16,1024]{1,0:T(8,128)(2,1)S(1)}, u32[]{:S(2)}, u32[]{:S(2)}) collective-permute-start(bf16[16,1024]{1,0:T(8,128)(2,1)S(1)} %slice.61), channel_id=1, source_target_pairs={{0,8},{4,12},{8,0},{12,4},{1,9},{5,13},{9,1},{13,5},{2,10},{6,14},... | collective-permute-start | bytes 98312 | tf_op jit(solution)/shard_map/ppermute | solution.py:24
  56.0 3.9 %collective-permute-start.6 = (bf16[8,1024]{1,0:T(8,128)(2,1)S(1)}, bf16[8,1024]{1,0:T(8,128)(2,1)S(1)}, u32[]{:S(2)}, u32[]{:S(2)}) collective-permute-start(bf16[8,1024]{1,0:T(8,128)(2,1)S(1)} %slice.62), channel_id=1, source_target_pairs={{0,4},{4,0},{8,12},{12,8},{1,5},{5,1},{9,13},{13,9},{2,6},{6,2},{1... | collective-permute-start | bytes 49160 | tf_op jit(solution)/shard_map/ppermute | solution.py:24
  59.9 1.2 %collective-permute-start.7 = (bf16[8,1024]{1,0:T(8,128)(2,1)S(1)}, bf16[8,1024]{1,0:T(8,128)(2,1)S(1)}, u32[]{:S(2)}, u32[]{:S(2)}) collective-permute-start(bf16[8,1024]{1,0:T(8,128)(2,1)S(1)} %fusion.17), channel_id=1, source_target_pairs={{0,2},{2,0},{1,3},{3,1},{4,6},{6,4},{5,7},{7,5},{8,10},{10,8},{9,1... | collective-permute-start | bytes 49160 | tf_op jit(solution)/shard_map/ppermute | solution.py:24

commit v2 on v1

v2 whole, which is shorter than its diff:
```python
import functools
import math

import jax
import jax.numpy as jnp
from jax import lax
from jax.experimental import pallas as pl
from jax.experimental.pallas import tpu as pltpu
from jax.sharding import PartitionSpec as P

HD = 128
BF = jnp.bfloat16
F32 = jnp.float32
VMEM = pl.BlockSpec(memory_space=pltpu.VMEM)
HBM = pl.BlockSpec(memory_space=pltpu.HBM)


def in_vmem(x):
    return pltpu.with_memory_space_constraint(x, pltpu.VMEM)


def in_hbm(x):
    return pltpu.with_memory_space_constraint(x, pltpu.HBM)


def partners(count):
    steps = []
    k = 1
    while k < count:
        steps.append(k)
        k *= 2
    return steps


def swap(x, axis, k):
    count = lax.axis_size(axis)
    return lax.ppermute(x, axis, [(i, i ^ k) for i in range(count)])


def sum_over(low, axis):
    total = low.astype(F32)
    for k in partners(lax.axis_size(axis)):
        low = total.astype(BF)
        total = low.astype(F32) + swap(low, axis, k).astype(F32)
    return total


def attend_kernel(
    lengths_hbm,
    query_hbm,
    new_key_hbm,
    new_value_hbm,
    cache_keys_hbm,
    cache_values_hbm,
    expert_ids_hbm,
    route_weights_hbm,
    hidden_hbm,
    norm_gain_hbm,
    out_weight_hbm,
    attended_out,
    coefficient_out,
    hidden_out,
    norm_gain_out,
    out_weight_out,
    lengths,
    query,
    new_key,
    new_value,
    cache_keys,
    cache_values,
    expert_ids,
    route_weights,
    arrivals,
):
    moves = [
        (lengths_hbm, lengths),
        (query_hbm, query),
        (cache_keys_hbm, cache_keys),
        (new_key_hbm, new_key),
        (new_value_hbm, new_value),
        (cache_values_hbm, cache_values),
        (expert_ids_hbm, expert_ids),
        (route_weights_hbm, route_weights),
        (hidden_hbm, hidden_out),
        (norm_gain_hbm, norm_gain_out),
        (out_weight_hbm, out_weight_out),
    ]
    copies = [
        pltpu.make_async_copy(source, target, arrivals.at[i])
        for i, (source, target) in enumerate(moves)
    ]
    for copy in copies:
        copy.start()
    rows, kv_local, width = query.shape
    context = cache_keys.shape[1]
    heads = width // HD
    total = rows * context
    scale = 1.0 / math.sqrt(HD)
    pairs = [(g, n) for g in range(kv_local) for n in range(heads)]
    for copy in copies[:4]:
        copy.wait()
    zero = jnp.zeros((rows, HD), BF)
    queries = [query[:, g, n * HD : (n + 1) * HD] for g, n in pairs]
    placed = [
        jnp.concatenate([q if g == other else zero for other in range(kv_local)], 1)
        for (g, n), q in zip(pairs, queries)
    ]
    stacked = jnp.concatenate(placed, 0)
    keys = cache_keys[...].reshape(total, kv_local * HD)
    contract = (((1,), (1,)), ((), ()))
    scores = lax.dot_general(stacked, keys, contract, preferred_element_type=F32) * scale
    scores = scores.reshape(len(pairs), rows, total)
    row = lax.broadcasted_iota(jnp.int32, (rows, total), 0)
    column = lax.broadcasted_iota(jnp.int32, (rows, total), 1)
    start = row * context
    end = start
    for r in range(rows):
        end = jnp.where(row == r, r * context + lengths[r], end)
    usable = (column >= start) & (column < end)
    scores = jnp.where(usable[None], scores, F32(-1e30))
    fresh = jnp.stack(
        [
            jnp.sum(
                q.astype(F32) * new_key[:, g * HD : (g + 1) * HD].astype(F32), 1, keepdims=True
            )
            for (g, n), q in zip(pairs, queries)
        ],
        0,
    ) * scale
    highest = jnp.maximum(jnp.max(scores, -1, keepdims=True), fresh)
    weights = jnp.exp(scores - highest)
    own = jnp.exp(fresh - highest)
    denominator = jnp.sum(weights, -1, keepdims=True) + own
    low = weights.astype(BF).reshape(len(pairs) * rows, total)
    for copy in copies[4:8]:
        copy.wait()
    values = cache_values[...].reshape(total, kv_local * HD)
    mixed = jnp.dot(low, values, preferred_element_type=F32)
    mixed = mixed.reshape(len(pairs), rows, kv_local * HD)
    own_low = own.astype(BF).astype(F32)
    for i, (g, n) in enumerate(pairs):
        block = slice(g * HD, (g + 1) * HD)
        value = mixed[i][:, block] + own_low[i] * new_value[:, block].astype(F32)
        attended_out[:, i * HD : (i + 1) * HD] = (value / denominator[i]).astype(BF)
    experts = coefficient_out.shape[1] // 2
    weight = route_weights[...]
    share = weight / jnp.sum(weight, 1, keepdims=True)
    lane = lax.broadcasted_iota(jnp.int32, (rows, experts), 1)
    coefficient = jnp.zeros((rows, experts), F32)
    for k in range(weight.shape[1]):
        coefficient += jnp.where(lane == expert_ids[:, k : k + 1], share[:, k : k + 1], F32(0.0))
    high = coefficient.astype(BF)
    rest = (coefficient - high.astype(F32)).astype(BF)
    coefficient_out[...] = jnp.concatenate([high, rest], 1)
    for copy in copies[8:]:
        copy.wait()


def project_kernel(attended, out_weight, hidden, partial_out):
    depth = out_weight.shape[2]
    projected = jnp.dot(
        attended[...],
        out_weight[...].reshape(attended.shape[1], depth),
        preferred_element_type=F32,
    )
    first = (lax.axis_index("side") == 0) & (lax.axis_index("head") == 0)
    base = jnp.where(first, hidden[...].astype(F32), F32(0.0))
    partial_out[...] = (projected + base).astype(BF)


def expert_kernel(
    gathered, norm_gain, gate_weight, up_weight, down_weight, out, inner, width
):
    count, depth, hidden_units = gate_weight.shape
    experts = (gathered.shape[1] - depth) // 2
    rows = gathered.shape[0]
    stream = gathered[:, :depth].astype(F32)
    norm = lax.rsqrt(jnp.mean(stream * stream, -1, keepdims=True) + 1e-06)
    normed = (stream * norm * norm_gain[...]).astype(BF)
    coefficient = gathered[:, depth : depth + experts].astype(F32) + gathered[
        :, depth + experts :
    ].astype(F32)
    lane = lax.broadcasted_iota(jnp.int32, (rows, experts), 1)
    me = lax.axis_index("ep")
    first = (me * lax.axis_size("side") + lax.axis_index("side")) * count
    for e in range(count):
        gate = jnp.dot(normed, gate_weight[e], preferred_element_type=F32)
        upper = jnp.dot(normed, up_weight[e], preferred_element_type=F32)
        share = jnp.sum(jnp.where(lane == first + e, coefficient, F32(0.0)), 1, keepdims=True)
        value = gate / (1.0 + jnp.exp(-gate)) * upper * share
        inner[:, e * hidden_units : (e + 1) * hidden_units] = value.astype(BF)
    result = jnp.dot(
        inner[...],
        down_weight[...].reshape(count * hidden_units, depth),
        preferred_element_type=F32,
    ).astype(BF)
    blocks, block_rows, _ = out.shape
    heads = depth // width
    for j in range(blocks // heads):
        target = me ^ j
        for h in range(heads):
            out[target * heads + h] = result[
                j * block_rows : (j + 1) * block_rows, h * width : (h + 1) * width
            ]


def on_device(
    hidden,
    query,
    new_key,
    new_value,
    cache_keys,
    cache_values,
    lengths,
    out_weight,
    norm_gain,
    expert_ids,
    route_weights,
    gate_weight,
    up_weight,
    down_weight,
):
    ep_count = lax.axis_size("ep")
    side_count = lax.axis_size("side")
    head_count = lax.axis_size("head")
    head_index = lax.axis_index("head")
    rows, depth = hidden.shape
    local_count, _, hidden_units = gate_weight.shape
    experts = local_count * ep_count * side_count
    width = depth // head_count
    top = expert_ids.shape[1]
    gain = norm_gain.reshape(1, depth)
    attended, coefficient, hidden_near, gain_near, out_weight_near = pl.pallas_call(
        attend_kernel,
        out_shape=(
            pltpu.VMEM((rows, out_weight.shape[0] * out_weight.shape[1]), BF),
            pltpu.VMEM((rows, 2 * experts), BF),
            pltpu.VMEM(hidden.shape, BF),
            pltpu.VMEM(gain.shape, F32),
            pltpu.VMEM(out_weight.shape, BF),
        ),
        in_specs=[HBM] * 11,
        out_specs=(VMEM,) * 5,
        scratch_shapes=[
            pltpu.SMEM(lengths.shape, jnp.int32),
            pltpu.VMEM(query.shape, BF),
            pltpu.VMEM(new_key.shape, BF),
            pltpu.VMEM(new_value.shape, BF),
            pltpu.VMEM(cache_keys.shape, BF),
            pltpu.VMEM(cache_values.shape, BF),
            pltpu.VMEM((rows, top), jnp.int32),
            pltpu.VMEM((rows, top), F32),
            pltpu.SemaphoreType.DMA((11,)),
        ],
        compiler_params=pltpu.CompilerParams(vmem_limit_bytes=8 << 20),
        name="attend",
    )(
        in_hbm(lengths),
        in_hbm(query),
        in_hbm(new_key),
        in_hbm(new_value),
        in_hbm(cache_keys),
        in_hbm(cache_values),
        in_hbm(expert_ids),
        in_hbm(route_weights),
        in_hbm(hidden),
        in_hbm(gain),
        in_hbm(out_weight),
    )
    partial_value = pl.pallas_call(
        project_kernel,
        out_shape=pltpu.VMEM((rows, depth), BF),
        in_specs=[VMEM] * 3,
        out_specs=VMEM,
        compiler_params=pltpu.CompilerParams(vmem_limit_bytes=8 << 20),
        cost_estimate=pl.CostEstimate(
            flops=10**12, bytes_accessed=200 * 10**6, transcendentals=0
        ),
        name="project",
    )(in_vmem(attended), in_vmem(out_weight_near), in_vmem(hidden_near))
    stream = sum_over(sum_over(partial_value, "side").astype(BF), "head")
    after_attention = lax.dynamic_slice_in_dim(stream, head_index * width, width, 1)
    packed = jnp.concatenate([stream.astype(BF), coefficient], 1)
    if ep_count <= 4:
        gathered = jnp.concatenate(
            [packed] + [swap(packed, "ep", k) for k in range(1, ep_count)], 0
        )
    else:
        gathered = packed
        for k in partners(ep_count):
            gathered = jnp.concatenate([gathered, swap(gathered, "ep", k)], 0)
    weight_bytes = 2 * (gate_weight.size + up_weight.size + down_weight.size)
    result = pl.pallas_call(
        functools.partial(expert_kernel, width=width),
        out_shape=jax.ShapeDtypeStruct((ep_count * head_count, rows, width), BF),
        in_specs=[VMEM] * 5,
        out_specs=VMEM,
        scratch_shapes=[pltpu.VMEM((ep_count * rows, local_count * hidden_units), BF)],
        compiler_params=pltpu.CompilerParams(vmem_limit_bytes=8 << 20),
        cost_estimate=pl.CostEstimate(
            flops=ep_count * rows * weight_bytes, bytes_accessed=weight_bytes, transcendentals=0
        ),
        name="experts",
    )(
        in_vmem(gathered),
        in_vmem(gain_near),
        in_vmem(gate_weight),
        in_vmem(up_weight),
        in_vmem(down_weight),
    )
    arrived = lax.all_to_all(result, ("ep", "head"), 0, 0, tiled=True)
    local_sum = jnp.sum(arrived.astype(F32), 0).astype(BF)
    expert_sum = sum_over(local_sum, "side").astype(BF)
    return (after_attention, expert_sum)


def solution(mesh):
    placed = (
        P(("groups", "ep"), None),
        P(("groups", "ep"), "head", "side"),
        P(("groups", "ep"), "head"),
        P(("groups", "ep"), "head"),
        P(("groups", "ep"), None, "head"),
        P(("groups", "ep"), None, "head"),
        P(("groups", "ep")),
        P("head", "side", None),
        P(),
        P(("groups", "ep"), None),
        P(("groups", "ep"), None),
        P(("ep", "side"), None, "head"),
        P(("ep", "side"), None, "head"),
        P(("ep", "side"), "head", None),
    )
    return jax.shard_map(
        on_device,
        mesh=mesh,
        in_specs=placed,
        out_specs=(P(("groups", "ep"), "head"), P(("groups", "ep"), "head")),
        check_vma=False,
    )
```

time: 62.3 us -> 39.4 us (0.63)
  matrix products: 24.9 us -> 0 us
  Pallas kernels: 0 us -> 9.16 us
  other arithmetic: 6.48 us -> 0.68 us
  starting transfers between devices: 15.1 us -> 11.6 us
  waiting for transfers between devices: 12.9 us -> 16.3 us
  local copies, waits for them, and re-layouts: 1.56 us -> 0.65 us
    dot_general x6 -> x0, matrix products: 24.9 us -> none  [the longest x1 12.6 us: on_device(): jnp.einsum('lnf,lfd->nd', inner, down_weight, preferred_element_type=F32)]
    pallas_call x0 -> x3, Pallas kernels: none -> 9.16 us  [the longest x1 5.79 us: on_device(): pl.pallas_call(functools.partial(expert_kernel, width=width), out_shape=j...]
    all_to_all x0 -> x1, waiting for transfers between devices: none -> 7.28 us  [on_device(): arrived = lax.all_to_all(result, ('ep', 'head'), 0, 0, tiled=True)]
    ppermute x8 -> x6, starting transfers between devices: 15.1 us -> 8.23 us  [swap(): return lax.ppermute(x, axis, [(i, i ^ k) for i in range(count)])]
    ppermute x8 -> x6, waiting for transfers between devices: 12.9 us -> 9.03 us  [swap(): return lax.ppermute(x, axis, [(i, i ^ k) for i in range(count)])]
    all_to_all x0 -> x1, starting transfers between devices: none -> 3.37 us  [on_device(): arrived = lax.all_to_all(result, ('ep', 'head'), 0, 0, tiled=True)]
    reduce_sum x4 -> x1, other arithmetic: 2.66 us -> 0.02 us  [on_device(): local_sum = jnp.sum(arrived.astype(F32), 0).astype(BF)]
    convert_element_type x8 -> x3, other arithmetic: 2.14 us -> 0.63 us  [the longest x1 0.61 us: on_device(): expert_sum = sum_over(local_sum, 'side').astype(BF)]
  transfers between devices with their start and end apart: 8 -> 7, of which waited for: 7 -> 6; matrix products, arithmetic and copies ran while one was open for 5% -> 2% of each run, Pallas kernels for 0% -> 0%
where the time goes in v2:
time: 39.4 us; the launch traced here: 39.1 us
  waiting for transfers between devices  16.3 us (41%)
  starting transfers between devices  11.6 us (29%)
  Pallas kernels  9.16 us (23%)
  between operations  0.73 us (2%)
  other arithmetic  0.68 us (2%)
  local copies, waits for them, and re-layouts  0.65 us (2%)
    ppermute x6, waiting for transfers between devices, swap(): return lax.ppermute(x, axis, [(i, i ^ k) for i in range(count)])  9.03 us
    ppermute x6, starting transfers between devices, swap(): return lax.ppermute(x, axis, [(i, i ^ k) for i in range(count)])  8.23 us
    all_to_all x1, waiting for transfers between devices, on_device(): arrived = lax.all_to_all(result, ('ep', 'head'), 0, 0, tiled=True)  7.28 us
    pallas_call x1, Pallas kernels, on_device(): pl.pallas_call(functools.partial(expert_kernel, width=width), out_shape=j...  5.79 us
    all_to_all x1, starting transfers between devices, on_device(): arrived = lax.all_to_all(result, ('ep', 'head'), 0, 0, tiled=True)  3.37 us
    pallas_call x1, Pallas kernels, on_device(): pl.pallas_call(attend_kernel, out_shape=(pltpu.VMEM((rows, out_weight.sha...  2.72 us
  transfers between devices with their start and end apart: 7, of which 6 were waited for; matrix products, arithmetic and copies ran while one was open for 2% of the time, Pallas kernels for 0%

profile of v2, /device:TPU:0, one launch (start us, length us, event | category | flops | bytes accessed | tf_op | source)
XLA Modules:
  0.0 39.1 jit_solution(15078339247193854787)
XLA Ops:
  0.6 2.7 %attend.1 = (bf16[8,1024]{1,0:T(8,128)(2,1)S(1)}, bf16[8,128]{1,0:T(8,128)(2,1)S(1)}, bf16[8,2048]{1,0:T(8,128)(2,1)S(1)}, f32[1,2048]{1,0:T(1,128)S(1)}, bf16[2,512,2048]{2,1,0:T(8,128)(2,1)S(1)}) custom-call(s32[8]{0:T(128)} %lengths_hbm.1, bf16[8,2,512]{2,1,0:T(2,128)(2,1)} %query_hbm.1, bf16[8,256]{1,0:T(8,128)(2,1)} %new_key_hbm.1, ...), custom_call_target="tpu_custom_call" | custom-call | tf_op jit(solution)/shard_map/attend/pallas_call | solution.py:233
  3.4 0.0 copy-start
  3.4 0.0 copy-start.1
  3.4 0.0 copy-start.2
  3.4 0.7 %project.1 = bf16[8,2048]{1,0:T(8,128)(2,1)S(1)} custom-call(bf16[8,1024]{1,0:T(8,128)(2,1)S(1)} %get-tuple-element.7.attended, bf16[2,512,2048]{2,1,0:T(8,128)(2,1)S(1)} %get-tuple-element.8.out_weight, bf16[8,2048]{1,0:T(8,128)(2,1)S(1)} %get-tuple-element.9.hidden), custom_call_target="tpu_custom_call" | custom-call | flops 999999995904 | bytes 200000000 | tf_op jit(solution)/shard_map/project/pallas_call | solution.py:270
  4.0 0.5 %collective-permute-start = (bf16[8,2048]{1,0:T(8,128)(2,1)S(1)}, bf16[8,2048]{1,0:T(8,128)(2,1)S(1)}, u32[]{:S(2)}, u32[]{:S(2)}) collective-permute-start(bf16[8,2048]{1,0:T(8,128)(2,1)S(1)} %project.1), channel_id=1, source_target_pairs={{0,2},{2,0},{1,3},{3,1},{4,6},{6,4},{5,7},{7,5},{8,10},{10,8},{9,1... | collective-permute-start | bytes 98312 | tf_op jit(solution)/shard_map/ppermute | solution.py:37
  4.6 0.9 %collective-permute-done = bf16[8,2048]{1,0:T(8,128)(2,1)S(1)} collective-permute-done((bf16[8,2048]{1,0:T(8,128)(2,1)S(1)}, bf16[8,2048]{1,0:T(8,128)(2,1)S(1)}, u32[]{:S(2)}, u32[]{:S(2)}) %collective-permute-start) | collective-permute-done | bytes 32800 | tf_op jit(solution)/shard_map/ppermute | solution.py:37
  5.4 2.9 %collective-permute-start.1 = (bf16[8,2048]{1,0:T(8,128)(2,1)S(1)}, bf16[8,2048]{1,0:T(8,128)(2,1)S(1)}, u32[]{:S(2)}, u32[]{:S(2)}) collective-permute-start(bf16[8,2048]{1,0:T(8,128)(2,1)S(1)} %add_convert_fusion), channel_id=1, source_target_pairs={{0,1},{1,0},{2,3},{3,2},{4,5},{5,4},{6,7},{7,6},{8,9},{9,8},{10,11... | collective-permute-start | bytes 98312 | tf_op jit(solution)/shard_map/ppermute | solution.py:37
  8.3 1.9 %collective-permute-done.1 = bf16[8,2048]{1,0:T(8,128)(2,1)S(1)} collective-permute-done((bf16[8,2048]{1,0:T(8,128)(2,1)S(1)}, bf16[8,2048]{1,0:T(8,128)(2,1)S(1)}, u32[]{:S(2)}, u32[]{:S(2)}) %collective-permute-start.1) | collective-permute-done | bytes 32800 | tf_op jit(solution)/shard_map/ppermute | solution.py:37
  10.2 2.2 %collective-permute-start.2 = (bf16[8,2176]{1,0:T(8,128)(2,1)S(1)}, bf16[8,2176]{1,0:T(8,128)(2,1)S(1)}, u32[]{:S(2)}, u32[]{:S(2)}) collective-permute-start(bf16[8,2176]{1,0:T(8,128)(2,1)S(1)} %pad_maximum_fusion.1), channel_id=1, source_target_pairs={{0,4},{4,0},{8,12},{12,8},{1,5},{5,1},{9,13},{13,9},{2,6},{6,2},{1... | collective-permute-start | bytes 104456 | tf_op jit(solution)/shard_map/ppermute | solution.py:37
  12.4 2.6 %collective-permute-start.3 = (bf16[8,2176]{1,0:T(8,128)(2,1)S(1)}, bf16[8,2176]{1,0:T(8,128)(2,1)S(1)}, u32[]{:S(2)}, u32[]{:S(2)}) collective-permute-start(bf16[8,2176]{1,0:T(8,128)(2,1)S(1)} %pad_maximum_fusion.1), channel_id=1, source_target_pairs={{0,8},{4,12},{8,0},{12,4},{1,9},{5,13},{9,1},{13,5},{2,10},{6,14},... | collective-permute-start | bytes 104456 | tf_op jit(solution)/shard_map/ppermute | solution.py:37
  15.0 0.0 collective-permute-start.4
  15.0 0.0 collective-permute-done.2
  15.0 2.5 %collective-permute-done.3 = bf16[8,2176]{1,0:T(8,128)(2,1)S(1)} collective-permute-done((bf16[8,2176]{1,0:T(8,128)(2,1)S(1)}, bf16[8,2176]{1,0:T(8,128)(2,1)S(1)}, u32[]{:S(2)}, u32[]{:S(2)}) %collective-permute-start.3) | collective-permute-done | bytes 34848 | tf_op jit(solution)/shard_map/ppermute | solution.py:37
  17.5 3.2 %collective-permute-done.4 = bf16[8,2176]{1,0:T(8,128)(2,1)S(1)} collective-permute-done((bf16[8,2176]{1,0:T(8,128)(2,1)S(1)}, bf16[8,2176]{1,0:T(8,128)(2,1)S(1)}, u32[]{:S(2)}, u32[]{:S(2)}) %collective-permute-start.4) | collective-permute-done | bytes 34848 | tf_op jit(solution)/shard_map/ppermute | solution.py:37
  20.7 0.0 copy-done
  20.8 0.0 copy-done.1
  20.8 0.0 copy-done.2
  20.8 5.8 %experts.1 = bf16[8,8,1024]{2,1,0:T(8,128)(2,1)} custom-call(bf16[32,2176]{1,0:T(8,128)(2,1)S(1)} %pad_maximum_fusion.gathered, f32[1,2048]{1,0:T(1,128)S(1)} %get-tuple-element.11.norm_gain, bf16[8,2048,384]{2,1,0:T(8,128)(2,1)S(1)} %copy-done, bf16[8,2048,384]{2,1,0:T(8,128)(2,1)S(1)} %copy-done.1, bf16[8,384,2048]{2,1,0:T(8,128)(2,1)S(1)} %copy-done.2), custom_call_target="tpu_custom_call" | custom-call | flops 1207959552 | bytes 37748736 | tf_op jit(solution)/shard_map/experts/pallas_call | solution.py:293
  26.6 3.4 %all-to-all-start = ((bf16[8,8,1024]{2,1,0:T(8,128)(2,1)}), bf16[8,8,1024]{2,1,0:T(8,128)(2,1)S(1)}, u32[]{:S(2)}, u32[]{:S(2)}) async-start(bf16[8,8,1024]{2,1,0:T(8,128)(2,1)} %experts.1), calls=%async_computation | async-start | bytes 262144 | tf_op jit(solution)/shard_map/all_to_all | solution.py:311
  30.0 7.3 %all-to-all-done = bf16[8,8,1024]{2,1,0:T(8,128)(2,1)S(1)} async-done(((bf16[8,8,1024]{2,1,0:T(8,128)(2,1)}), bf16[8,8,1024]{2,1,0:T(8,128)(2,1)S(1)}, u32[]{:S(2)}, u32[]{:S(2)}) %all-to-all-start) | async-done | bytes 131104 | tf_op jit(solution)/shard_map/all_to_all | solution.py:311
  37.3 0.1 collective-permute-start.5
  37.3 0.6 %constant_dynamic-slice_fusion = f32[8,1024]{1,0:T(8,128)} fusion(f32[8,2048]{1,0:T(8,128)S(1)} %get-tuple-element.13, s32[]{:T(128)S(6)} %select_n.3), kind=kLoop, calls=%fused_computation.5 | loop fusion | bytes 65540 | tf_op jit(solution)/shard_map/dynamic_slice | solution.py:282
  38.0 0.5 %collective-permute-done.5 = bf16[8,1024]{1,0:T(8,128)(2,1)S(1)} collective-permute-done((bf16[8,1024]{1,0:T(8,128)(2,1)S(1)}, bf16[8,1024]{1,0:T(8,128)(2,1)S(1)}, u32[]{:S(2)}, u32[]{:S(2)}) %collective-permute-start.5) | collective-permute-done | bytes 16416 | tf_op jit(solution)/shard_map/ppermute | solution.py:37
  38.5 0.6 %add_convert_fusion.1 = bf16[8,1024]{1,0:T(8,128)(2,1)} fusion(bf16[8,1024]{1,0:T(8,128)(2,1)S(1)} %collective-permute-done.5, bf16[8,1024]{1,0:T(8,128)(2,1)S(1)} %reduce_sum.12), kind=kLoop, calls=%fused_computation.4 | loop fusion | flops 32768 | bytes 49152 | tf_op jit(solution)/shard_map/convert_element_type | solution.py:313
  (5 shorter events, 0.1 us)
Async XLA Ops:
  3.4 17.4 %copy-start = (bf16[8,2048,384]{2,1,0:T(8,128)(2,1)S(1)}, bf16[8,2048,384]{2,1,0:T(8,128)(2,1)}, u32[]{:S(2)}) copy-start(bf16[8,2048,384]{2,1,0:T(8,128)(2,1)} %gate_weight.1) | copy-start | bytes 37748740
  3.4 17.4 %copy-start.1 = (bf16[8,2048,384]{2,1,0:T(8,128)(2,1)S(1)}, bf16[8,2048,384]{2,1,0:T(8,128)(2,1)}, u32[]{:S(2)}) copy-start(bf16[8,2048,384]{2,1,0:T(8,128)(2,1)} %up_weight.1) | copy-start | bytes 37748740
  3.4 17.4 %copy-start.2 = (bf16[8,384,2048]{2,1,0:T(8,128)(2,1)S(1)}, bf16[8,384,2048]{2,1,0:T(8,128)(2,1)}, u32[]{:S(2)}) copy-start(bf16[8,384,2048]{2,1,0:T(8,128)(2,1)} %down_weight.1) | copy-start | bytes 37748740
  4.0 1.4 %collective-permute-start = (bf16[8,2048]{1,0:T(8,128)(2,1)S(1)}, bf16[8,2048]{1,0:T(8,128)(2,1)S(1)}, u32[]{:S(2)}, u32[]{:S(2)}) collective-permute-start(bf16[8,2048]{1,0:T(8,128)(2,1)S(1)} %project.1), channel_id=1, source_target_pairs={{0,2},{2,0},{1,3},{3,1},{4,6},{6,4},{5,7},{7,5},{8,10},{10,8},{9,1... | collective-permute-start | bytes 98312 | tf_op jit(solution)/shard_map/ppermute | solution.py:37
  5.4 4.8 %collective-permute-start.1 = (bf16[8,2048]{1,0:T(8,128)(2,1)S(1)}, bf16[8,2048]{1,0:T(8,128)(2,1)S(1)}, u32[]{:S(2)}, u32[]{:S(2)}) collective-permute-start(bf16[8,2048]{1,0:T(8,128)(2,1)S(1)} %add_convert_fusion), channel_id=1, source_target_pairs={{0,1},{1,0},{2,3},{3,2},{4,5},{5,4},{6,7},{7,6},{8,9},{9,8},{10,11... | collective-permute-start | bytes 98312 | tf_op jit(solution)/shard_map/ppermute | solution.py:37
  10.2 4.8 %collective-permute-start.2 = (bf16[8,2176]{1,0:T(8,128)(2,1)S(1)}, bf16[8,2176]{1,0:T(8,128)(2,1)S(1)}, u32[]{:S(2)}, u32[]{:S(2)}) collective-permute-start(bf16[8,2176]{1,0:T(8,128)(2,1)S(1)} %pad_maximum_fusion.1), channel_id=1, source_target_pairs={{0,4},{4,0},{8,12},{12,8},{1,5},{5,1},{9,13},{13,9},{2,6},{6,2},{1... | collective-permute-start | bytes 104456 | tf_op jit(solution)/shard_map/ppermute | solution.py:37
  12.4 5.1 %collective-permute-start.3 = (bf16[8,2176]{1,0:T(8,128)(2,1)S(1)}, bf16[8,2176]{1,0:T(8,128)(2,1)S(1)}, u32[]{:S(2)}, u32[]{:S(2)}) collective-permute-start(bf16[8,2176]{1,0:T(8,128)(2,1)S(1)} %pad_maximum_fusion.1), channel_id=1, source_target_pairs={{0,8},{4,12},{8,0},{12,4},{1,9},{5,13},{9,1},{13,5},{2,10},{6,14},... | collective-permute-start | bytes 104456 | tf_op jit(solution)/shard_map/ppermute | solution.py:37
  15.0 5.7 %collective-permute-start.4 = (bf16[8,2176]{1,0:T(8,128)(2,1)S(1)}, bf16[8,2176]{1,0:T(8,128)(2,1)S(1)}, u32[]{:S(2)}, u32[]{:S(2)}) collective-permute-start(bf16[8,2176]{1,0:T(8,128)(2,1)S(1)} %pad_maximum_fusion.1), channel_id=1, source_target_pairs={{0,12},{4,8},{8,4},{12,0},{1,13},{5,9},{9,5},{13,1},{2,14},{6,10},... | collective-permute-start | bytes 104456 | tf_op jit(solution)/shard_map/ppermute | solution.py:37
  26.6 10.7 %all-to-all-start = ((bf16[8,8,1024]{2,1,0:T(8,128)(2,1)}), bf16[8,8,1024]{2,1,0:T(8,128)(2,1)S(1)}, u32[]{:S(2)}, u32[]{:S(2)}) async-start(bf16[8,8,1024]{2,1,0:T(8,128)(2,1)} %experts.1), calls=%async_computation | async-start | bytes 262144 | tf_op jit(solution)/shard_map/all_to_all | solution.py:311
  37.3 1.2 %collective-permute-start.5 = (bf16[8,1024]{1,0:T(8,128)(2,1)S(1)}, bf16[8,1024]{1,0:T(8,128)(2,1)S(1)}, u32[]{:S(2)}, u32[]{:S(2)}) collective-permute-start(bf16[8,1024]{1,0:T(8,128)(2,1)S(1)} %reduce_sum.12), channel_id=1, source_target_pairs={{0,2},{2,0},{1,3},{3,1},{4,6},{6,4},{5,7},{7,5},{8,10},{10,8},{9,1... | collective-permute-start | bytes 49160 | tf_op jit(solution)/shard_map/ppermute | solution.py:37

commit v3 on v2

--- a/solution.py
+++ b/solution.py
@@ -35,6 +35,50 @@
 def swap(x, axis, k):
     count = lax.axis_size(axis)
     return lax.ppermute(x, axis, [(i, i ^ k) for i in range(count)])
+
+
+def joint(x, axes, partner):
+    sizes = [lax.axis_size(axis) for axis in axes]
+    pairs = []
+    for source in range(math.prod(sizes)):
+        rest, place = source, []
+        for size in reversed(sizes):
+            place.insert(0, rest % size)
+            rest //= size
+        target = 0
+        for size, index in zip(sizes, partner(*place)):
+            target = target * size + index
+        pairs.append((source, target))
+    return lax.ppermute(x, axes, pairs)
+
+
+def sum_heads(low):
+    flip = min(lax.axis_size("side") - 1, 1)
+    total = low.astype(F32)
+    for k in partners(lax.axis_size("head")):
+        low = total.astype(BF)
+        other = joint(low, ("side", "head"), lambda s, h: (s ^ flip, h ^ k))
+        total = low.astype(F32) + other.astype(F32)
+    return total
+
+
+def gather_rows(packed):
+    ep_count, side_count = lax.axis_size("ep"), lax.axis_size("side")
+    if (ep_count, side_count) == (4, 2):
+        far = joint(packed, ("ep", "side"), lambda e, s: (e ^ (2 + s), s))
+        near = joint(packed, ("ep", "side"), lambda e, s: (e ^ 1, s ^ 1))
+        return jnp.concatenate([packed, near, far, swap(far, "side", 1)], 0)
+    for k in partners(ep_count):
+        packed = jnp.concatenate([packed, swap(packed, "ep", k)], 0)
+    return packed
+
+
+def source_of(block):
+    me = lax.axis_index("ep")
+    if (lax.axis_size("ep"), lax.axis_size("side")) == (4, 2) and block >= 2:
+        side = lax.axis_index("side")
+        return me ^ (block + side if block == 2 else block - side)
+    return me ^ block
 
 
 def sum_over(low, axis):
@@ -197,7 +241,7 @@
     blocks, block_rows, _ = out.shape
     heads = depth // width
     for j in range(blocks // heads):
-        target = me ^ j
+        target = source_of(j)
         for h in range(heads):
             out[target * heads + h] = result[
                 j * block_rows : (j + 1) * block_rows, h * width : (h + 1) * width
@@ -278,17 +322,10 @@
         ),
         name="project",
     )(in_vmem(attended), in_vmem(out_weight_near), in_vmem(hidden_near))
-    stream = sum_over(sum_over(partial_value, "side").astype(BF), "head")
+    stream = sum_heads(sum_over(partial_value, "side").astype(BF))
     after_attention = lax.dynamic_slice_in_dim(stream, head_index * width, width, 1)
     packed = jnp.concatenate([stream.astype(BF), coefficient], 1)
-    if ep_count <= 4:
-        gathered = jnp.concatenate(
-            [packed] + [swap(packed, "ep", k) for k in range(1, ep_count)], 0
-        )
-    else:
-        gathered = packed
-        for k in partners(ep_count):
-            gathered = jnp.concatenate([gathered, swap(gathered, "ep", k)], 0)
+    gathered = gather_rows(packed)
     weight_bytes = 2 * (gate_weight.size + up_weight.size + down_weight.size)
     result = pl.pallas_call(
         functools.partial(expert_kernel, width=width),

time: 39.4 us -> 38.1 us (0.967)
  waiting for transfers between devices: 16.3 us -> 13.4 us
  starting transfers between devices: 11.6 us -> 13.3 us
    ppermute x6 -> x3, waiting for transfers between devices: 9.03 us -> 1.41 us  [swap(): return lax.ppermute(x, axis, [(i, i ^ k) for i in range(count)])]
    ppermute x6 -> x3, starting transfers between devices: 8.23 us -> 0.87 us  [swap(): return lax.ppermute(x, axis, [(i, i ^ k) for i in range(count)])]
    ppermute x0 -> x3, starting transfers between devices: none -> 5.85 us  [joint(): return lax.ppermute(x, axes, pairs)]
    ppermute x0 -> x3, waiting for transfers between devices: none -> 4.61 us  [joint(): return lax.ppermute(x, axes, pairs)]
    all_to_all x1, starting transfers between devices: 3.37 us -> 6.53 us  [on_device(): arrived = lax.all_to_all(result, ('ep', 'head'), 0, 0, tiled=True)]
where the time goes in v3:
time: 38.1 us; the launch traced here: 37.8 us
  waiting for transfers between devices  13.4 us (35%)
  starting transfers between devices  13.3 us (35%)
  Pallas kernels  9.16 us (24%)
  between operations  0.72 us (2%)
  other arithmetic  0.68 us (2%)
  local copies, waits for them, and re-layouts  0.65 us (2%)
    all_to_all x1, waiting for transfers between devices, on_device(): arrived = lax.all_to_all(result, ('ep', 'head'), 0, 0, tiled=True)  7.34 us
    all_to_all x1, starting transfers between devices, on_device(): arrived = lax.all_to_all(result, ('ep', 'head'), 0, 0, tiled=True)  6.53 us
    ppermute x3, starting transfers between devices, joint(): return lax.ppermute(x, axes, pairs)  5.85 us
    pallas_call x1, Pallas kernels, on_device(): pl.pallas_call(functools.partial(expert_kernel, width=width), out_shape=j...  5.79 us
    ppermute x3, waiting for transfers between devices, joint(): return lax.ppermute(x, axes, pairs)  4.61 us
    pallas_call x1, Pallas kernels, on_device(): pl.pallas_call(attend_kernel, out_shape=(pltpu.VMEM((rows, out_weight.sha...  2.72 us
    ppermute x3, waiting for transfers between devices, swap(): return lax.ppermute(x, axis, [(i, i ^ k) for i in range(count)])  1.41 us
    ppermute x3, starting transfers between devices, swap(): return lax.ppermute(x, axis, [(i, i ^ k) for i in range(count)])  0.87 us
  transfers between devices with their start and end apart: 7, of which 6 were waited for; matrix products, arithmetic and copies ran while one was open for 2% of the time, Pallas kernels for 0%

profile of v3, /device:TPU:0, one launch (start us, length us, event | category | flops | bytes accessed | tf_op | source)
XLA Modules:
  0.0 37.8 jit_solution(1258457206519306391)
XLA Ops:
  0.6 2.7 %attend.1 = (bf16[8,1024]{1,0:T(8,128)(2,1)S(1)}, bf16[8,128]{1,0:T(8,128)(2,1)S(1)}, bf16[8,2048]{1,0:T(8,128)(2,1)S(1)}, f32[1,2048]{1,0:T(1,128)S(1)}, bf16[2,512,2048]{2,1,0:T(8,128)(2,1)S(1)}) custom-call(s32[8]{0:T(128)} %lengths_hbm.1, bf16[8,2,512]{2,1,0:T(2,128)(2,1)} %query_hbm.1, bf16[8,256]{1,0:T(8,128)(2,1)} %new_key_hbm.1, ...), custom_call_target="tpu_custom_call" | custom-call | tf_op jit(solution)/shard_map/attend/pallas_call | solution.py:277
  3.4 0.0 copy-start
  3.4 0.0 copy-start.1
  3.4 0.0 copy-start.2
  3.4 0.7 %project.1 = bf16[8,2048]{1,0:T(8,128)(2,1)S(1)} custom-call(bf16[8,1024]{1,0:T(8,128)(2,1)S(1)} %get-tuple-element.7.attended, bf16[2,512,2048]{2,1,0:T(8,128)(2,1)S(1)} %get-tuple-element.8.out_weight, bf16[8,2048]{1,0:T(8,128)(2,1)S(1)} %get-tuple-element.9.hidden), custom_call_target="tpu_custom_call" | custom-call | flops 999999995904 | bytes 200000000 | tf_op jit(solution)/shard_map/project/pallas_call | solution.py:314
  4.0 0.5 %collective-permute-start = (bf16[8,2048]{1,0:T(8,128)(2,1)S(1)}, bf16[8,2048]{1,0:T(8,128)(2,1)S(1)}, u32[]{:S(2)}, u32[]{:S(2)}) collective-permute-start(bf16[8,2048]{1,0:T(8,128)(2,1)S(1)} %project.1), channel_id=1, source_target_pairs={{0,2},{2,0},{1,3},{3,1},{4,6},{6,4},{5,7},{7,5},{8,10},{10,8},{9,1... | collective-permute-start | bytes 98312 | tf_op jit(solution)/shard_map/ppermute | solution.py:37
  4.6 0.9 %collective-permute-done = bf16[8,2048]{1,0:T(8,128)(2,1)S(1)} collective-permute-done((bf16[8,2048]{1,0:T(8,128)(2,1)S(1)}, bf16[8,2048]{1,0:T(8,128)(2,1)S(1)}, u32[]{:S(2)}, u32[]{:S(2)}) %collective-permute-start) | collective-permute-done | bytes 32800 | tf_op jit(solution)/shard_map/ppermute | solution.py:37
  5.4 2.7 %collective-permute-start.1 = (bf16[8,2048]{1,0:T(8,128)(2,1)S(1)}, bf16[8,2048]{1,0:T(8,128)(2,1)S(1)}, u32[]{:S(2)}, u32[]{:S(2)}) collective-permute-start(bf16[8,2048]{1,0:T(8,128)(2,1)S(1)} %add_convert_fusion), channel_id=1, source_target_pairs={{0,3},{1,2},{2,1},{3,0},{4,7},{5,6},{6,5},{7,4},{8,11},{9,10},{10,... | collective-permute-start | bytes 98312 | tf_op jit(solution)/shard_map/ppermute | solution.py:52
  8.1 1.6 %collective-permute-done.1 = bf16[8,2048]{1,0:T(8,128)(2,1)S(1)} collective-permute-done((bf16[8,2048]{1,0:T(8,128)(2,1)S(1)}, bf16[8,2048]{1,0:T(8,128)(2,1)S(1)}, u32[]{:S(2)}, u32[]{:S(2)}) %collective-permute-start.1) | collective-permute-done | bytes 32800 | tf_op jit(solution)/shard_map/ppermute | solution.py:52
  9.7 3.1 %collective-permute-start.3 = (bf16[8,2176]{1,0:T(8,128)(2,1)S(1)}, bf16[8,2176]{1,0:T(8,128)(2,1)S(1)}, u32[]{:S(2)}, u32[]{:S(2)}) collective-permute-start(bf16[8,2176]{1,0:T(8,128)(2,1)S(1)} %pad_maximum_fusion.1), channel_id=1, source_target_pairs={{0,8},{2,14},{4,12},{6,10},{8,0},{10,6},{12,4},{14,2},{1,9},{3,15}... | collective-permute-start | bytes 104456 | tf_op jit(solution)/shard_map/ppermute | solution.py:52
  12.9 0.1 collective-permute-start.2
  12.9 1.9 %collective-permute-done.3 = bf16[8,2176]{1,0:T(8,128)(2,1)S(1)} collective-permute-done((bf16[8,2176]{1,0:T(8,128)(2,1)S(1)}, bf16[8,2176]{1,0:T(8,128)(2,1)S(1)}, u32[]{:S(2)}, u32[]{:S(2)}) %collective-permute-start.3) | collective-permute-done | bytes 34848 | tf_op jit(solution)/shard_map/ppermute | solution.py:52
  14.8 0.3 collective-permute-start.4
  15.1 1.1 %collective-permute-done.2 = bf16[8,2176]{1,0:T(8,128)(2,1)S(1)} collective-permute-done((bf16[8,2176]{1,0:T(8,128)(2,1)S(1)}, bf16[8,2176]{1,0:T(8,128)(2,1)S(1)}, u32[]{:S(2)}, u32[]{:S(2)}) %collective-permute-start.2) | collective-permute-done | bytes 34848 | tf_op jit(solution)/shard_map/ppermute | solution.py:52
  16.2 0.0 collective-permute-done.4
  16.2 0.0 copy-done
  16.2 0.0 copy-done.1
  16.3 0.0 copy-done.2
  16.3 5.8 %experts.1 = bf16[8,8,1024]{2,1,0:T(8,128)(2,1)} custom-call(bf16[32,2176]{1,0:T(8,128)(2,1)S(1)} %pad_maximum_fusion.gathered, f32[1,2048]{1,0:T(1,128)S(1)} %get-tuple-element.11.norm_gain, bf16[8,2048,384]{2,1,0:T(8,128)(2,1)S(1)} %copy-done, bf16[8,2048,384]{2,1,0:T(8,128)(2,1)S(1)} %copy-done.1, bf16[8,384,2048]{2,1,0:T(8,128)(2,1)S(1)} %copy-done.2), custom_call_target="tpu_custom_call" | custom-call | flops 1207959552 | bytes 37748736 | tf_op jit(solution)/shard_map/experts/pallas_call | solution.py:330
  22.1 6.5 %all-to-all-start = ((bf16[8,8,1024]{2,1,0:T(8,128)(2,1)}), bf16[8,8,1024]{2,1,0:T(8,128)(2,1)S(1)}, u32[]{:S(2)}, u32[]{:S(2)}) async-start(bf16[8,8,1024]{2,1,0:T(8,128)(2,1)} %experts.1), calls=%async_computation | async-start | bytes 262144 | tf_op jit(solution)/shard_map/all_to_all | solution.py:348
  28.6 7.3 %all-to-all-done = bf16[8,8,1024]{2,1,0:T(8,128)(2,1)S(1)} async-done(((bf16[8,8,1024]{2,1,0:T(8,128)(2,1)}), bf16[8,8,1024]{2,1,0:T(8,128)(2,1)S(1)}, u32[]{:S(2)}, u32[]{:S(2)}) %all-to-all-start) | async-done | bytes 131104 | tf_op jit(solution)/shard_map/all_to_all | solution.py:348
  36.0 0.1 collective-permute-start.5
  36.0 0.6 %constant_dynamic-slice_fusion = f32[8,1024]{1,0:T(8,128)} fusion(f32[8,2048]{1,0:T(8,128)S(1)} %get-tuple-element.13, s32[]{:T(128)S(6)} %select_n.3), kind=kLoop, calls=%fused_computation.5 | loop fusion | bytes 65540 | tf_op jit(solution)/shard_map/dynamic_slice | solution.py:326
  36.7 0.5 %collective-permute-done.5 = bf16[8,1024]{1,0:T(8,128)(2,1)S(1)} collective-permute-done((bf16[8,1024]{1,0:T(8,128)(2,1)S(1)}, bf16[8,1024]{1,0:T(8,128)(2,1)S(1)}, u32[]{:S(2)}, u32[]{:S(2)}) %collective-permute-start.5) | collective-permute-done | bytes 16416 | tf_op jit(solution)/shard_map/ppermute | solution.py:37
  37.2 0.6 %add_convert_fusion.1 = bf16[8,1024]{1,0:T(8,128)(2,1)} fusion(bf16[8,1024]{1,0:T(8,128)(2,1)S(1)} %collective-permute-done.5, bf16[8,1024]{1,0:T(8,128)(2,1)S(1)} %reduce_sum.12), kind=kLoop, calls=%fused_computation.4 | loop fusion | flops 32768 | bytes 49152 | tf_op jit(solution)/shard_map/convert_element_type | solution.py:350
  (5 shorter events, 0.1 us)
Async XLA Ops:
  3.4 12.9 %copy-start = (bf16[8,2048,384]{2,1,0:T(8,128)(2,1)S(1)}, bf16[8,2048,384]{2,1,0:T(8,128)(2,1)}, u32[]{:S(2)}) copy-start(bf16[8,2048,384]{2,1,0:T(8,128)(2,1)} %gate_weight.1) | copy-start | bytes 37748740
  3.4 12.9 %copy-start.1 = (bf16[8,2048,384]{2,1,0:T(8,128)(2,1)S(1)}, bf16[8,2048,384]{2,1,0:T(8,128)(2,1)}, u32[]{:S(2)}) copy-start(bf16[8,2048,384]{2,1,0:T(8,128)(2,1)} %up_weight.1) | copy-start | bytes 37748740
  3.4 12.9 %copy-start.2 = (bf16[8,384,2048]{2,1,0:T(8,128)(2,1)S(1)}, bf16[8,384,2048]{2,1,0:T(8,128)(2,1)}, u32[]{:S(2)}) copy-start(bf16[8,384,2048]{2,1,0:T(8,128)(2,1)} %down_weight.1) | copy-start | bytes 37748740
  4.0 1.4 %collective-permute-start = (bf16[8,2048]{1,0:T(8,128)(2,1)S(1)}, bf16[8,2048]{1,0:T(8,128)(2,1)S(1)}, u32[]{:S(2)}, u32[]{:S(2)}) collective-permute-start(bf16[8,2048]{1,0:T(8,128)(2,1)S(1)} %project.1), channel_id=1, source_target_pairs={{0,2},{2,0},{1,3},{3,1},{4,6},{6,4},{5,7},{7,5},{8,10},{10,8},{9,1... | collective-permute-start | bytes 98312 | tf_op jit(solution)/shard_map/ppermute | solution.py:37
  5.4 4.3 %collective-permute-start.1 = (bf16[8,2048]{1,0:T(8,128)(2,1)S(1)}, bf16[8,2048]{1,0:T(8,128)(2,1)S(1)}, u32[]{:S(2)}, u32[]{:S(2)}) collective-permute-start(bf16[8,2048]{1,0:T(8,128)(2,1)S(1)} %add_convert_fusion), channel_id=1, source_target_pairs={{0,3},{1,2},{2,1},{3,0},{4,7},{5,6},{6,5},{7,4},{8,11},{9,10},{10,... | collective-permute-start | bytes 98312 | tf_op jit(solution)/shard_map/ppermute | solution.py:52
  9.7 5.1 %collective-permute-start.3 = (bf16[8,2176]{1,0:T(8,128)(2,1)S(1)}, bf16[8,2176]{1,0:T(8,128)(2,1)S(1)}, u32[]{:S(2)}, u32[]{:S(2)}) collective-permute-start(bf16[8,2176]{1,0:T(8,128)(2,1)S(1)} %pad_maximum_fusion.1), channel_id=1, source_target_pairs={{0,8},{2,14},{4,12},{6,10},{8,0},{10,6},{12,4},{14,2},{1,9},{3,15}... | collective-permute-start | bytes 104456 | tf_op jit(solution)/shard_map/ppermute | solution.py:52
  12.9 3.4 %collective-permute-start.2 = (bf16[8,2176]{1,0:T(8,128)(2,1)S(1)}, bf16[8,2176]{1,0:T(8,128)(2,1)S(1)}, u32[]{:S(2)}, u32[]{:S(2)}) collective-permute-start(bf16[8,2176]{1,0:T(8,128)(2,1)S(1)} %pad_maximum_fusion.1), channel_id=1, source_target_pairs={{0,6},{2,4},{4,2},{6,0},{8,14},{10,12},{12,10},{14,8},{1,7},{3,5},... | collective-permute-start | bytes 104456 | tf_op jit(solution)/shard_map/ppermute | solution.py:52
  14.8 1.4 %collective-permute-start.4 = (bf16[8,2176]{1,0:T(8,128)(2,1)S(1)}, bf16[8,2176]{1,0:T(8,128)(2,1)S(1)}, u32[]{:S(2)}, u32[]{:S(2)}) collective-permute-start(bf16[8,2176]{1,0:T(8,128)(2,1)S(1)} %collective-permute-done.3), channel_id=1, source_target_pairs={{0,2},{2,0},{1,3},{3,1},{4,6},{6,4},{5,7},{7,5},{8,10},{10,8},{9,1... | collective-permute-start | bytes 104456 | tf_op jit(solution)/shard_map/ppermute | solution.py:37
  22.1 13.9 %all-to-all-start = ((bf16[8,8,1024]{2,1,0:T(8,128)(2,1)}), bf16[8,8,1024]{2,1,0:T(8,128)(2,1)S(1)}, u32[]{:S(2)}, u32[]{:S(2)}) async-start(bf16[8,8,1024]{2,1,0:T(8,128)(2,1)} %experts.1), calls=%async_computation | async-start | bytes 262144 | tf_op jit(solution)/shard_map/all_to_all | solution.py:348
  36.0 1.2 %collective-permute-start.5 = (bf16[8,1024]{1,0:T(8,128)(2,1)S(1)}, bf16[8,1024]{1,0:T(8,128)(2,1)S(1)}, u32[]{:S(2)}, u32[]{:S(2)}) collective-permute-start(bf16[8,1024]{1,0:T(8,128)(2,1)S(1)} %reduce_sum.12), channel_id=1, source_target_pairs={{0,2},{2,0},{1,3},{3,1},{4,6},{6,4},{5,7},{7,5},{8,10},{10,8},{9,1... | collective-permute-start | bytes 49160 | tf_op jit(solution)/shard_map/ppermute | solution.py:37

commit v4 on v3

--- a/solution.py
+++ b/solution.py
@@ -101,11 +101,9 @@
     hidden_hbm,
     norm_gain_hbm,
     out_weight_hbm,
-    attended_out,
+    partial_out,
     coefficient_out,
-    hidden_out,
     norm_gain_out,
-    out_weight_out,
     lengths,
     query,
     new_key,
@@ -114,7 +112,10 @@
     cache_values,
     expert_ids,
     route_weights,
+    hidden,
+    out_weight,
     arrivals,
+    weight_arrivals,
 ):
     moves = [
         (lengths_hbm, lengths),
@@ -125,17 +126,27 @@
         (cache_values_hbm, cache_values),
         (expert_ids_hbm, expert_ids),
         (route_weights_hbm, route_weights),
-        (hidden_hbm, hidden_out),
+        (hidden_hbm, hidden),
         (norm_gain_hbm, norm_gain_out),
-        (out_weight_hbm, out_weight_out),
     ]
     copies = [
         pltpu.make_async_copy(source, target, arrivals.at[i])
         for i, (source, target) in enumerate(moves)
     ]
-    for copy in copies:
+    rows, kv_local, width = query.shape
+    depth = out_weight.shape[2]
+    step = math.gcd(width, 2 * HD)
+    pieces = [(g, c) for g in range(kv_local) for c in range(0, width, step)]
+    weight_copies = [
+        pltpu.make_async_copy(
+            out_weight_hbm.at[g, pl.ds(c, step)],
+            out_weight.at[g, pl.ds(c, step)],
+            weight_arrivals.at[i],
+        )
+        for i, (g, c) in enumerate(pieces)
+    ]
+    for copy in copies + weight_copies:
         copy.start()
-    rows, kv_local, width = query.shape
     context = cache_keys.shape[1]
     heads = width // HD
     total = rows * context
@@ -182,10 +193,12 @@
     mixed = jnp.dot(low, values, preferred_element_type=F32)
     mixed = mixed.reshape(len(pairs), rows, kv_local * HD)
     own_low = own.astype(BF).astype(F32)
+    attended = []
     for i, (g, n) in enumerate(pairs):
         block = slice(g * HD, (g + 1) * HD)
         value = mixed[i][:, block] + own_low[i] * new_value[:, block].astype(F32)
-        attended_out[:, i * HD : (i + 1) * HD] = (value / denominator[i]).astype(BF)
+        attended.append((value / denominator[i]).astype(BF))
+    attended = jnp.concatenate(attended, 1)
     experts = coefficient_out.shape[1] // 2
     weight = route_weights[...]
     share = weight / jnp.sum(weight, 1, keepdims=True)
@@ -198,26 +211,33 @@
     coefficient_out[...] = jnp.concatenate([high, rest], 1)
     for copy in copies[8:]:
         copy.wait()
-
-
-def project_kernel(attended, out_weight, hidden, partial_out):
-    depth = out_weight.shape[2]
-    projected = jnp.dot(
-        attended[...],
-        out_weight[...].reshape(attended.shape[1], depth),
-        preferred_element_type=F32,
-    )
     first = (lax.axis_index("side") == 0) & (lax.axis_index("head") == 0)
-    base = jnp.where(first, hidden[...].astype(F32), F32(0.0))
-    partial_out[...] = (projected + base).astype(BF)
+    projected = jnp.where(first, hidden[...].astype(F32), F32(0.0))
+    for copy, (g, c) in zip(weight_copies, pieces):
+        copy.wait()
+        low = g * width + c
+        projected += jnp.dot(
+            attended[:, low : low + step], out_weight[g, c : c + step], preferred_element_type=F32
+        )
+    partial_out[...] = projected.astype(BF)
+
+
+def add_kernel(mine, other, out):
+    out[...] = (mine[...].astype(F32) + other[...].astype(F32)).astype(BF)
 
 
 def expert_kernel(
-    gathered, norm_gain, gate_weight, up_weight, down_weight, out, inner, width
+    gathered, norm_gain, gate_weight, up_weight, down_weight_hbm, out, inner, total, down_weight, arrivals, width
 ):
     count, depth, hidden_units = gate_weight.shape
     experts = (gathered.shape[1] - depth) // 2
     rows = gathered.shape[0]
+    copies = [
+        pltpu.make_async_copy(down_weight_hbm.at[e], down_weight.at[e], arrivals.at[e])
+        for e in range(count)
+    ]
+    for copy in copies:
+        copy.start()
     stream = gathered[:, :depth].astype(F32)
     norm = lax.rsqrt(jnp.mean(stream * stream, -1, keepdims=True) + 1e-06)
     normed = (stream * norm * norm_gain[...]).astype(BF)
@@ -233,11 +253,20 @@
         share = jnp.sum(jnp.where(lane == first + e, coefficient, F32(0.0)), 1, keepdims=True)
         value = gate / (1.0 + jnp.exp(-gate)) * upper * share
         inner[:, e * hidden_units : (e + 1) * hidden_units] = value.astype(BF)
-    result = jnp.dot(
-        inner[...],
-        down_weight[...].reshape(count * hidden_units, depth),
-        preferred_element_type=F32,
-    ).astype(BF)
+    group = 2 if count % 2 == 0 else 1
+    for low in range(0, count, group):
+        for copy in copies[low : low + group]:
+            copy.wait()
+        part = jnp.dot(
+            inner[:, low * hidden_units : (low + group) * hidden_units],
+            down_weight[low : low + group].reshape(group * hidden_units, depth),
+            preferred_element_type=F32,
+        )
+        if low == 0:
+            total[...] = part
+        else:
+            total[...] += part
+    result = total[...].astype(BF)
     blocks, block_rows, _ = out.shape
     heads = depth // width
     for j in range(blocks // heads):
@@ -246,6 +275,36 @@
             out[target * heads + h] = result[
                 j * block_rows : (j + 1) * block_rows, h * width : (h + 1) * width
             ]
+
+
+def run_experts(gathered, gain, gate_weight, up_weight, down_weight, head_count, ep_count):
+    local_count, depth, hidden_units = gate_weight.shape
+    rows = gathered.shape[0] // ep_count
+    width = depth // head_count
+    weight_bytes = 2 * (gate_weight.size + up_weight.size + down_weight.size)
+    return pl.pallas_call(
+        functools.partial(expert_kernel, width=width),
+        out_shape=jax.ShapeDtypeStruct((ep_count * head_count, rows, width), BF),
+        in_specs=[VMEM] * 4 + [HBM],
+        out_specs=VMEM,
+        scratch_shapes=[
+            pltpu.VMEM((ep_count * rows, local_count * hidden_units), BF),
+            pltpu.VMEM((ep_count * rows, depth), F32),
+            pltpu.VMEM(down_weight.shape, BF),
+            pltpu.SemaphoreType.DMA((local_count,)),
+        ],
+        compiler_params=pltpu.CompilerParams(vmem_limit_bytes=24 << 20),
+        cost_estimate=pl.CostEstimate(
+            flops=ep_count * rows * weight_bytes, bytes_accessed=weight_bytes, transcendentals=0
+        ),
+        name="experts",
+    )(
+        in_vmem(gathered),
+        in_vmem(gain),
+        in_vmem(gate_weight),
+        in_vmem(up_weight),
+        in_hbm(down_weight),
+    )
 
 
 def on_device(
@@ -274,17 +333,16 @@
     width = depth // head_count
     top = expert_ids.shape[1]
     gain = norm_gain.reshape(1, depth)
-    attended, coefficient, hidden_near, gain_near, out_weight_near = pl.pallas_call(
+    pieces = out_weight.shape[0] * (out_weight.shape[1] // math.gcd(out_weight.shape[1], 2 * HD))
+    partial_value, coefficient, gain_near = pl.pallas_call(
         attend_kernel,
         out_shape=(
-            pltpu.VMEM((rows, out_weight.shape[0] * out_weight.shape[1]), BF),
+            pltpu.VMEM((rows, depth), BF),
             pltpu.VMEM((rows, 2 * experts), BF),
-            pltpu.VMEM(hidden.shape, BF),
             pltpu.VMEM(gain.shape, F32),
-            pltpu.VMEM(out_weight.shape, BF),
         ),
         in_specs=[HBM] * 11,
-        out_specs=(VMEM,) * 5,
+        out_specs=(VMEM,) * 3,
         scratch_shapes=[
             pltpu.SMEM(lengths.shape, jnp.int32),
             pltpu.VMEM(query.shape, BF),
@@ -294,9 +352,12 @@
             pltpu.VMEM(cache_values.shape, BF),
             pltpu.VMEM((rows, top), jnp.int32),
             pltpu.VMEM((rows, top), F32),
-            pltpu.SemaphoreType.DMA((11,)),
+            pltpu.VMEM(hidden.shape, BF),
+            pltpu.VMEM(out_weight.shape, BF),
+            pltpu.SemaphoreType.DMA((10,)),
+            pltpu.SemaphoreType.DMA((pieces,)),
         ],
-        compiler_params=pltpu.CompilerParams(vmem_limit_bytes=8 << 20),
+        compiler_params=pltpu.CompilerParams(vmem_limit_bytes=16 << 20),
         name="attend",
     )(
         in_hbm(lengths),
@@ -311,39 +372,25 @@
         in_hbm(gain),
         in_hbm(out_weight),
     )
-    partial_value = pl.pallas_call(
-        project_kernel,
-        out_shape=pltpu.VMEM((rows, depth), BF),
-        in_specs=[VMEM] * 3,
-        out_specs=VMEM,
-        compiler_params=pltpu.CompilerParams(vmem_limit_bytes=8 << 20),
-        cost_estimate=pl.CostEstimate(
-            flops=10**12, bytes_accessed=200 * 10**6, transcendentals=0
-        ),
-        name="project",
-    )(in_vmem(attended), in_vmem(out_weight_near), in_vmem(hidden_near))
-    stream = sum_heads(sum_over(partial_value, "side").astype(BF))
+    for k in partners(side_count):
+        other = swap(partial_value, "side", k)
+        partial_value = pl.pallas_call(
+            add_kernel,
+            out_shape=pltpu.VMEM((rows, depth), BF),
+            in_specs=[VMEM] * 2,
+            out_specs=VMEM,
+            compiler_params=pltpu.CompilerParams(vmem_limit_bytes=4 << 20),
+            cost_estimate=pl.CostEstimate(
+                flops=10**12, bytes_accessed=200 * 10**6, transcendentals=0
+            ),
+            name="side_sum",
+        )(in_vmem(partial_value), in_vmem(other))
+    stream = sum_heads(partial_value)
     after_attention = lax.dynamic_slice_in_dim(stream, head_index * width, width, 1)
     packed = jnp.concatenate([stream.astype(BF), coefficient], 1)
     gathered = gather_rows(packed)
-    weight_bytes = 2 * (gate_weight.size + up_weight.size + down_weight.size)
-    result = pl.pallas_call(
-        functools.partial(expert_kernel, width=width),
-        out_shape=jax.ShapeDtypeStruct((ep_count * head_count, rows, width), BF),
-        in_specs=[VMEM] * 5,
-        out_specs=VMEM,
-        scratch_shapes=[pltpu.VMEM((ep_count * rows, local_count * hidden_units), BF)],
-        compiler_params=pltpu.CompilerParams(vmem_limit_bytes=8 << 20),
-        cost_estimate=pl.CostEstimate(
-            flops=ep_count * rows * weight_bytes, bytes_accessed=weight_bytes, transcendentals=0
-        ),
-        name="experts",
-    )(
-        in_vmem(gathered),
-        in_vmem(gain_near),
-        in_vmem(gate_weight),
-        in_vmem(up_weight),
-        in_vmem(down_weight),
+    result = run_experts(
+        gathered, gain_near, gate_weight, up_weight, down_weight, head_count, ep_count
     )
     arrived = lax.all_to_all(result, ("ep", "head"), 0, 0, tiled=True)
     local_sum = jnp.sum(arrived.astype(F32), 0).astype(BF)

time: 38.1 us -> 41.3 us (1.084)
  Pallas kernels: 9.16 us -> 12.4 us
    pallas_call x3, Pallas kernels: 9.16 us -> 12.4 us  [the longest x1 9.38 us: run_experts(): pl.pallas_call(functools.partial(expert_kernel, width=width), out_shape=j...]
where the time goes in v4:
time: 41.3 us; the launch traced here: 41 us
  waiting for transfers between devices  13.4 us (32%)
  starting transfers between devices  13.3 us (32%)
  Pallas kernels  12.4 us (30%)
  between operations  0.7 us (2%)
  other arithmetic  0.67 us (2%)
  local copies, waits for them, and re-layouts  0.63 us (2%)
    pallas_call x1, Pallas kernels, run_experts(): pl.pallas_call(functools.partial(expert_kernel, width=width), out_shape=j...  9.38 us
    all_to_all x1, waiting for transfers between devices, on_device(): arrived = lax.all_to_all(result, ('ep', 'head'), 0, 0, tiled=True)  7.34 us
    all_to_all x1, starting transfers between devices, on_device(): arrived = lax.all_to_all(result, ('ep', 'head'), 0, 0, tiled=True)  6.54 us
    ppermute x3, starting transfers between devices, joint(): return lax.ppermute(x, axes, pairs)  5.85 us
    ppermute x3, waiting for transfers between devices, joint(): return lax.ppermute(x, axes, pairs)  4.61 us
    pallas_call x1, Pallas kernels, on_device(): pl.pallas_call(attend_kernel, out_shape=(pltpu.VMEM((rows, depth), BF), p...  2.97 us
    ppermute x3, waiting for transfers between devices, swap(): return lax.ppermute(x, axis, [(i, i ^ k) for i in range(count)])  1.41 us
    ppermute x3, starting transfers between devices, swap(): return lax.ppermute(x, axis, [(i, i ^ k) for i in range(count)])  0.93 us
  transfers between devices with their start and end apart: 7, of which 6 were waited for; matrix products, arithmetic and copies ran while one was open for 2% of the time, Pallas kernels for 0%

profile of v4, /device:TPU:0, one launch (start us, length us, event | category | flops | bytes accessed | tf_op | source)
XLA Modules:
  0.0 41.0 jit_solution(2311268960081357886)
XLA Ops:
  0.6 3.0 %attend.1 = (bf16[8,2048]{1,0:T(8,128)(2,1)S(1)}, bf16[8,128]{1,0:T(8,128)(2,1)S(1)}, f32[1,2048]{1,0:T(1,128)S(1)}) custom-call(s32[8]{0:T(128)} %lengths_hbm.1, bf16[8,2,512]{2,1,0:T(2,128)(2,1)} %query_hbm.1, bf16[8,256]{1,0:T(8,128)(2,1)} %new_key_hbm.1, bf16[8,256]{1,0:T(8,128)(2,1)} %new_value_hbm.1, bf16[8,128,256]{2,1,0:T(8,128)(2,1)} %cache_keys_hbm.1, ...), custom_call_target="tpu_custom_call" | custom-call | tf_op jit(solution)/shard_map/attend/pallas_call | solution.py:337
  3.6 0.6 %collective-permute-start = (bf16[8,2048]{1,0:T(8,128)(2,1)S(1)}, bf16[8,2048]{1,0:T(8,128)(2,1)S(1)}, u32[]{:S(2)}, u32[]{:S(2)}) collective-permute-start(bf16[8,2048]{1,0:T(8,128)(2,1)S(1)} %get-tuple-element.5.mine), channel_id=1, source_target_pairs={{0,2},{2,0},{1,3},{3,1},{4,6},{6,4},{5,7},{7,5},{8,10},{10,8},{9,1... | collective-permute-start | bytes 98312 | tf_op jit(solution)/shard_map/ppermute | solution.py:37
  4.2 0.9 %collective-permute-done.other = bf16[8,2048]{1,0:T(8,128)(2,1)S(1)} collective-permute-done((bf16[8,2048]{1,0:T(8,128)(2,1)S(1)}, bf16[8,2048]{1,0:T(8,128)(2,1)S(1)}, u32[]{:S(2)}, u32[]{:S(2)}) %collective-permute-start) | collective-permute-done | bytes 32800 | tf_op jit(solution)/shard_map/ppermute | solution.py:37
  5.0 0.0 copy-start
  5.0 0.0 copy-start.1
  5.0 2.7 %collective-permute-start.1 = (bf16[8,2048]{1,0:T(8,128)(2,1)S(1)}, bf16[8,2048]{1,0:T(8,128)(2,1)S(1)}, u32[]{:S(2)}, u32[]{:S(2)}) collective-permute-start(bf16[8,2048]{1,0:T(8,128)(2,1)S(1)} %side_sum.1), channel_id=1, source_target_pairs={{0,3},{1,2},{2,1},{3,0},{4,7},{5,6},{6,5},{7,4},{8,11},{9,10},{10,... | collective-permute-start | bytes 98312 | tf_op jit(solution)/shard_map/ppermute | solution.py:52
  7.7 1.6 %collective-permute-done.1 = bf16[8,2048]{1,0:T(8,128)(2,1)S(1)} collective-permute-done((bf16[8,2048]{1,0:T(8,128)(2,1)S(1)}, bf16[8,2048]{1,0:T(8,128)(2,1)S(1)}, u32[]{:S(2)}, u32[]{:S(2)}) %collective-permute-start.1) | collective-permute-done | bytes 32800 | tf_op jit(solution)/shard_map/ppermute | solution.py:52
  9.3 3.1 %collective-permute-start.3 = (bf16[8,2176]{1,0:T(8,128)(2,1)S(1)}, bf16[8,2176]{1,0:T(8,128)(2,1)S(1)}, u32[]{:S(2)}, u32[]{:S(2)}) collective-permute-start(bf16[8,2176]{1,0:T(8,128)(2,1)S(1)} %pad_maximum_fusion.1), channel_id=1, source_target_pairs={{0,8},{2,14},{4,12},{6,10},{8,0},{10,6},{12,4},{14,2},{1,9},{3,15}... | collective-permute-start | bytes 104456 | tf_op jit(solution)/shard_map/ppermute | solution.py:52
  12.5 0.1 collective-permute-start.2
  12.5 1.9 %collective-permute-done.3 = bf16[8,2176]{1,0:T(8,128)(2,1)S(1)} collective-permute-done((bf16[8,2176]{1,0:T(8,128)(2,1)S(1)}, bf16[8,2176]{1,0:T(8,128)(2,1)S(1)}, u32[]{:S(2)}, u32[]{:S(2)}) %collective-permute-start.3) | collective-permute-done | bytes 34848 | tf_op jit(solution)/shard_map/ppermute | solution.py:52
  14.4 0.3 collective-permute-start.4
  14.7 1.1 %collective-permute-done.2 = bf16[8,2176]{1,0:T(8,128)(2,1)S(1)} collective-permute-done((bf16[8,2176]{1,0:T(8,128)(2,1)S(1)}, bf16[8,2176]{1,0:T(8,128)(2,1)S(1)}, u32[]{:S(2)}, u32[]{:S(2)}) %collective-permute-start.2) | collective-permute-done | bytes 34848 | tf_op jit(solution)/shard_map/ppermute | solution.py:52
  15.8 0.0 collective-permute-done.4
  15.8 0.0 copy-done
  15.9 0.0 copy-done.1
  15.9 9.4 %experts.1 = bf16[8,8,1024]{2,1,0:T(8,128)(2,1)} custom-call(bf16[32,2176]{1,0:T(8,128)(2,1)S(1)} %pad_maximum_fusion.gathered, f32[1,2048]{1,0:T(1,128)S(1)} %get-tuple-element.7.norm_gain, bf16[8,2048,384]{2,1,0:T(8,128)(2,1)S(1)} %copy-done, bf16[8,2048,384]{2,1,0:T(8,128)(2,1)S(1)} %copy-done.1, bf16[8,384,2048]{2,1,0:T(8,128)(2,1)} %down_weight_hbm.1), custom_call_target="tpu_custom_call" | custom-call | flops 1207959552 | bytes 37748736 | tf_op jit(solution)/shard_map/experts/pallas_call | solution.py:285
  25.3 6.5 %all-to-all-start = ((bf16[8,8,1024]{2,1,0:T(8,128)(2,1)}), bf16[8,8,1024]{2,1,0:T(8,128)(2,1)S(1)}, u32[]{:S(2)}, u32[]{:S(2)}) async-start(bf16[8,8,1024]{2,1,0:T(8,128)(2,1)} %experts.1), calls=%async_computation | async-start | bytes 262144 | tf_op jit(solution)/shard_map/all_to_all | solution.py:395
  31.8 7.3 %all-to-all-done = bf16[8,8,1024]{2,1,0:T(8,128)(2,1)S(1)} async-done(((bf16[8,8,1024]{2,1,0:T(8,128)(2,1)}), bf16[8,8,1024]{2,1,0:T(8,128)(2,1)S(1)}, u32[]{:S(2)}, u32[]{:S(2)}) %all-to-all-start) | async-done | bytes 131104 | tf_op jit(solution)/shard_map/all_to_all | solution.py:395
  39.2 0.1 collective-permute-start.5
  39.2 0.6 %constant_dynamic-slice_fusion = f32[8,1024]{1,0:T(8,128)} fusion(f32[8,2048]{1,0:T(8,128)S(1)} %get-tuple-element.9, s32[]{:T(128)S(6)} %select_n.3), kind=kLoop, calls=%fused_computation.4 | loop fusion | bytes 65540 | tf_op jit(solution)/shard_map/dynamic_slice | solution.py:389
  39.9 0.5 %collective-permute-done.5 = bf16[8,1024]{1,0:T(8,128)(2,1)S(1)} collective-permute-done((bf16[8,1024]{1,0:T(8,128)(2,1)S(1)}, bf16[8,1024]{1,0:T(8,128)(2,1)S(1)}, u32[]{:S(2)}, u32[]{:S(2)}) %collective-permute-start.5) | collective-permute-done | bytes 16416 | tf_op jit(solution)/shard_map/ppermute | solution.py:37
  40.4 0.6 %add_convert_fusion = bf16[8,1024]{1,0:T(8,128)(2,1)} fusion(bf16[8,1024]{1,0:T(8,128)(2,1)S(1)} %collective-permute-done.5, bf16[8,1024]{1,0:T(8,128)(2,1)S(1)} %reduce_sum.12), kind=kLoop, calls=%fused_computation.3 | loop fusion | flops 32768 | bytes 49152 | tf_op jit(solution)/shard_map/convert_element_type | solution.py:397
  (5 shorter events, 0.1 us)
Async XLA Ops:
  3.6 1.4 %collective-permute-start = (bf16[8,2048]{1,0:T(8,128)(2,1)S(1)}, bf16[8,2048]{1,0:T(8,128)(2,1)S(1)}, u32[]{:S(2)}, u32[]{:S(2)}) collective-permute-start(bf16[8,2048]{1,0:T(8,128)(2,1)S(1)} %get-tuple-element.5.mine), channel_id=1, source_target_pairs={{0,2},{2,0},{1,3},{3,1},{4,6},{6,4},{5,7},{7,5},{8,10},{10,8},{9,1... | collective-permute-start | bytes 98312 | tf_op jit(solution)/shard_map/ppermute | solution.py:37
  5.0 10.8 %copy-start = (bf16[8,2048,384]{2,1,0:T(8,128)(2,1)S(1)}, bf16[8,2048,384]{2,1,0:T(8,128)(2,1)}, u32[]{:S(2)}) copy-start(bf16[8,2048,384]{2,1,0:T(8,128)(2,1)} %gate_weight.1) | copy-start | bytes 37748740
  5.0 10.8 %copy-start.1 = (bf16[8,2048,384]{2,1,0:T(8,128)(2,1)S(1)}, bf16[8,2048,384]{2,1,0:T(8,128)(2,1)}, u32[]{:S(2)}) copy-start(bf16[8,2048,384]{2,1,0:T(8,128)(2,1)} %up_weight.1) | copy-start | bytes 37748740
  5.0 4.3 %collective-permute-start.1 = (bf16[8,2048]{1,0:T(8,128)(2,1)S(1)}, bf16[8,2048]{1,0:T(8,128)(2,1)S(1)}, u32[]{:S(2)}, u32[]{:S(2)}) collective-permute-start(bf16[8,2048]{1,0:T(8,128)(2,1)S(1)} %side_sum.1), channel_id=1, source_target_pairs={{0,3},{1,2},{2,1},{3,0},{4,7},{5,6},{6,5},{7,4},{8,11},{9,10},{10,... | collective-permute-start | bytes 98312 | tf_op jit(solution)/shard_map/ppermute | solution.py:52
  9.3 5.1 %collective-permute-start.3 = (bf16[8,2176]{1,0:T(8,128)(2,1)S(1)}, bf16[8,2176]{1,0:T(8,128)(2,1)S(1)}, u32[]{:S(2)}, u32[]{:S(2)}) collective-permute-start(bf16[8,2176]{1,0:T(8,128)(2,1)S(1)} %pad_maximum_fusion.1), channel_id=1, source_target_pairs={{0,8},{2,14},{4,12},{6,10},{8,0},{10,6},{12,4},{14,2},{1,9},{3,15}... | collective-permute-start | bytes 104456 | tf_op jit(solution)/shard_map/ppermute | solution.py:52
  12.5 3.4 %collective-permute-start.2 = (bf16[8,2176]{1,0:T(8,128)(2,1)S(1)}, bf16[8,2176]{1,0:T(8,128)(2,1)S(1)}, u32[]{:S(2)}, u32[]{:S(2)}) collective-permute-start(bf16[8,2176]{1,0:T(8,128)(2,1)S(1)} %pad_maximum_fusion.1), channel_id=1, source_target_pairs={{0,6},{2,4},{4,2},{6,0},{8,14},{10,12},{12,10},{14,8},{1,7},{3,5},... | collective-permute-start | bytes 104456 | tf_op jit(solution)/shard_map/ppermute | solution.py:52
  14.4 1.4 %collective-permute-start.4 = (bf16[8,2176]{1,0:T(8,128)(2,1)S(1)}, bf16[8,2176]{1,0:T(8,128)(2,1)S(1)}, u32[]{:S(2)}, u32[]{:S(2)}) collective-permute-start(bf16[8,2176]{1,0:T(8,128)(2,1)S(1)} %collective-permute-done.3), channel_id=1, source_target_pairs={{0,2},{2,0},{1,3},{3,1},{4,6},{6,4},{5,7},{7,5},{8,10},{10,8},{9,1... | collective-permute-start | bytes 104456 | tf_op jit(solution)/shard_map/ppermute | solution.py:37
  25.3 13.9 %all-to-all-start = ((bf16[8,8,1024]{2,1,0:T(8,128)(2,1)}), bf16[8,8,1024]{2,1,0:T(8,128)(2,1)S(1)}, u32[]{:S(2)}, u32[]{:S(2)}) async-start(bf16[8,8,1024]{2,1,0:T(8,128)(2,1)} %experts.1), calls=%async_computation | async-start | bytes 262144 | tf_op jit(solution)/shard_map/all_to_all | solution.py:395
  39.2 1.2 %collective-permute-start.5 = (bf16[8,1024]{1,0:T(8,128)(2,1)S(1)}, bf16[8,1024]{1,0:T(8,128)(2,1)S(1)}, u32[]{:S(2)}, u32[]{:S(2)}) collective-permute-start(bf16[8,1024]{1,0:T(8,128)(2,1)S(1)} %reduce_sum.12), channel_id=1, source_target_pairs={{0,2},{2,0},{1,3},{3,1},{4,6},{6,4},{5,7},{7,5},{8,10},{10,8},{9,1... | collective-permute-start | bytes 49160 | tf_op jit(solution)/shard_map/ppermute | solution.py:37

commit v5 on v4

--- a/solution.py
+++ b/solution.py
@@ -227,17 +227,11 @@
 
 
 def expert_kernel(
-    gathered, norm_gain, gate_weight, up_weight, down_weight_hbm, out, inner, total, down_weight, arrivals, width
+    gathered, norm_gain, gate_weight, up_weight, down_weight, out, inner, width
 ):
     count, depth, hidden_units = gate_weight.shape
     experts = (gathered.shape[1] - depth) // 2
     rows = gathered.shape[0]
-    copies = [
-        pltpu.make_async_copy(down_weight_hbm.at[e], down_weight.at[e], arrivals.at[e])
-        for e in range(count)
-    ]
-    for copy in copies:
-        copy.start()
     stream = gathered[:, :depth].astype(F32)
     norm = lax.rsqrt(jnp.mean(stream * stream, -1, keepdims=True) + 1e-06)
     normed = (stream * norm * norm_gain[...]).astype(BF)
@@ -253,20 +247,11 @@
         share = jnp.sum(jnp.where(lane == first + e, coefficient, F32(0.0)), 1, keepdims=True)
         value = gate / (1.0 + jnp.exp(-gate)) * upper * share
         inner[:, e * hidden_units : (e + 1) * hidden_units] = value.astype(BF)
-    group = 2 if count % 2 == 0 else 1
-    for low in range(0, count, group):
-        for copy in copies[low : low + group]:
-            copy.wait()
-        part = jnp.dot(
-            inner[:, low * hidden_units : (low + group) * hidden_units],
-            down_weight[low : low + group].reshape(group * hidden_units, depth),
-            preferred_element_type=F32,
-        )
-        if low == 0:
-            total[...] = part
-        else:
-            total[...] += part
-    result = total[...].astype(BF)
+    result = jnp.dot(
+        inner[...],
+        down_weight[...].reshape(count * hidden_units, depth),
+        preferred_element_type=F32,
+    ).astype(BF)
     blocks, block_rows, _ = out.shape
     heads = depth // width
     for j in range(blocks // heads):
@@ -285,15 +270,12 @@
     return pl.pallas_call(
         functools.partial(expert_kernel, width=width),
         out_shape=jax.ShapeDtypeStruct((ep_count * head_count, rows, width), BF),
-        in_specs=[VMEM] * 4 + [HBM],
+        in_specs=[VMEM] * 5,
         out_specs=VMEM,
         scratch_shapes=[
             pltpu.VMEM((ep_count * rows, local_count * hidden_units), BF),
-            pltpu.VMEM((ep_count * rows, depth), F32),
-            pltpu.VMEM(down_weight.shape, BF),
-            pltpu.SemaphoreType.DMA((local_count,)),
         ],
-        compiler_params=pltpu.CompilerParams(vmem_limit_bytes=24 << 20),
+        compiler_params=pltpu.CompilerParams(vmem_limit_bytes=8 << 20),
         cost_estimate=pl.CostEstimate(
             flops=ep_count * rows * weight_bytes, bytes_accessed=weight_bytes, transcendentals=0
         ),
@@ -303,7 +285,7 @@
         in_vmem(gain),
         in_vmem(gate_weight),
         in_vmem(up_weight),
-        in_hbm(down_weight),
+        in_vmem(down_weight),
     )
 
 
@@ -358,6 +340,9 @@
             pltpu.SemaphoreType.DMA((pieces,)),
         ],
         compiler_params=pltpu.CompilerParams(vmem_limit_bytes=16 << 20),
+        cost_estimate=pl.CostEstimate(
+            flops=10**12, bytes_accessed=200 * 10**6, transcendentals=0
+        ),
         name="attend",
     )(
         in_hbm(lengths),
@@ -380,9 +365,6 @@
             in_specs=[VMEM] * 2,
             out_specs=VMEM,
             compiler_params=pltpu.CompilerParams(vmem_limit_bytes=4 << 20),
-            cost_estimate=pl.CostEstimate(
-                flops=10**12, bytes_accessed=200 * 10**6, transcendentals=0
-            ),
             name="side_sum",
         )(in_vmem(partial_value), in_vmem(other))
     stream = sum_heads(partial_value)

time: 41.3 us -> 37.9 us (0.918)
  Pallas kernels: 12.4 us -> 8.96 us
    pallas_call x1, Pallas kernels: 9.38 us -> 5.86 us  [run_experts(): pl.pallas_call(functools.partial(expert_kernel, width=width), out_shape=j...]
where the time goes in v5:
time: 37.9 us; the launch traced here: 37.6 us
  waiting for transfers between devices  13.4 us (35%)
  starting transfers between devices  13.3 us (35%)
  Pallas kernels  8.96 us (24%)
  between operations  0.72 us (2%)
  other arithmetic  0.67 us (2%)
  local copies, waits for them, and re-layouts  0.64 us (2%)
    all_to_all x1, waiting for transfers between devices, on_device(): arrived = lax.all_to_all(result, ('ep', 'head'), 0, 0, tiled=True)  7.34 us
    all_to_all x1, starting transfers between devices, on_device(): arrived = lax.all_to_all(result, ('ep', 'head'), 0, 0, tiled=True)  6.53 us
    pallas_call x1, Pallas kernels, run_experts(): pl.pallas_call(functools.partial(expert_kernel, width=width), out_shape=j...  5.86 us
    ppermute x3, starting transfers between devices, joint(): return lax.ppermute(x, axes, pairs)  5.85 us
    ppermute x3, waiting for transfers between devices, joint(): return lax.ppermute(x, axes, pairs)  4.61 us
    pallas_call x1, Pallas kernels, on_device(): pl.pallas_call(attend_kernel, out_shape=(pltpu.VMEM((rows, depth), BF), p...  3.08 us
    ppermute x3, waiting for transfers between devices, swap(): return lax.ppermute(x, axis, [(i, i ^ k) for i in range(count)])  1.41 us
    ppermute x3, starting transfers between devices, swap(): return lax.ppermute(x, axis, [(i, i ^ k) for i in range(count)])  0.93 us
  transfers between devices with their start and end apart: 7, of which 6 were waited for; matrix products, arithmetic and copies ran while one was open for 2% of the time, Pallas kernels for 0%

profile of v5, /device:TPU:0, one launch (start us, length us, event | category | flops | bytes accessed | tf_op | source)
XLA Modules:
  0.0 37.6 jit_solution(8451478414208438552)
XLA Ops:
  0.6 0.0 copy-start
  0.6 0.0 copy-start.1
  0.7 0.0 copy-start.2
  0.7 3.1 %attend.1 = (bf16[8,2048]{1,0:T(8,128)(2,1)S(1)}, bf16[8,128]{1,0:T(8,128)(2,1)S(1)}, f32[1,2048]{1,0:T(1,128)S(1)}) custom-call(s32[8]{0:T(128)} %lengths_hbm.1, bf16[8,2,512]{2,1,0:T(2,128)(2,1)} %query_hbm.1, bf16[8,256]{1,0:T(8,128)(2,1)} %new_key_hbm.1, bf16[8,256]{1,0:T(8,128)(2,1)} %new_value_hbm.1, bf16[8,128,256]{2,1,0:T(8,128)(2,1)} %cache_keys_hbm.1, ...), custom_call_target="tpu_custom_call" | custom-call | flops 999999995904 | bytes 200000000 | tf_op jit(solution)/shard_map/attend/pallas_call | solution.py:319
  3.8 0.6 %collective-permute-start = (bf16[8,2048]{1,0:T(8,128)(2,1)S(1)}, bf16[8,2048]{1,0:T(8,128)(2,1)S(1)}, u32[]{:S(2)}, u32[]{:S(2)}) collective-permute-start(bf16[8,2048]{1,0:T(8,128)(2,1)S(1)} %get-tuple-element.5.mine), channel_id=1, source_target_pairs={{0,2},{2,0},{1,3},{3,1},{4,6},{6,4},{5,7},{7,5},{8,10},{10,8},{9,1... | collective-permute-start | bytes 98312 | tf_op jit(solution)/shard_map/ppermute | solution.py:37
  4.3 0.9 %collective-permute-done.other = bf16[8,2048]{1,0:T(8,128)(2,1)S(1)} collective-permute-done((bf16[8,2048]{1,0:T(8,128)(2,1)S(1)}, bf16[8,2048]{1,0:T(8,128)(2,1)S(1)}, u32[]{:S(2)}, u32[]{:S(2)}) %collective-permute-start) | collective-permute-done | bytes 32800 | tf_op jit(solution)/shard_map/ppermute | solution.py:37
  5.2 2.7 %collective-permute-start.1 = (bf16[8,2048]{1,0:T(8,128)(2,1)S(1)}, bf16[8,2048]{1,0:T(8,128)(2,1)S(1)}, u32[]{:S(2)}, u32[]{:S(2)}) collective-permute-start(bf16[8,2048]{1,0:T(8,128)(2,1)S(1)} %side_sum.1), channel_id=1, source_target_pairs={{0,3},{1,2},{2,1},{3,0},{4,7},{5,6},{6,5},{7,4},{8,11},{9,10},{10,... | collective-permute-start | bytes 98312 | tf_op jit(solution)/shard_map/ppermute | solution.py:52
  7.8 1.6 %collective-permute-done.1 = bf16[8,2048]{1,0:T(8,128)(2,1)S(1)} collective-permute-done((bf16[8,2048]{1,0:T(8,128)(2,1)S(1)}, bf16[8,2048]{1,0:T(8,128)(2,1)S(1)}, u32[]{:S(2)}, u32[]{:S(2)}) %collective-permute-start.1) | collective-permute-done | bytes 32800 | tf_op jit(solution)/shard_map/ppermute | solution.py:52
  9.5 3.1 %collective-permute-start.3 = (bf16[8,2176]{1,0:T(8,128)(2,1)S(1)}, bf16[8,2176]{1,0:T(8,128)(2,1)S(1)}, u32[]{:S(2)}, u32[]{:S(2)}) collective-permute-start(bf16[8,2176]{1,0:T(8,128)(2,1)S(1)} %pad_maximum_fusion.1), channel_id=1, source_target_pairs={{0,8},{2,14},{4,12},{6,10},{8,0},{10,6},{12,4},{14,2},{1,9},{3,15}... | collective-permute-start | bytes 104456 | tf_op jit(solution)/shard_map/ppermute | solution.py:52
  12.6 0.1 collective-permute-start.2
  12.7 1.9 %collective-permute-done.3 = bf16[8,2176]{1,0:T(8,128)(2,1)S(1)} collective-permute-done((bf16[8,2176]{1,0:T(8,128)(2,1)S(1)}, bf16[8,2176]{1,0:T(8,128)(2,1)S(1)}, u32[]{:S(2)}, u32[]{:S(2)}) %collective-permute-start.3) | collective-permute-done | bytes 34848 | tf_op jit(solution)/shard_map/ppermute | solution.py:52
  14.5 0.3 collective-permute-start.4
  14.8 1.1 %collective-permute-done.2 = bf16[8,2176]{1,0:T(8,128)(2,1)S(1)} collective-permute-done((bf16[8,2176]{1,0:T(8,128)(2,1)S(1)}, bf16[8,2176]{1,0:T(8,128)(2,1)S(1)}, u32[]{:S(2)}, u32[]{:S(2)}) %collective-permute-start.2) | collective-permute-done | bytes 34848 | tf_op jit(solution)/shard_map/ppermute | solution.py:52
  16.0 0.0 collective-permute-done.4
  16.0 0.0 copy-done
  16.0 0.0 copy-done.1
  16.0 0.0 copy-done.2
  16.0 5.9 %experts.1 = bf16[8,8,1024]{2,1,0:T(8,128)(2,1)} custom-call(bf16[32,2176]{1,0:T(8,128)(2,1)S(1)} %pad_maximum_fusion.gathered, f32[1,2048]{1,0:T(1,128)S(1)} %get-tuple-element.7.norm_gain, bf16[8,2048,384]{2,1,0:T(8,128)(2,1)S(1)} %copy-done, bf16[8,2048,384]{2,1,0:T(8,128)(2,1)S(1)} %copy-done.1, bf16[8,384,2048]{2,1,0:T(8,128)(2,1)S(1)} %copy-done.2), custom_call_target="tpu_custom_call" | custom-call | flops 1207959552 | bytes 37748736 | tf_op jit(solution)/shard_map/experts/pallas_call | solution.py:270
  21.9 6.5 %all-to-all-start = ((bf16[8,8,1024]{2,1,0:T(8,128)(2,1)}), bf16[8,8,1024]{2,1,0:T(8,128)(2,1)S(1)}, u32[]{:S(2)}, u32[]{:S(2)}) async-start(bf16[8,8,1024]{2,1,0:T(8,128)(2,1)} %experts.1), calls=%async_computation | async-start | bytes 262144 | tf_op jit(solution)/shard_map/all_to_all | solution.py:377
  28.4 7.3 %all-to-all-done = bf16[8,8,1024]{2,1,0:T(8,128)(2,1)S(1)} async-done(((bf16[8,8,1024]{2,1,0:T(8,128)(2,1)}), bf16[8,8,1024]{2,1,0:T(8,128)(2,1)S(1)}, u32[]{:S(2)}, u32[]{:S(2)}) %all-to-all-start) | async-done | bytes 131104 | tf_op jit(solution)/shard_map/all_to_all | solution.py:377
  35.8 0.1 collective-permute-start.5
  35.9 0.6 %constant_dynamic-slice_fusion = f32[8,1024]{1,0:T(8,128)} fusion(f32[8,2048]{1,0:T(8,128)S(1)} %get-tuple-element.9, s32[]{:T(128)S(6)} %select_n.3), kind=kLoop, calls=%fused_computation.4 | loop fusion | bytes 65540 | tf_op jit(solution)/shard_map/dynamic_slice | solution.py:371
  36.5 0.5 %collective-permute-done.5 = bf16[8,1024]{1,0:T(8,128)(2,1)S(1)} collective-permute-done((bf16[8,1024]{1,0:T(8,128)(2,1)S(1)}, bf16[8,1024]{1,0:T(8,128)(2,1)S(1)}, u32[]{:S(2)}, u32[]{:S(2)}) %collective-permute-start.5) | collective-permute-done | bytes 16416 | tf_op jit(solution)/shard_map/ppermute | solution.py:37
  37.0 0.6 %add_convert_fusion = bf16[8,1024]{1,0:T(8,128)(2,1)} fusion(bf16[8,1024]{1,0:T(8,128)(2,1)S(1)} %collective-permute-done.5, bf16[8,1024]{1,0:T(8,128)(2,1)S(1)} %reduce_sum.12), kind=kLoop, calls=%fused_computation.3 | loop fusion | flops 32768 | bytes 49152 | tf_op jit(solution)/shard_map/convert_element_type | solution.py:379
  (5 shorter events, 0.1 us)
Async XLA Ops:
  0.6 15.4 %copy-start = (bf16[8,2048,384]{2,1,0:T(8,128)(2,1)S(1)}, bf16[8,2048,384]{2,1,0:T(8,128)(2,1)}, u32[]{:S(2)}) copy-start(bf16[8,2048,384]{2,1,0:T(8,128)(2,1)} %gate_weight.1) | copy-start | bytes 37748740
  0.6 15.4 %copy-start.1 = (bf16[8,2048,384]{2,1,0:T(8,128)(2,1)S(1)}, bf16[8,2048,384]{2,1,0:T(8,128)(2,1)}, u32[]{:S(2)}) copy-start(bf16[8,2048,384]{2,1,0:T(8,128)(2,1)} %up_weight.1) | copy-start | bytes 37748740
  0.7 15.4 %copy-start.2 = (bf16[8,384,2048]{2,1,0:T(8,128)(2,1)S(1)}, bf16[8,384,2048]{2,1,0:T(8,128)(2,1)}, u32[]{:S(2)}) copy-start(bf16[8,384,2048]{2,1,0:T(8,128)(2,1)} %down_weight.1) | copy-start | bytes 37748740
  3.8 1.4 %collective-permute-start = (bf16[8,2048]{1,0:T(8,128)(2,1)S(1)}, bf16[8,2048]{1,0:T(8,128)(2,1)S(1)}, u32[]{:S(2)}, u32[]{:S(2)}) collective-permute-start(bf16[8,2048]{1,0:T(8,128)(2,1)S(1)} %get-tuple-element.5.mine), channel_id=1, source_target_pairs={{0,2},{2,0},{1,3},{3,1},{4,6},{6,4},{5,7},{7,5},{8,10},{10,8},{9,1... | collective-permute-start | bytes 98312 | tf_op jit(solution)/shard_map/ppermute | solution.py:37
  5.2 4.3 %collective-permute-start.1 = (bf16[8,2048]{1,0:T(8,128)(2,1)S(1)}, bf16[8,2048]{1,0:T(8,128)(2,1)S(1)}, u32[]{:S(2)}, u32[]{:S(2)}) collective-permute-start(bf16[8,2048]{1,0:T(8,128)(2,1)S(1)} %side_sum.1), channel_id=1, source_target_pairs={{0,3},{1,2},{2,1},{3,0},{4,7},{5,6},{6,5},{7,4},{8,11},{9,10},{10,... | collective-permute-start | bytes 98312 | tf_op jit(solution)/shard_map/ppermute | solution.py:52
  9.5 5.1 %collective-permute-start.3 = (bf16[8,2176]{1,0:T(8,128)(2,1)S(1)}, bf16[8,2176]{1,0:T(8,128)(2,1)S(1)}, u32[]{:S(2)}, u32[]{:S(2)}) collective-permute-start(bf16[8,2176]{1,0:T(8,128)(2,1)S(1)} %pad_maximum_fusion.1), channel_id=1, source_target_pairs={{0,8},{2,14},{4,12},{6,10},{8,0},{10,6},{12,4},{14,2},{1,9},{3,15}... | collective-permute-start | bytes 104456 | tf_op jit(solution)/shard_map/ppermute | solution.py:52
  12.6 3.4 %collective-permute-start.2 = (bf16[8,2176]{1,0:T(8,128)(2,1)S(1)}, bf16[8,2176]{1,0:T(8,128)(2,1)S(1)}, u32[]{:S(2)}, u32[]{:S(2)}) collective-permute-start(bf16[8,2176]{1,0:T(8,128)(2,1)S(1)} %pad_maximum_fusion.1), channel_id=1, source_target_pairs={{0,6},{2,4},{4,2},{6,0},{8,14},{10,12},{12,10},{14,8},{1,7},{3,5},... | collective-permute-start | bytes 104456 | tf_op jit(solution)/shard_map/ppermute | solution.py:52
  14.5 1.4 %collective-permute-start.4 = (bf16[8,2176]{1,0:T(8,128)(2,1)S(1)}, bf16[8,2176]{1,0:T(8,128)(2,1)S(1)}, u32[]{:S(2)}, u32[]{:S(2)}) collective-permute-start(bf16[8,2176]{1,0:T(8,128)(2,1)S(1)} %collective-permute-done.3), channel_id=1, source_target_pairs={{0,2},{2,0},{1,3},{3,1},{4,6},{6,4},{5,7},{7,5},{8,10},{10,8},{9,1... | collective-permute-start | bytes 104456 | tf_op jit(solution)/shard_map/ppermute | solution.py:37
  21.9 13.9 %all-to-all-start = ((bf16[8,8,1024]{2,1,0:T(8,128)(2,1)}), bf16[8,8,1024]{2,1,0:T(8,128)(2,1)S(1)}, u32[]{:S(2)}, u32[]{:S(2)}) async-start(bf16[8,8,1024]{2,1,0:T(8,128)(2,1)} %experts.1), calls=%async_computation | async-start | bytes 262144 | tf_op jit(solution)/shard_map/all_to_all | solution.py:377
  35.8 1.2 %collective-permute-start.5 = (bf16[8,1024]{1,0:T(8,128)(2,1)S(1)}, bf16[8,1024]{1,0:T(8,128)(2,1)S(1)}, u32[]{:S(2)}, u32[]{:S(2)}) collective-permute-start(bf16[8,1024]{1,0:T(8,128)(2,1)S(1)} %reduce_sum.12), channel_id=1, source_target_pairs={{0,2},{2,0},{1,3},{3,1},{4,6},{6,4},{5,7},{7,5},{8,10},{10,8},{9,1... | collective-permute-start | bytes 49160 | tf_op jit(solution)/shard_map/ppermute | solution.py:37

commit v6 on v5

--- a/solution.py
+++ b/solution.py
@@ -226,6 +226,15 @@
     out[...] = (mine[...].astype(F32) + other[...].astype(F32)).astype(BF)
 
 
+def take_kernel(stream, out):
+    width = out.shape[1]
+    me = lax.axis_index("head")
+    taken = stream[:, :width]
+    for h in range(1, stream.shape[1] // width):
+        taken = jnp.where(me == h, stream[:, h * width : (h + 1) * width], taken)
+    out[...] = taken
+
+
 def expert_kernel(
     gathered, norm_gain, gate_weight, up_weight, down_weight, out, inner, width
 ):
@@ -308,7 +317,6 @@
     ep_count = lax.axis_size("ep")
     side_count = lax.axis_size("side")
     head_count = lax.axis_size("head")
-    head_index = lax.axis_index("head")
     rows, depth = hidden.shape
     local_count, _, hidden_units = gate_weight.shape
     experts = local_count * ep_count * side_count
@@ -368,7 +376,15 @@
             name="side_sum",
         )(in_vmem(partial_value), in_vmem(other))
     stream = sum_heads(partial_value)
-    after_attention = lax.dynamic_slice_in_dim(stream, head_index * width, width, 1)
+    after_attention = pl.pallas_call(
+        take_kernel,
+        out_shape=jax.ShapeDtypeStruct((rows, width), F32),
+        in_specs=[VMEM],
+        out_specs=VMEM,
+        compiler_params=pltpu.CompilerParams(vmem_limit_bytes=4 << 20),
+        cost_estimate=pl.CostEstimate(flops=10**4, bytes_accessed=10**5, transcendentals=0),
+        name="take",
+    )(in_vmem(stream))
     packed = jnp.concatenate([stream.astype(BF), coefficient], 1)
     gathered = gather_rows(packed)
     result = run_experts(

time: 37.9 us -> 37 us (0.976)
  blocking collectives: 0 us -> 13.7 us
  waiting for transfers between devices: 13.4 us -> 6.01 us
  starting transfers between devices: 13.3 us -> 6.78 us
  local copies, waits for them, and re-layouts: 0.64 us -> 0.01 us
    all_to_all x0 -> x1, blocking collectives: none -> 13.7 us  [on_device(): arrived = lax.all_to_all(result, ('ep', 'head'), 0, 0, tiled=True)]
    all_to_all x1 -> x0, waiting for transfers between devices: 7.34 us -> none  [on_device(): arrived = lax.all_to_all(result, ('ep', 'head'), 0, 0, tiled=True)]
    all_to_all x1 -> x0, starting transfers between devices: 6.53 us -> none  [on_device(): arrived = lax.all_to_all(result, ('ep', 'head'), 0, 0, tiled=True)]
    pallas_call x1, Pallas kernels: 5.86 us -> 5.2 us  [run_experts(): pl.pallas_call(functools.partial(expert_kernel, width=width), out_shape=j...]
    pallas_call x0 -> x1, Pallas kernels: none -> 0.63 us  [on_device(): pl.pallas_call(take_kernel, out_shape=jax.ShapeDtypeStruct((rows, width),...]
    dynamic_slice x1 -> x0, local copies, waits for them, and re-layouts: 0.63 us -> none  [on_device(): lax.dynamic_slice_in_dim(stream, head_index * width, width, 1)]
  transfers between devices with their start and end apart: 7 -> 6, of which waited for: 6 -> 5; matrix products, arithmetic and copies ran while one was open for 2% -> 0% of each run, Pallas kernels for 0% -> 2%
where the time goes in v6:
time: 37 us; the launch traced here: 36.8 us
  blocking collectives  13.7 us (37%)
  Pallas kernels  8.92 us (24%)
  starting transfers between devices  6.78 us (18%)
  waiting for transfers between devices  6.01 us (16%)
  between operations  0.73 us (2%)
  other arithmetic  0.67 us (2%)
    all_to_all x1, blocking collectives, on_device(): arrived = lax.all_to_all(result, ('ep', 'head'), 0, 0, tiled=True)  13.7 us
    ppermute x3, starting transfers between devices, joint(): return lax.ppermute(x, axes, pairs)  5.85 us
    pallas_call x1, Pallas kernels, run_experts(): pl.pallas_call(functools.partial(expert_kernel, width=width), out_shape=j...  5.2 us
    ppermute x3, waiting for transfers between devices, joint(): return lax.ppermute(x, axes, pairs)  4.61 us
    pallas_call x1, Pallas kernels, on_device(): pl.pallas_call(attend_kernel, out_shape=(pltpu.VMEM((rows, depth), BF), p...  3.08 us
    ppermute x3, waiting for transfers between devices, swap(): return lax.ppermute(x, axis, [(i, i ^ k) for i in range(count)])  1.41 us
    ppermute x3, starting transfers between devices, swap(): return lax.ppermute(x, axis, [(i, i ^ k) for i in range(count)])  0.93 us
  transfers between devices with their start and end apart: 6, of which 5 were waited for; matrix products, arithmetic and copies ran while one was open for 0% of the time, Pallas kernels for 2%

profile of v6, /device:TPU:0, one launch (start us, length us, event | category | flops | bytes accessed | tf_op | source)
XLA Modules:
  0.0 36.8 jit_solution(1398027737782890017)
XLA Ops:
  0.6 0.0 copy-start
  0.6 0.0 copy-start.1
  0.7 0.0 copy-start.2
  0.7 3.1 %attend.1 = (bf16[8,2048]{1,0:T(8,128)(2,1)S(1)}, bf16[8,128]{1,0:T(8,128)(2,1)S(1)}, f32[1,2048]{1,0:T(1,128)S(1)}) custom-call(s32[8]{0:T(128)} %lengths_hbm.1, bf16[8,2,512]{2,1,0:T(2,128)(2,1)} %query_hbm.1, bf16[8,256]{1,0:T(8,128)(2,1)} %new_key_hbm.1, bf16[8,256]{1,0:T(8,128)(2,1)} %new_value_hbm.1, bf16[8,128,256]{2,1,0:T(8,128)(2,1)} %cache_keys_hbm.1, ...), custom_call_target="tpu_custom_call" | custom-call | flops 999999995904 | bytes 200000000 | tf_op jit(solution)/shard_map/attend/pallas_call | solution.py:327
  3.8 0.6 %collective-permute-start = (bf16[8,2048]{1,0:T(8,128)(2,1)S(1)}, bf16[8,2048]{1,0:T(8,128)(2,1)S(1)}, u32[]{:S(2)}, u32[]{:S(2)}) collective-permute-start(bf16[8,2048]{1,0:T(8,128)(2,1)S(1)} %get-tuple-element.5.mine), channel_id=1, source_target_pairs={{0,2},{2,0},{1,3},{3,1},{4,6},{6,4},{5,7},{7,5},{8,10},{10,8},{9,1... | collective-permute-start | bytes 98312 | tf_op jit(solution)/shard_map/ppermute | solution.py:37
  4.3 0.9 %collective-permute-done.other = bf16[8,2048]{1,0:T(8,128)(2,1)S(1)} collective-permute-done((bf16[8,2048]{1,0:T(8,128)(2,1)S(1)}, bf16[8,2048]{1,0:T(8,128)(2,1)S(1)}, u32[]{:S(2)}, u32[]{:S(2)}) %collective-permute-start) | collective-permute-done | bytes 32800 | tf_op jit(solution)/shard_map/ppermute | solution.py:37
  5.2 2.7 %collective-permute-start.1 = (bf16[8,2048]{1,0:T(8,128)(2,1)S(1)}, bf16[8,2048]{1,0:T(8,128)(2,1)S(1)}, u32[]{:S(2)}, u32[]{:S(2)}) collective-permute-start(bf16[8,2048]{1,0:T(8,128)(2,1)S(1)} %side_sum.1), channel_id=1, source_target_pairs={{0,3},{1,2},{2,1},{3,0},{4,7},{5,6},{6,5},{7,4},{8,11},{9,10},{10,... | collective-permute-start | bytes 98312 | tf_op jit(solution)/shard_map/ppermute | solution.py:52
  7.8 1.6 %collective-permute-done.1 = bf16[8,2048]{1,0:T(8,128)(2,1)S(1)} collective-permute-done((bf16[8,2048]{1,0:T(8,128)(2,1)S(1)}, bf16[8,2048]{1,0:T(8,128)(2,1)S(1)}, u32[]{:S(2)}, u32[]{:S(2)}) %collective-permute-start.1) | collective-permute-done | bytes 32800 | tf_op jit(solution)/shard_map/ppermute | solution.py:52
  9.5 3.1 %collective-permute-start.3 = (bf16[8,2176]{1,0:T(8,128)(2,1)S(1)}, bf16[8,2176]{1,0:T(8,128)(2,1)S(1)}, u32[]{:S(2)}, u32[]{:S(2)}) collective-permute-start(bf16[8,2176]{1,0:T(8,128)(2,1)S(1)} %pad_maximum_fusion.1), channel_id=1, source_target_pairs={{0,8},{2,14},{4,12},{6,10},{8,0},{10,6},{12,4},{14,2},{1,9},{3,15}... | collective-permute-start | bytes 104456 | tf_op jit(solution)/shard_map/ppermute | solution.py:52
  12.6 0.1 collective-permute-start.2
  12.7 1.9 %collective-permute-done.3 = bf16[8,2176]{1,0:T(8,128)(2,1)S(1)} collective-permute-done((bf16[8,2176]{1,0:T(8,128)(2,1)S(1)}, bf16[8,2176]{1,0:T(8,128)(2,1)S(1)}, u32[]{:S(2)}, u32[]{:S(2)}) %collective-permute-start.3) | collective-permute-done | bytes 34848 | tf_op jit(solution)/shard_map/ppermute | solution.py:52
  14.5 0.3 collective-permute-start.4
  14.8 1.1 %collective-permute-done.2 = bf16[8,2176]{1,0:T(8,128)(2,1)S(1)} collective-permute-done((bf16[8,2176]{1,0:T(8,128)(2,1)S(1)}, bf16[8,2176]{1,0:T(8,128)(2,1)S(1)}, u32[]{:S(2)}, u32[]{:S(2)}) %collective-permute-start.2) | collective-permute-done | bytes 34848 | tf_op jit(solution)/shard_map/ppermute | solution.py:52
  16.0 0.0 collective-permute-done.4
  16.0 0.0 copy-done
  16.0 0.0 copy-done.1
  16.0 0.0 copy-done.2
  16.0 5.2 %experts.1 = bf16[8,8,1024]{2,1,0:T(8,128)(2,1)S(1)} custom-call(bf16[32,2176]{1,0:T(8,128)(2,1)S(1)} %pad_maximum_fusion.gathered, f32[1,2048]{1,0:T(1,128)S(1)} %get-tuple-element.7.norm_gain, bf16[8,2048,384]{2,1,0:T(8,128)(2,1)S(1)} %copy-done, bf16[8,2048,384]{2,1,0:T(8,128)(2,1)S(1)} %copy-done.1, bf16[8,384,2048]{2,1,0:T(8,128)(2,1)S(1)} %copy-done.2), custom_call_target="tpu_custom_call" | custom-call | flops 1207959552 | bytes 37748736 | tf_op jit(solution)/shard_map/experts/pallas_call | solution.py:279
  21.2 13.7 %all_to_all.5 = bf16[8,8,1024]{2,1,0:T(8,128)(2,1)S(1)} all-to-all(bf16[8,8,1024]{2,1,0:T(8,128)(2,1)S(1)} %experts.1), channel_id=1, replica_groups=mesh['groups'=2,'ep'=4,'side'=2,'head'=2] {'ep','head'}, dimensions={0} | all-to-all | bytes 262144 | tf_op jit(solution)/shard_map/all_to_all | solution.py:393
  34.9 0.1 collective-permute-start.5
  35.0 0.6 %take.1 = f32[8,1024]{1,0:T(8,128)} custom-call(f32[8,2048]{1,0:T(8,128)S(1)} %get-tuple-element.9.stream), custom_call_target="tpu_custom_call" | custom-call | flops 10000 | bytes 100000 | tf_op jit(solution)/shard_map/take/pallas_call | solution.py:379
  35.6 0.5 %collective-permute-done.5 = bf16[8,1024]{1,0:T(8,128)(2,1)S(1)} collective-permute-done((bf16[8,1024]{1,0:T(8,128)(2,1)S(1)}, bf16[8,1024]{1,0:T(8,128)(2,1)S(1)}, u32[]{:S(2)}, u32[]{:S(2)}) %collective-permute-start.5) | collective-permute-done | bytes 16416 | tf_op jit(solution)/shard_map/ppermute | solution.py:37
  36.2 0.6 %add_convert_fusion = bf16[8,1024]{1,0:T(8,128)(2,1)} fusion(bf16[8,1024]{1,0:T(8,128)(2,1)S(1)} %collective-permute-done.5, bf16[8,1024]{1,0:T(8,128)(2,1)S(1)} %reduce_sum.12), kind=kLoop, calls=%fused_computation.3 | loop fusion | flops 32768 | bytes 49152 | tf_op jit(solution)/shard_map/convert_element_type | solution.py:395
  (5 shorter events, 0.1 us)
Async XLA Ops:
  0.6 15.4 %copy-start = (bf16[8,2048,384]{2,1,0:T(8,128)(2,1)S(1)}, bf16[8,2048,384]{2,1,0:T(8,128)(2,1)}, u32[]{:S(2)}) copy-start(bf16[8,2048,384]{2,1,0:T(8,128)(2,1)} %gate_weight.1) | copy-start | bytes 37748740
  0.6 15.4 %copy-start.1 = (bf16[8,2048,384]{2,1,0:T(8,128)(2,1)S(1)}, bf16[8,2048,384]{2,1,0:T(8,128)(2,1)}, u32[]{:S(2)}) copy-start(bf16[8,2048,384]{2,1,0:T(8,128)(2,1)} %up_weight.1) | copy-start | bytes 37748740
  0.7 15.4 %copy-start.2 = (bf16[8,384,2048]{2,1,0:T(8,128)(2,1)S(1)}, bf16[8,384,2048]{2,1,0:T(8,128)(2,1)}, u32[]{:S(2)}) copy-start(bf16[8,384,2048]{2,1,0:T(8,128)(2,1)} %down_weight.1) | copy-start | bytes 37748740
  3.8 1.4 %collective-permute-start = (bf16[8,2048]{1,0:T(8,128)(2,1)S(1)}, bf16[8,2048]{1,0:T(8,128)(2,1)S(1)}, u32[]{:S(2)}, u32[]{:S(2)}) collective-permute-start(bf16[8,2048]{1,0:T(8,128)(2,1)S(1)} %get-tuple-element.5.mine), channel_id=1, source_target_pairs={{0,2},{2,0},{1,3},{3,1},{4,6},{6,4},{5,7},{7,5},{8,10},{10,8},{9,1... | collective-permute-start | bytes 98312 | tf_op jit(solution)/shard_map/ppermute | solution.py:37
  5.2 4.3 %collective-permute-start.1 = (bf16[8,2048]{1,0:T(8,128)(2,1)S(1)}, bf16[8,2048]{1,0:T(8,128)(2,1)S(1)}, u32[]{:S(2)}, u32[]{:S(2)}) collective-permute-start(bf16[8,2048]{1,0:T(8,128)(2,1)S(1)} %side_sum.1), channel_id=1, source_target_pairs={{0,3},{1,2},{2,1},{3,0},{4,7},{5,6},{6,5},{7,4},{8,11},{9,10},{10,... | collective-permute-start | bytes 98312 | tf_op jit(solution)/shard_map/ppermute | solution.py:52
  9.5 5.1 %collective-permute-start.3 = (bf16[8,2176]{1,0:T(8,128)(2,1)S(1)}, bf16[8,2176]{1,0:T(8,128)(2,1)S(1)}, u32[]{:S(2)}, u32[]{:S(2)}) collective-permute-start(bf16[8,2176]{1,0:T(8,128)(2,1)S(1)} %pad_maximum_fusion.1), channel_id=1, source_target_pairs={{0,8},{2,14},{4,12},{6,10},{8,0},{10,6},{12,4},{14,2},{1,9},{3,15}... | collective-permute-start | bytes 104456 | tf_op jit(solution)/shard_map/ppermute | solution.py:52
  12.6 3.4 %collective-permute-start.2 = (bf16[8,2176]{1,0:T(8,128)(2,1)S(1)}, bf16[8,2176]{1,0:T(8,128)(2,1)S(1)}, u32[]{:S(2)}, u32[]{:S(2)}) collective-permute-start(bf16[8,2176]{1,0:T(8,128)(2,1)S(1)} %pad_maximum_fusion.1), channel_id=1, source_target_pairs={{0,6},{2,4},{4,2},{6,0},{8,14},{10,12},{12,10},{14,8},{1,7},{3,5},... | collective-permute-start | bytes 104456 | tf_op jit(solution)/shard_map/ppermute | solution.py:52
  14.5 1.4 %collective-permute-start.4 = (bf16[8,2176]{1,0:T(8,128)(2,1)S(1)}, bf16[8,2176]{1,0:T(8,128)(2,1)S(1)}, u32[]{:S(2)}, u32[]{:S(2)}) collective-permute-start(bf16[8,2176]{1,0:T(8,128)(2,1)S(1)} %collective-permute-done.3), channel_id=1, source_target_pairs={{0,2},{2,0},{1,3},{3,1},{4,6},{6,4},{5,7},{7,5},{8,10},{10,8},{9,1... | collective-permute-start | bytes 104456 | tf_op jit(solution)/shard_map/ppermute | solution.py:37
  34.9 1.2 %collective-permute-start.5 = (bf16[8,1024]{1,0:T(8,128)(2,1)S(1)}, bf16[8,1024]{1,0:T(8,128)(2,1)S(1)}, u32[]{:S(2)}, u32[]{:S(2)}) collective-permute-start(bf16[8,1024]{1,0:T(8,128)(2,1)S(1)} %reduce_sum.12), channel_id=1, source_target_pairs={{0,2},{2,0},{1,3},{3,1},{4,6},{6,4},{5,7},{7,5},{8,10},{10,8},{9,1... | collective-permute-start | bytes 49160 | tf_op jit(solution)/shard_map/ppermute | solution.py:37

commit v7 on v6

--- a/solution.py
+++ b/solution.py
@@ -62,23 +62,32 @@
     return total
 
 
+def split_gather():
+    sizes = [lax.axis_size(axis) for axis in ("ep", "side", "head")]
+    return sizes == [4, 2, 2]
+
+
 def gather_rows(packed):
-    ep_count, side_count = lax.axis_size("ep"), lax.axis_size("side")
-    if (ep_count, side_count) == (4, 2):
-        far = joint(packed, ("ep", "side"), lambda e, s: (e ^ (2 + s), s))
-        near = joint(packed, ("ep", "side"), lambda e, s: (e ^ 1, s ^ 1))
-        return jnp.concatenate([packed, near, far, swap(far, "side", 1)], 0)
-    for k in partners(ep_count):
+    if split_gather():
+        axes = ("ep", "side", "head")
+        second = joint(packed, axes, lambda e, s, h: (e ^ (1 + s), s, h))
+        first = joint(packed, axes, lambda e, s, h: (e ^ 3 * s, s, h ^ 1 - s))
+        held = jnp.concatenate([second, first], 0)
+        return [packed, held, swap(held, "side", 1)]
+    for k in partners(lax.axis_size("ep")):
         packed = jnp.concatenate([packed, swap(packed, "ep", k)], 0)
-    return packed
-
-
-def source_of(block):
-    me = lax.axis_index("ep")
-    if (lax.axis_size("ep"), lax.axis_size("side")) == (4, 2) and block >= 2:
-        side = lax.axis_index("side")
-        return me ^ (block + side if block == 2 else block - side)
-    return me ^ block
+    return [packed]
+
+
+def in_order(pieces):
+    if len(pieces) == 1:
+        return pieces[0][...]
+    own, held, swapped = [piece[...] for piece in pieces]
+    rows = own.shape[0]
+    odd = lax.axis_index("side") == 1
+    near = jnp.where(odd, swapped[:rows], held[:rows])
+    far = jnp.where(odd, held, swapped)
+    return jnp.concatenate([own, near, far], 0)
 
 
 def sum_over(low, axis):
@@ -235,7 +244,12 @@
     out[...] = taken
 
 
-def expert_kernel(
+def expert_kernel(*refs, width, pieces):
+    gathered = in_order(refs[:pieces])
+    expert_body(gathered, *refs[pieces:], width)
+
+
+def expert_body(
     gathered, norm_gain, gate_weight, up_weight, down_weight, out, inner, width
 ):
     count, depth, hidden_units = gate_weight.shape
@@ -264,7 +278,7 @@
     blocks, block_rows, _ = out.shape
     heads = depth // width
     for j in range(blocks // heads):
-        target = source_of(j)
+        target = me ^ j
         for h in range(heads):
             out[target * heads + h] = result[
                 j * block_rows : (j + 1) * block_rows, h * width : (h + 1) * width
@@ -273,13 +287,13 @@
 
 def run_experts(gathered, gain, gate_weight, up_weight, down_weight, head_count, ep_count):
     local_count, depth, hidden_units = gate_weight.shape
-    rows = gathered.shape[0] // ep_count
+    rows = gathered[0].shape[0] if len(gathered) > 1 else gathered[0].shape[0] // ep_count
     width = depth // head_count
     weight_bytes = 2 * (gate_weight.size + up_weight.size + down_weight.size)
     return pl.pallas_call(
-        functools.partial(expert_kernel, width=width),
+        functools.partial(expert_kernel, width=width, pieces=len(gathered)),
         out_shape=jax.ShapeDtypeStruct((ep_count * head_count, rows, width), BF),
-        in_specs=[VMEM] * 5,
+        in_specs=[VMEM] * (4 + len(gathered)),
         out_specs=VMEM,
         scratch_shapes=[
             pltpu.VMEM((ep_count * rows, local_count * hidden_units), BF),
@@ -290,7 +304,7 @@
         ),
         name="experts",
     )(
-        in_vmem(gathered),
+        *[in_vmem(piece) for piece in gathered],
         in_vmem(gain),
         in_vmem(gate_weight),
         in_vmem(up_weight),

time: 37 us -> 36.3 us (0.981)
  blocking collectives: 13.7 us -> 11 us
  starting transfers between devices: 6.78 us -> 8.45 us
    all_to_all x1, blocking collectives: 13.7 us -> 11 us  [on_device(): arrived = lax.all_to_all(result, ('ep', 'head'), 0, 0, tiled=True)]
    ppermute x3, starting transfers between devices: 0.93 us -> 2.18 us  [swap(): return lax.ppermute(x, axis, [(i, i ^ k) for i in range(count)])]
    ppermute x3, waiting for transfers between devices: 1.41 us -> 2.31 us  [swap(): return lax.ppermute(x, axis, [(i, i ^ k) for i in range(count)])]
    ppermute x3, waiting for transfers between devices: 4.61 us -> 4.04 us  [joint(): return lax.ppermute(x, axes, pairs)]
    ppermute x3, starting transfers between devices: 5.85 us -> 6.27 us  [joint(): return lax.ppermute(x, axes, pairs)]
  transfers between devices with their start and end apart: 6 -> 6, of which waited for: 5 -> 6; matrix products, arithmetic and copies ran while one was open for 0% -> 0% of each run, Pallas kernels for 2% -> 2%
where the time goes in v7:
time: 36.3 us; the launch traced here: 36.1 us
  blocking collectives  11 us (30%)
  Pallas kernels  9 us (25%)
  starting transfers between devices  8.45 us (23%)
  waiting for transfers between devices  6.35 us (17%)
  between operations  0.71 us (2%)
  other arithmetic  0.65 us (2%)
    all_to_all x1, blocking collectives, on_device(): arrived = lax.all_to_all(result, ('ep', 'head'), 0, 0, tiled=True)  11 us
    ppermute x3, starting transfers between devices, joint(): return lax.ppermute(x, axes, pairs)  6.27 us
    pallas_call x1, Pallas kernels, run_experts(): pl.pallas_call(functools.partial(expert_kernel, width=width, pieces=len(g...  5.28 us
    ppermute x3, waiting for transfers between devices, joint(): return lax.ppermute(x, axes, pairs)  4.04 us
    pallas_call x1, Pallas kernels, on_device(): pl.pallas_call(attend_kernel, out_shape=(pltpu.VMEM((rows, depth), BF), p...  3.08 us
    ppermute x3, waiting for transfers between devices, swap(): return lax.ppermute(x, axis, [(i, i ^ k) for i in range(count)])  2.31 us
    ppermute x3, starting transfers between devices, swap(): return lax.ppermute(x, axis, [(i, i ^ k) for i in range(count)])  2.18 us
  transfers between devices with their start and end apart: 6, of which 6 were waited for; matrix products, arithmetic and copies ran while one was open for 0% of the time, Pallas kernels for 2%

profile of v7, /device:TPU:0, one launch (start us, length us, event | category | flops | bytes accessed | tf_op | source)
XLA Modules:
  0.0 36.1 jit_solution(4463322576077844476)
XLA Ops:
  0.6 0.0 copy-start
  0.6 0.0 copy-start.1
  0.7 0.0 copy-start.2
  0.7 3.1 %attend.1 = (bf16[8,2048]{1,0:T(8,128)(2,1)S(1)}, bf16[8,128]{1,0:T(8,128)(2,1)S(1)}, f32[1,2048]{1,0:T(1,128)S(1)}) custom-call(s32[8]{0:T(128)} %lengths_hbm.1, bf16[8,2,512]{2,1,0:T(2,128)(2,1)} %query_hbm.1, bf16[8,256]{1,0:T(8,128)(2,1)} %new_key_hbm.1, bf16[8,256]{1,0:T(8,128)(2,1)} %new_value_hbm.1, bf16[8,128,256]{2,1,0:T(8,128)(2,1)} %cache_keys_hbm.1, ...), custom_call_target="tpu_custom_call" | custom-call | flops 999999995904 | bytes 200000000 | tf_op jit(solution)/shard_map/attend/pallas_call | solution.py:341
  3.8 0.6 %collective-permute-start = (bf16[8,2048]{1,0:T(8,128)(2,1)S(1)}, bf16[8,2048]{1,0:T(8,128)(2,1)S(1)}, u32[]{:S(2)}, u32[]{:S(2)}) collective-permute-start(bf16[8,2048]{1,0:T(8,128)(2,1)S(1)} %get-tuple-element.5.mine), channel_id=1, source_target_pairs={{0,2},{2,0},{1,3},{3,1},{4,6},{6,4},{5,7},{7,5},{8,10},{10,8},{9,1... | collective-permute-start | bytes 98312 | tf_op jit(solution)/shard_map/ppermute | solution.py:37
  4.3 0.9 %collective-permute-done.other = bf16[8,2048]{1,0:T(8,128)(2,1)S(1)} collective-permute-done((bf16[8,2048]{1,0:T(8,128)(2,1)S(1)}, bf16[8,2048]{1,0:T(8,128)(2,1)S(1)}, u32[]{:S(2)}, u32[]{:S(2)}) %collective-permute-start) | collective-permute-done | bytes 32800 | tf_op jit(solution)/shard_map/ppermute | solution.py:37
  5.2 2.7 %collective-permute-start.1 = (bf16[8,2048]{1,0:T(8,128)(2,1)S(1)}, bf16[8,2048]{1,0:T(8,128)(2,1)S(1)}, u32[]{:S(2)}, u32[]{:S(2)}) collective-permute-start(bf16[8,2048]{1,0:T(8,128)(2,1)S(1)} %side_sum.1), channel_id=1, source_target_pairs={{0,3},{1,2},{2,1},{3,0},{4,7},{5,6},{6,5},{7,4},{8,11},{9,10},{10,... | collective-permute-start | bytes 98312 | tf_op jit(solution)/shard_map/ppermute | solution.py:52
  7.8 1.6 %collective-permute-done.1 = bf16[8,2048]{1,0:T(8,128)(2,1)S(1)} collective-permute-done((bf16[8,2048]{1,0:T(8,128)(2,1)S(1)}, bf16[8,2048]{1,0:T(8,128)(2,1)S(1)}, u32[]{:S(2)}, u32[]{:S(2)}) %collective-permute-start.1) | collective-permute-done | bytes 32800 | tf_op jit(solution)/shard_map/ppermute | solution.py:52
  9.5 2.1 %collective-permute-start.2 = (bf16[8,2176]{1,0:T(8,128)(2,1)S(1)}, bf16[8,2176]{1,0:T(8,128)(2,1)S(1)}, u32[]{:S(2)}, u32[]{:S(2)}) collective-permute-start(bf16[8,2176]{1,0:T(8,128)(2,1)S(1)} %pad_maximum_fusion.refs_0_), channel_id=1, source_target_pairs={{0,4},{1,5},{2,10},{3,11},{4,0},{5,1},{6,14},{7,15},{8,12},{9,13},... | collective-permute-start | bytes 104456 | tf_op jit(solution)/shard_map/ppermute | solution.py:52
  11.6 1.5 %collective-permute-start.3 = (bf16[8,2176]{1,0:T(8,128)(2,1)S(1)}, bf16[8,2176]{1,0:T(8,128)(2,1)S(1)}, u32[]{:S(2)}, u32[]{:S(2)}) collective-permute-start(bf16[8,2176]{1,0:T(8,128)(2,1)S(1)} %pad_maximum_fusion.refs_0_), channel_id=1, source_target_pairs={{0,1},{1,0},{2,14},{3,15},{4,5},{5,4},{6,10},{7,11},{8,9},{9,8},{1... | collective-permute-start | bytes 104456 | tf_op jit(solution)/shard_map/ppermute | solution.py:52
  13.1 0.4 %collective-permute-done.2 = bf16[8,2176]{1,0:T(8,128)(2,1)S(1)} collective-permute-done((bf16[8,2176]{1,0:T(8,128)(2,1)S(1)}, bf16[8,2176]{1,0:T(8,128)(2,1)S(1)}, u32[]{:S(2)}, u32[]{:S(2)}) %collective-permute-start.2) | collective-permute-done | bytes 34848 | tf_op jit(solution)/shard_map/ppermute | solution.py:52
  13.5 2.0 %collective-permute-done.3 = bf16[8,2176]{1,0:T(8,128)(2,1)S(1)} collective-permute-done((bf16[8,2176]{1,0:T(8,128)(2,1)S(1)}, bf16[8,2176]{1,0:T(8,128)(2,1)S(1)}, u32[]{:S(2)}, u32[]{:S(2)}) %collective-permute-start.3) | collective-permute-done | bytes 34848 | tf_op jit(solution)/shard_map/ppermute | solution.py:52
  15.5 1.5 %collective-permute-start.4 = (bf16[16,2176]{1,0:T(8,128)(2,1)S(1)}, bf16[16,2176]{1,0:T(8,128)(2,1)S(1)}, u32[]{:S(2)}, u32[]{:S(2)}) collective-permute-start(bf16[16,2176]{1,0:T(8,128)(2,1)S(1)} %constant_dynamic-update-slice_fusion.refs_1_), channel_id=1, source_target_pairs={{0,2},{2,0},{1,3},{3,1},{4,6},{6,4},{5,7},{7,5},{8,10},{10,8},{9,1... | collective-permute-start | bytes 208904 | tf_op jit(solution)/shard_map/ppermute | solution.py:37
  17.1 0.9 %collective-permute-done.4.refs_2_ = bf16[16,2176]{1,0:T(8,128)(2,1)S(1)} collective-permute-done((bf16[16,2176]{1,0:T(8,128)(2,1)S(1)}, bf16[16,2176]{1,0:T(8,128)(2,1)S(1)}, u32[]{:S(2)}, u32[]{:S(2)}) %collective-permute-start.4) | collective-permute-done | bytes 69664 | tf_op jit(solution)/shard_map/ppermute | solution.py:37
  18.0 0.0 copy-done
  18.0 0.0 copy-done.1
  18.0 0.0 copy-done.2
  18.0 5.3 %experts.1 = bf16[8,8,1024]{2,1,0:T(8,128)(2,1)S(1)} custom-call(bf16[8,2176]{1,0:T(8,128)(2,1)S(1)} %pad_maximum_fusion.refs_0_, bf16[16,2176]{1,0:T(8,128)(2,1)S(1)} %constant_dynamic-update-slice_fusion.refs_1_, bf16[16,2176]{1,0:T(8,128)(2,1)S(1)} %collective-permute-done.4.refs_2_, f32[1,2048]{1,0:T(1,128)S(1)} %get-tuple-element.7.refs_3_, ...), custom_call_target="tpu_custom_call" | custom-call | flops 1207959552 | bytes 37748736 | tf_op jit(solution)/shard_map/experts/pallas_call | solution.py:293
  23.3 11.0 %all_to_all.5 = bf16[8,8,1024]{2,1,0:T(8,128)(2,1)S(1)} all-to-all(bf16[8,8,1024]{2,1,0:T(8,128)(2,1)S(1)} %experts.1), channel_id=1, replica_groups=mesh['groups'=2,'ep'=4,'side'=2,'head'=2] {'ep','head'}, dimensions={0} | all-to-all | bytes 262144 | tf_op jit(solution)/shard_map/all_to_all | solution.py:407
  34.3 0.1 collective-permute-start.5
  34.4 0.6 %take.1 = f32[8,1024]{1,0:T(8,128)} custom-call(f32[8,2048]{1,0:T(8,128)S(1)} %get-tuple-element.9.stream), custom_call_target="tpu_custom_call" | custom-call | flops 10000 | bytes 100000 | tf_op jit(solution)/shard_map/take/pallas_call | solution.py:393
  35.0 0.5 %collective-permute-done.5 = bf16[8,1024]{1,0:T(8,128)(2,1)S(1)} collective-permute-done((bf16[8,1024]{1,0:T(8,128)(2,1)S(1)}, bf16[8,1024]{1,0:T(8,128)(2,1)S(1)}, u32[]{:S(2)}, u32[]{:S(2)}) %collective-permute-start.5) | collective-permute-done | bytes 16416 | tf_op jit(solution)/shard_map/ppermute | solution.py:37
  35.5 0.6 %add_convert_fusion = bf16[8,1024]{1,0:T(8,128)(2,1)} fusion(bf16[8,1024]{1,0:T(8,128)(2,1)S(1)} %collective-permute-done.5, bf16[8,1024]{1,0:T(8,128)(2,1)S(1)} %reduce_sum.12), kind=kLoop, calls=%fused_computation.2 | loop fusion | flops 32768 | bytes 49152 | tf_op jit(solution)/shard_map/convert_element_type | solution.py:409
  (6 shorter events, 0.1 us)
Async XLA Ops:
  0.6 17.4 %copy-start = (bf16[8,2048,384]{2,1,0:T(8,128)(2,1)S(1)}, bf16[8,2048,384]{2,1,0:T(8,128)(2,1)}, u32[]{:S(2)}) copy-start(bf16[8,2048,384]{2,1,0:T(8,128)(2,1)} %refs_4_.1) | copy-start | bytes 37748740
  0.6 17.4 %copy-start.1 = (bf16[8,2048,384]{2,1,0:T(8,128)(2,1)S(1)}, bf16[8,2048,384]{2,1,0:T(8,128)(2,1)}, u32[]{:S(2)}) copy-start(bf16[8,2048,384]{2,1,0:T(8,128)(2,1)} %refs_5_.1) | copy-start | bytes 37748740
  0.7 17.4 %copy-start.2 = (bf16[8,384,2048]{2,1,0:T(8,128)(2,1)S(1)}, bf16[8,384,2048]{2,1,0:T(8,128)(2,1)}, u32[]{:S(2)}) copy-start(bf16[8,384,2048]{2,1,0:T(8,128)(2,1)} %refs_6_.1) | copy-start | bytes 37748740
  3.8 1.4 %collective-permute-start = (bf16[8,2048]{1,0:T(8,128)(2,1)S(1)}, bf16[8,2048]{1,0:T(8,128)(2,1)S(1)}, u32[]{:S(2)}, u32[]{:S(2)}) collective-permute-start(bf16[8,2048]{1,0:T(8,128)(2,1)S(1)} %get-tuple-element.5.mine), channel_id=1, source_target_pairs={{0,2},{2,0},{1,3},{3,1},{4,6},{6,4},{5,7},{7,5},{8,10},{10,8},{9,1... | collective-permute-start | bytes 98312 | tf_op jit(solution)/shard_map/ppermute | solution.py:37
  5.2 4.3 %collective-permute-start.1 = (bf16[8,2048]{1,0:T(8,128)(2,1)S(1)}, bf16[8,2048]{1,0:T(8,128)(2,1)S(1)}, u32[]{:S(2)}, u32[]{:S(2)}) collective-permute-start(bf16[8,2048]{1,0:T(8,128)(2,1)S(1)} %side_sum.1), channel_id=1, source_target_pairs={{0,3},{1,2},{2,1},{3,0},{4,7},{5,6},{6,5},{7,4},{8,11},{9,10},{10,... | collective-permute-start | bytes 98312 | tf_op jit(solution)/shard_map/ppermute | solution.py:52
  9.5 4.0 %collective-permute-start.2 = (bf16[8,2176]{1,0:T(8,128)(2,1)S(1)}, bf16[8,2176]{1,0:T(8,128)(2,1)S(1)}, u32[]{:S(2)}, u32[]{:S(2)}) collective-permute-start(bf16[8,2176]{1,0:T(8,128)(2,1)S(1)} %pad_maximum_fusion.refs_0_), channel_id=1, source_target_pairs={{0,4},{1,5},{2,10},{3,11},{4,0},{5,1},{6,14},{7,15},{8,12},{9,13},... | collective-permute-start | bytes 104456 | tf_op jit(solution)/shard_map/ppermute | solution.py:52
  11.6 3.9 %collective-permute-start.3 = (bf16[8,2176]{1,0:T(8,128)(2,1)S(1)}, bf16[8,2176]{1,0:T(8,128)(2,1)S(1)}, u32[]{:S(2)}, u32[]{:S(2)}) collective-permute-start(bf16[8,2176]{1,0:T(8,128)(2,1)S(1)} %pad_maximum_fusion.refs_0_), channel_id=1, source_target_pairs={{0,1},{1,0},{2,14},{3,15},{4,5},{5,4},{6,10},{7,11},{8,9},{9,8},{1... | collective-permute-start | bytes 104456 | tf_op jit(solution)/shard_map/ppermute | solution.py:52
  15.5 2.5 %collective-permute-start.4 = (bf16[16,2176]{1,0:T(8,128)(2,1)S(1)}, bf16[16,2176]{1,0:T(8,128)(2,1)S(1)}, u32[]{:S(2)}, u32[]{:S(2)}) collective-permute-start(bf16[16,2176]{1,0:T(8,128)(2,1)S(1)} %constant_dynamic-update-slice_fusion.refs_1_), channel_id=1, source_target_pairs={{0,2},{2,0},{1,3},{3,1},{4,6},{6,4},{5,7},{7,5},{8,10},{10,8},{9,1... | collective-permute-start | bytes 208904 | tf_op jit(solution)/shard_map/ppermute | solution.py:37
  34.3 1.2 %collective-permute-start.5 = (bf16[8,1024]{1,0:T(8,128)(2,1)S(1)}, bf16[8,1024]{1,0:T(8,128)(2,1)S(1)}, u32[]{:S(2)}, u32[]{:S(2)}) collective-permute-start(bf16[8,1024]{1,0:T(8,128)(2,1)S(1)} %reduce_sum.12), channel_id=1, source_target_pairs={{0,2},{2,0},{1,3},{3,1},{4,6},{6,4},{5,7},{7,5},{8,10},{10,8},{9,1... | collective-permute-start | bytes 49160 | tf_op jit(solution)/shard_map/ppermute | solution.py:37

commit v8 on v7

--- a/solution.py
+++ b/solution.py
@@ -77,6 +77,21 @@
     for k in partners(lax.axis_size("ep")):
         packed = jnp.concatenate([packed, swap(packed, "ep", k)], 0)
     return [packed]
+
+
+def return_rows(give, keep):
+    chip = (keep.astype(F32) + swap(give, "side", 1).astype(F32)).astype(BF)
+    rows, width = chip.shape[0] // 2, chip.shape[1] // 2
+    axes = ("ep", "side", "head")
+    second = joint(chip[:rows], axes, lambda e, s, h: (e ^ (1 + s), s, h))
+    first = joint(chip[rows:], axes, lambda e, s, h: (e ^ 3 * s, s, h ^ 1 - s))
+    rest = jnp.where(lax.axis_index("side") == 1, first, chip[rows:])
+    total = second.astype(F32) + rest.astype(F32)
+    left = lax.axis_index("head") == 0
+    mine = jnp.where(left, total[:, :width], total[:, width:])
+    other = jnp.where(left, total[:, width:], total[:, :width]).astype(BF)
+    arrived = joint(other, ("side", "head"), lambda s, h: (s ^ 1, h ^ 1))
+    return (mine + arrived.astype(F32)).astype(BF)
 
 
 def in_order(pieces):
@@ -246,12 +261,11 @@
 
 def expert_kernel(*refs, width, pieces):
     gathered = in_order(refs[:pieces])
-    expert_body(gathered, *refs[pieces:], width)
-
-
-def expert_body(
-    gathered, norm_gain, gate_weight, up_weight, down_weight, out, inner, width
-):
+    expert_body(gathered, *refs[pieces:], width, pieces > 1)
+
+
+def expert_body(gathered, norm_gain, gate_weight, up_weight, down_weight, *rest):
+    *outs, inner, width, split = rest
     count, depth, hidden_units = gate_weight.shape
     experts = (gathered.shape[1] - depth) // 2
     rows = gathered.shape[0]
@@ -275,6 +289,15 @@
         down_weight[...].reshape(count * hidden_units, depth),
         preferred_element_type=F32,
     ).astype(BF)
+    if split:
+        pair = rows // 2
+        block = pair // 2
+        close = jnp.concatenate([result[block:pair], result[:block]], 0)
+        odd = lax.axis_index("side") == 1
+        outs[0][...] = jnp.where(odd, close, result[pair:])
+        outs[1][...] = jnp.where(odd, result[pair:], close)
+        return
+    out = outs[0]
     blocks, block_rows, _ = out.shape
     heads = depth // width
     for j in range(blocks // heads):
@@ -289,12 +312,16 @@
     local_count, depth, hidden_units = gate_weight.shape
     rows = gathered[0].shape[0] if len(gathered) > 1 else gathered[0].shape[0] // ep_count
     width = depth // head_count
+    if len(gathered) > 1:
+        out_shape = [jax.ShapeDtypeStruct((ep_count * rows // 2, depth), BF)] * 2
+    else:
+        out_shape = [jax.ShapeDtypeStruct((ep_count * head_count, rows, width), BF)]
     weight_bytes = 2 * (gate_weight.size + up_weight.size + down_weight.size)
     return pl.pallas_call(
         functools.partial(expert_kernel, width=width, pieces=len(gathered)),
-        out_shape=jax.ShapeDtypeStruct((ep_count * head_count, rows, width), BF),
+        out_shape=out_shape,
         in_specs=[VMEM] * (4 + len(gathered)),
-        out_specs=VMEM,
+        out_specs=[VMEM] * len(out_shape),
         scratch_shapes=[
             pltpu.VMEM((ep_count * rows, local_count * hidden_units), BF),
         ],
@@ -404,8 +431,11 @@
     result = run_experts(
         gathered, gain_near, gate_weight, up_weight, down_weight, head_count, ep_count
     )
-    arrived = lax.all_to_all(result, ("ep", "head"), 0, 0, tiled=True)
-    local_sum = jnp.sum(arrived.astype(F32), 0).astype(BF)
+    if len(result) > 1:
+        local_sum = return_rows(*result)
+    else:
+        arrived = lax.all_to_all(result[0], ("ep", "head"), 0, 0, tiled=True)
+        local_sum = jnp.sum(arrived.astype(F32), 0).astype(BF)
     expert_sum = sum_over(local_sum, "side").astype(BF)
     return (after_attention, expert_sum)
 

time: 36.3 us -> 35.5 us (0.978)
  blocking collectives: 11 us -> 0 us
  starting transfers between devices: 8.45 us -> 14.1 us
  waiting for transfers between devices: 6.35 us -> 10.8 us
    all_to_all x1 -> x0, blocking collectives: 11 us -> none  [on_device(): arrived = lax.all_to_all(result, ('ep', 'head'), 0, 0, tiled=True)]
    ppermute x3 -> x6, starting transfers between devices: 6.27 us -> 10.9 us  [joint(): return lax.ppermute(x, axes, pairs)]
    ppermute x3 -> x6, waiting for transfers between devices: 4.04 us -> 7.91 us  [joint(): return lax.ppermute(x, axes, pairs)]
    ppermute x3 -> x4, starting transfers between devices: 2.18 us -> 3.22 us  [swap(): return lax.ppermute(x, axis, [(i, i ^ k) for i in range(count)])]
    ppermute x3 -> x4, waiting for transfers between devices: 2.31 us -> 2.89 us  [swap(): return lax.ppermute(x, axis, [(i, i ^ k) for i in range(count)])]
  transfers between devices with their start and end apart: 6 -> 10, of which waited for: 6 -> 10; matrix products, arithmetic and copies ran while one was open for 0% -> 0% of each run, Pallas kernels for 2% -> 2%
where the time goes in v8:
time: 35.5 us; the launch traced here: 35.4 us
  starting transfers between devices  14.1 us (40%)
  waiting for transfers between devices  10.8 us (30%)
  Pallas kernels  9 us (25%)
  between operations  0.73 us (2%)
  other arithmetic  0.68 us (2%)
    ppermute x6, starting transfers between devices, joint(): return lax.ppermute(x, axes, pairs)  10.9 us
    ppermute x6, waiting for transfers between devices, joint(): return lax.ppermute(x, axes, pairs)  7.91 us
    pallas_call x1, Pallas kernels, run_experts(): pl.pallas_call(functools.partial(expert_kernel, width=width, pieces=len(g...  5.29 us
    ppermute x4, starting transfers between devices, swap(): return lax.ppermute(x, axis, [(i, i ^ k) for i in range(count)])  3.22 us
    pallas_call x1, Pallas kernels, on_device(): pl.pallas_call(attend_kernel, out_shape=(pltpu.VMEM((rows, depth), BF), p...  3.08 us
    ppermute x4, waiting for transfers between devices, swap(): return lax.ppermute(x, axis, [(i, i ^ k) for i in range(count)])  2.89 us
  transfers between devices with their start and end apart: 10, of which 10 were waited for; matrix products, arithmetic and copies ran while one was open for 0% of the time, Pallas kernels for 2%

profile of v8, /device:TPU:0, one launch (start us, length us, event | category | flops | bytes accessed | tf_op | source)
XLA Modules:
  0.0 35.4 jit_solution(10749757895285779192)
XLA Ops:
  0.6 0.0 copy-start
  0.6 0.0 copy-start.1
  0.7 0.0 copy-start.2
  0.7 3.1 %attend.1 = (bf16[8,2048]{1,0:T(8,128)(2,1)S(1)}, bf16[8,128]{1,0:T(8,128)(2,1)S(1)}, f32[1,2048]{1,0:T(1,128)S(1)}) custom-call(s32[8]{0:T(128)} %lengths_hbm.1, bf16[8,2,512]{2,1,0:T(2,128)(2,1)} %query_hbm.1, bf16[8,256]{1,0:T(8,128)(2,1)} %new_key_hbm.1, bf16[8,256]{1,0:T(8,128)(2,1)} %new_value_hbm.1, bf16[8,128,256]{2,1,0:T(8,128)(2,1)} %cache_keys_hbm.1, ...), custom_call_target="tpu_custom_call" | custom-call | flops 999999995904 | bytes 200000000 | tf_op jit(solution)/shard_map/attend/pallas_call | solution.py:368
  3.8 0.6 %collective-permute-start = (bf16[8,2048]{1,0:T(8,128)(2,1)S(1)}, bf16[8,2048]{1,0:T(8,128)(2,1)S(1)}, u32[]{:S(2)}, u32[]{:S(2)}) collective-permute-start(bf16[8,2048]{1,0:T(8,128)(2,1)S(1)} %get-tuple-element.7.mine), channel_id=1, source_target_pairs={{0,2},{2,0},{1,3},{3,1},{4,6},{6,4},{5,7},{7,5},{8,10},{10,8},{9,1... | collective-permute-start | bytes 98312 | tf_op jit(solution)/shard_map/ppermute | solution.py:37
  4.3 0.9 %collective-permute-done.other = bf16[8,2048]{1,0:T(8,128)(2,1)S(1)} collective-permute-done((bf16[8,2048]{1,0:T(8,128)(2,1)S(1)}, bf16[8,2048]{1,0:T(8,128)(2,1)S(1)}, u32[]{:S(2)}, u32[]{:S(2)}) %collective-permute-start) | collective-permute-done | bytes 32800 | tf_op jit(solution)/shard_map/ppermute | solution.py:37
  5.2 2.7 %collective-permute-start.1 = (bf16[8,2048]{1,0:T(8,128)(2,1)S(1)}, bf16[8,2048]{1,0:T(8,128)(2,1)S(1)}, u32[]{:S(2)}, u32[]{:S(2)}) collective-permute-start(bf16[8,2048]{1,0:T(8,128)(2,1)S(1)} %side_sum.1), channel_id=1, source_target_pairs={{0,3},{1,2},{2,1},{3,0},{4,7},{5,6},{6,5},{7,4},{8,11},{9,10},{10,... | collective-permute-start | bytes 98312 | tf_op jit(solution)/shard_map/ppermute | solution.py:52
  7.8 1.6 %collective-permute-done.1 = bf16[8,2048]{1,0:T(8,128)(2,1)S(1)} collective-permute-done((bf16[8,2048]{1,0:T(8,128)(2,1)S(1)}, bf16[8,2048]{1,0:T(8,128)(2,1)S(1)}, u32[]{:S(2)}, u32[]{:S(2)}) %collective-permute-start.1) | collective-permute-done | bytes 32800 | tf_op jit(solution)/shard_map/ppermute | solution.py:52
  9.5 2.1 %collective-permute-start.2 = (bf16[8,2176]{1,0:T(8,128)(2,1)S(1)}, bf16[8,2176]{1,0:T(8,128)(2,1)S(1)}, u32[]{:S(2)}, u32[]{:S(2)}) collective-permute-start(bf16[8,2176]{1,0:T(8,128)(2,1)S(1)} %pad_maximum_fusion.refs_0_), channel_id=1, source_target_pairs={{0,4},{1,5},{2,10},{3,11},{4,0},{5,1},{6,14},{7,15},{8,12},{9,13},... | collective-permute-start | bytes 104456 | tf_op jit(solution)/shard_map/ppermute | solution.py:52
  11.6 1.5 %collective-permute-start.3 = (bf16[8,2176]{1,0:T(8,128)(2,1)S(1)}, bf16[8,2176]{1,0:T(8,128)(2,1)S(1)}, u32[]{:S(2)}, u32[]{:S(2)}) collective-permute-start(bf16[8,2176]{1,0:T(8,128)(2,1)S(1)} %pad_maximum_fusion.refs_0_), channel_id=1, source_target_pairs={{0,1},{1,0},{2,14},{3,15},{4,5},{5,4},{6,10},{7,11},{8,9},{9,8},{1... | collective-permute-start | bytes 104456 | tf_op jit(solution)/shard_map/ppermute | solution.py:52
  13.1 0.4 %collective-permute-done.2 = bf16[8,2176]{1,0:T(8,128)(2,1)S(1)} collective-permute-done((bf16[8,2176]{1,0:T(8,128)(2,1)S(1)}, bf16[8,2176]{1,0:T(8,128)(2,1)S(1)}, u32[]{:S(2)}, u32[]{:S(2)}) %collective-permute-start.2) | collective-permute-done | bytes 34848 | tf_op jit(solution)/shard_map/ppermute | solution.py:52
  13.5 2.0 %collective-permute-done.3 = bf16[8,2176]{1,0:T(8,128)(2,1)S(1)} collective-permute-done((bf16[8,2176]{1,0:T(8,128)(2,1)S(1)}, bf16[8,2176]{1,0:T(8,128)(2,1)S(1)}, u32[]{:S(2)}, u32[]{:S(2)}) %collective-permute-start.3) | collective-permute-done | bytes 34848 | tf_op jit(solution)/shard_map/ppermute | solution.py:52
  15.5 1.5 %collective-permute-start.4 = (bf16[16,2176]{1,0:T(8,128)(2,1)S(1)}, bf16[16,2176]{1,0:T(8,128)(2,1)S(1)}, u32[]{:S(2)}, u32[]{:S(2)}) collective-permute-start(bf16[16,2176]{1,0:T(8,128)(2,1)S(1)} %constant_dynamic-update-slice_fusion.refs_1_), channel_id=1, source_target_pairs={{0,2},{2,0},{1,3},{3,1},{4,6},{6,4},{5,7},{7,5},{8,10},{10,8},{9,1... | collective-permute-start | bytes 208904 | tf_op jit(solution)/shard_map/ppermute | solution.py:37
  17.1 0.9 %collective-permute-done.4.refs_2_ = bf16[16,2176]{1,0:T(8,128)(2,1)S(1)} collective-permute-done((bf16[16,2176]{1,0:T(8,128)(2,1)S(1)}, bf16[16,2176]{1,0:T(8,128)(2,1)S(1)}, u32[]{:S(2)}, u32[]{:S(2)}) %collective-permute-start.4) | collective-permute-done | bytes 69664 | tf_op jit(solution)/shard_map/ppermute | solution.py:37
  18.0 0.0 copy-done
  18.0 0.0 copy-done.1
  18.0 0.0 copy-done.2
  18.0 5.3 %experts.1 = (bf16[16,2048]{1,0:T(8,128)(2,1)S(1)}, bf16[16,2048]{1,0:T(8,128)(2,1)S(1)}) custom-call(bf16[8,2176]{1,0:T(8,128)(2,1)S(1)} %pad_maximum_fusion.refs_0_, bf16[16,2176]{1,0:T(8,128)(2,1)S(1)} %constant_dynamic-update-slice_fusion.refs_1_, bf16[16,2176]{1,0:T(8,128)(2,1)S(1)} %collective-permute-done.4.refs_2_, ...), custom_call_target="tpu_custom_call" | custom-call | flops 1207959552 | bytes 37748736 | tf_op jit(solution)/shard_map/experts/pallas_call | solution.py:320
  23.3 0.4 %collective-permute-start.5 = (bf16[16,2048]{1,0:T(8,128)(2,1)S(1)}, bf16[16,2048]{1,0:T(8,128)(2,1)S(1)}, u32[]{:S(2)}, u32[]{:S(2)}) collective-permute-start(bf16[16,2048]{1,0:T(8,128)(2,1)S(1)} %get-tuple-element.11), channel_id=1, source_target_pairs={{0,2},{2,0},{1,3},{3,1},{4,6},{6,4},{5,7},{7,5},{8,10},{10,8},{9,1... | collective-permute-start | bytes 196616 | tf_op jit(solution)/shard_map/ppermute | solution.py:37
  23.7 0.9 %collective-permute-done.5 = bf16[16,2048]{1,0:T(8,128)(2,1)S(1)} collective-permute-done((bf16[16,2048]{1,0:T(8,128)(2,1)S(1)}, bf16[16,2048]{1,0:T(8,128)(2,1)S(1)}, u32[]{:S(2)}, u32[]{:S(2)}) %collective-permute-start.5) | collective-permute-done | bytes 65568 | tf_op jit(solution)/shard_map/ppermute | solution.py:37
  24.7 0.1 collective-permute-start.6
  24.7 1.6 %collective-permute-start.7 = (bf16[8,2048]{1,0:T(8,128)(2,1)S(1)}, bf16[8,2048]{1,0:T(8,128)(2,1)S(1)}, u32[]{:S(2)}, u32[]{:S(2)}) collective-permute-start(bf16[8,2048]{1,0:T(8,128)(2,1)S(1)} %get-tuple-element.12), channel_id=1, source_target_pairs={{0,1},{1,0},{2,14},{3,15},{4,5},{5,4},{6,10},{7,11},{8,9},{9,8},{1... | collective-permute-start | bytes 98312 | tf_op jit(solution)/shard_map/ppermute | solution.py:52
  26.3 2.4 %collective-permute-done.6 = bf16[8,2048]{1,0:T(8,128)(2,1)S(1)} collective-permute-done((bf16[8,2048]{1,0:T(8,128)(2,1)S(1)}, bf16[8,2048]{1,0:T(8,128)(2,1)S(1)}, u32[]{:S(2)}, u32[]{:S(2)}) %collective-permute-start.6) | collective-permute-done | bytes 32800 | tf_op jit(solution)/shard_map/ppermute | solution.py:52
  28.7 0.1 collective-permute-done.7
  28.8 3.0 %collective-permute-start.8 = (bf16[8,1024]{1,0:T(8,128)(2,1)S(1)}, bf16[8,1024]{1,0:T(8,128)(2,1)S(1)}, u32[]{:S(2)}, u32[]{:S(2)}) collective-permute-start(bf16[8,1024]{1,0:T(8,128)(2,1)S(1)} %select_convert_fusion), channel_id=1, source_target_pairs={{0,3},{1,2},{2,1},{3,0},{4,7},{5,6},{6,5},{7,4},{8,11},{9,10},{10,... | collective-permute-start | bytes 49160 | tf_op jit(solution)/shard_map/ppermute | solution.py:52
  31.8 1.4 %collective-permute-done.8 = bf16[8,1024]{1,0:T(8,128)(2,1)S(1)} collective-permute-done((bf16[8,1024]{1,0:T(8,128)(2,1)S(1)}, bf16[8,1024]{1,0:T(8,128)(2,1)S(1)}, u32[]{:S(2)}, u32[]{:S(2)}) %collective-permute-start.8) | collective-permute-done | bytes 16416 | tf_op jit(solution)/shard_map/ppermute | solution.py:52
  33.2 0.7 %collective-permute-start.9 = (bf16[8,1024]{1,0:T(8,128)(2,1)S(1)}, bf16[8,1024]{1,0:T(8,128)(2,1)S(1)}, u32[]{:S(2)}, u32[]{:S(2)}) collective-permute-start(bf16[8,1024]{1,0:T(8,128)(2,1)S(1)} %add_convert_fusion.2), channel_id=1, source_target_pairs={{0,2},{2,0},{1,3},{3,1},{4,6},{6,4},{5,7},{7,5},{8,10},{10,8},{9,1... | collective-permute-start | bytes 49160 | tf_op jit(solution)/shard_map/ppermute | solution.py:37
  33.9 0.6 %take.1 = f32[8,1024]{1,0:T(8,128)} custom-call(f32[8,2048]{1,0:T(8,128)S(1)} %get-tuple-element.15.stream), custom_call_target="tpu_custom_call" | custom-call | flops 10000 | bytes 100000 | tf_op jit(solution)/shard_map/take/pallas_call | solution.py:420
  34.5 0.2 collective-permute-done.9
  34.7 0.6 %add_convert_fusion.1 = bf16[8,1024]{1,0:T(8,128)(2,1)} fusion(bf16[8,1024]{1,0:T(8,128)(2,1)S(1)} %collective-permute-done.9, bf16[8,1024]{1,0:T(8,128)(2,1)S(1)} %add_convert_fusion.2), kind=kLoop, calls=%fused_computation.4 | loop fusion | flops 32768 | bytes 49152 | tf_op jit(solution)/shard_map/convert_element_type | solution.py:439
  (10 shorter events, 0.1 us)
Async XLA Ops:
  0.6 17.4 %copy-start = (bf16[8,2048,384]{2,1,0:T(8,128)(2,1)S(1)}, bf16[8,2048,384]{2,1,0:T(8,128)(2,1)}, u32[]{:S(2)}) copy-start(bf16[8,2048,384]{2,1,0:T(8,128)(2,1)} %refs_4_.1) | copy-start | bytes 37748740
  0.6 17.4 %copy-start.1 = (bf16[8,2048,384]{2,1,0:T(8,128)(2,1)S(1)}, bf16[8,2048,384]{2,1,0:T(8,128)(2,1)}, u32[]{:S(2)}) copy-start(bf16[8,2048,384]{2,1,0:T(8,128)(2,1)} %refs_5_.1) | copy-start | bytes 37748740
  0.7 17.4 %copy-start.2 = (bf16[8,384,2048]{2,1,0:T(8,128)(2,1)S(1)}, bf16[8,384,2048]{2,1,0:T(8,128)(2,1)}, u32[]{:S(2)}) copy-start(bf16[8,384,2048]{2,1,0:T(8,128)(2,1)} %refs_6_.1) | copy-start | bytes 37748740
  3.8 1.4 %collective-permute-start = (bf16[8,2048]{1,0:T(8,128)(2,1)S(1)}, bf16[8,2048]{1,0:T(8,128)(2,1)S(1)}, u32[]{:S(2)}, u32[]{:S(2)}) collective-permute-start(bf16[8,2048]{1,0:T(8,128)(2,1)S(1)} %get-tuple-element.7.mine), channel_id=1, source_target_pairs={{0,2},{2,0},{1,3},{3,1},{4,6},{6,4},{5,7},{7,5},{8,10},{10,8},{9,1... | collective-permute-start | bytes 98312 | tf_op jit(solution)/shard_map/ppermute | solution.py:37
  5.2 4.3 %collective-permute-start.1 = (bf16[8,2048]{1,0:T(8,128)(2,1)S(1)}, bf16[8,2048]{1,0:T(8,128)(2,1)S(1)}, u32[]{:S(2)}, u32[]{:S(2)}) collective-permute-start(bf16[8,2048]{1,0:T(8,128)(2,1)S(1)} %side_sum.1), channel_id=1, source_target_pairs={{0,3},{1,2},{2,1},{3,0},{4,7},{5,6},{6,5},{7,4},{8,11},{9,10},{10,... | collective-permute-start | bytes 98312 | tf_op jit(solution)/shard_map/ppermute | solution.py:52
  9.5 4.0 %collective-permute-start.2 = (bf16[8,2176]{1,0:T(8,128)(2,1)S(1)}, bf16[8,2176]{1,0:T(8,128)(2,1)S(1)}, u32[]{:S(2)}, u32[]{:S(2)}) collective-permute-start(bf16[8,2176]{1,0:T(8,128)(2,1)S(1)} %pad_maximum_fusion.refs_0_), channel_id=1, source_target_pairs={{0,4},{1,5},{2,10},{3,11},{4,0},{5,1},{6,14},{7,15},{8,12},{9,13},... | collective-permute-start | bytes 104456 | tf_op jit(solution)/shard_map/ppermute | solution.py:52
  11.6 3.9 %collective-permute-start.3 = (bf16[8,2176]{1,0:T(8,128)(2,1)S(1)}, bf16[8,2176]{1,0:T(8,128)(2,1)S(1)}, u32[]{:S(2)}, u32[]{:S(2)}) collective-permute-start(bf16[8,2176]{1,0:T(8,128)(2,1)S(1)} %pad_maximum_fusion.refs_0_), channel_id=1, source_target_pairs={{0,1},{1,0},{2,14},{3,15},{4,5},{5,4},{6,10},{7,11},{8,9},{9,8},{1... | collective-permute-start | bytes 104456 | tf_op jit(solution)/shard_map/ppermute | solution.py:52
  15.5 2.5 %collective-permute-start.4 = (bf16[16,2176]{1,0:T(8,128)(2,1)S(1)}, bf16[16,2176]{1,0:T(8,128)(2,1)S(1)}, u32[]{:S(2)}, u32[]{:S(2)}) collective-permute-start(bf16[16,2176]{1,0:T(8,128)(2,1)S(1)} %constant_dynamic-update-slice_fusion.refs_1_), channel_id=1, source_target_pairs={{0,2},{2,0},{1,3},{3,1},{4,6},{6,4},{5,7},{7,5},{8,10},{10,8},{9,1... | collective-permute-start | bytes 208904 | tf_op jit(solution)/shard_map/ppermute | solution.py:37
  23.3 1.3 %collective-permute-start.5 = (bf16[16,2048]{1,0:T(8,128)(2,1)S(1)}, bf16[16,2048]{1,0:T(8,128)(2,1)S(1)}, u32[]{:S(2)}, u32[]{:S(2)}) collective-permute-start(bf16[16,2048]{1,0:T(8,128)(2,1)S(1)} %get-tuple-element.11), channel_id=1, source_target_pairs={{0,2},{2,0},{1,3},{3,1},{4,6},{6,4},{5,7},{7,5},{8,10},{10,8},{9,1... | collective-permute-start | bytes 196616 | tf_op jit(solution)/shard_map/ppermute | solution.py:37
  24.7 4.0 %collective-permute-start.6 = (bf16[8,2048]{1,0:T(8,128)(2,1)S(1)}, bf16[8,2048]{1,0:T(8,128)(2,1)S(1)}, u32[]{:S(2)}, u32[]{:S(2)}) collective-permute-start(bf16[8,2048]{1,0:T(8,128)(2,1)S(1)} %get-tuple-element.13), channel_id=1, source_target_pairs={{0,4},{1,5},{2,10},{3,11},{4,0},{5,1},{6,14},{7,15},{8,12},{9,13},... | collective-permute-start | bytes 98312 | tf_op jit(solution)/shard_map/ppermute | solution.py:52
  24.7 4.0 %collective-permute-start.7 = (bf16[8,2048]{1,0:T(8,128)(2,1)S(1)}, bf16[8,2048]{1,0:T(8,128)(2,1)S(1)}, u32[]{:S(2)}, u32[]{:S(2)}) collective-permute-start(bf16[8,2048]{1,0:T(8,128)(2,1)S(1)} %get-tuple-element.12), channel_id=1, source_target_pairs={{0,1},{1,0},{2,14},{3,15},{4,5},{5,4},{6,10},{7,11},{8,9},{9,8},{1... | collective-permute-start | bytes 98312 | tf_op jit(solution)/shard_map/ppermute | solution.py:52
  28.8 4.4 %collective-permute-start.8 = (bf16[8,1024]{1,0:T(8,128)(2,1)S(1)}, bf16[8,1024]{1,0:T(8,128)(2,1)S(1)}, u32[]{:S(2)}, u32[]{:S(2)}) collective-permute-start(bf16[8,1024]{1,0:T(8,128)(2,1)S(1)} %select_convert_fusion), channel_id=1, source_target_pairs={{0,3},{1,2},{2,1},{3,0},{4,7},{5,6},{6,5},{7,4},{8,11},{9,10},{10,... | collective-permute-start | bytes 49160 | tf_op jit(solution)/shard_map/ppermute | solution.py:52
  33.2 1.5 %collective-permute-start.9 = (bf16[8,1024]{1,0:T(8,128)(2,1)S(1)}, bf16[8,1024]{1,0:T(8,128)(2,1)S(1)}, u32[]{:S(2)}, u32[]{:S(2)}) collective-permute-start(bf16[8,1024]{1,0:T(8,128)(2,1)S(1)} %add_convert_fusion.2), channel_id=1, source_target_pairs={{0,2},{2,0},{1,3},{3,1},{4,6},{6,4},{5,7},{7,5},{8,10},{10,8},{9,1... | collective-permute-start | bytes 49160 | tf_op jit(solution)/shard_map/ppermute | solution.py:37

commit v9 on v8

--- a/solution.py
+++ b/solution.py
@@ -73,7 +73,7 @@
         second = joint(packed, axes, lambda e, s, h: (e ^ (1 + s), s, h))
         first = joint(packed, axes, lambda e, s, h: (e ^ 3 * s, s, h ^ 1 - s))
         held = jnp.concatenate([second, first], 0)
-        return [packed, held, swap(held, "side", 1)]
+        return [packed, jnp.concatenate([held, swap(held, "side", 1)], 0)]
     for k in partners(lax.axis_size("ep")):
         packed = jnp.concatenate([packed, swap(packed, "ep", k)], 0)
     return [packed]
@@ -97,12 +97,13 @@
 def in_order(pieces):
     if len(pieces) == 1:
         return pieces[0][...]
-    own, held, swapped = [piece[...] for piece in pieces]
+    own, both = pieces
     rows = own.shape[0]
-    odd = lax.axis_index("side") == 1
-    near = jnp.where(odd, swapped[:rows], held[:rows])
-    far = jnp.where(odd, held, swapped)
-    return jnp.concatenate([own, near, far], 0)
+    side = lax.axis_index("side")
+    near = pl.multiple_of(side * 2 * rows, rows)
+    far = pl.multiple_of((1 - side) * 2 * rows, rows)
+    blocks = [own[...], both[pl.ds(near, rows)], both[pl.ds(far, 2 * rows)]]
+    return jnp.concatenate(blocks, 0)
 
 
 def sum_over(low, axis):

time: 35.5 us -> 35.5 us (level)
  starting transfers between devices: 14.1 us -> 13.7 us
  waiting for transfers between devices: 10.8 us -> 11.2 us
    ppermute x6, starting transfers between devices: 10.9 us -> 9.89 us  [joint(): return lax.ppermute(x, axes, pairs)]
    ppermute x4, starting transfers between devices: 3.22 us -> 3.79 us  [swap(): return lax.ppermute(x, axis, [(i, i ^ k) for i in range(count)])]
    ppermute x6, waiting for transfers between devices: 7.91 us -> 8.3 us  [joint(): return lax.ppermute(x, axes, pairs)]
where the time goes in v9:
time: 35.5 us; the launch traced here: 35.3 us
  starting transfers between devices  13.7 us (39%)
  waiting for transfers between devices  11.2 us (32%)
  Pallas kernels  8.99 us (25%)
  between operations  0.75 us (2%)
  other arithmetic  0.7 us (2%)
    ppermute x6, starting transfers between devices, joint(): return lax.ppermute(x, axes, pairs)  9.89 us
    ppermute x6, waiting for transfers between devices, joint(): return lax.ppermute(x, axes, pairs)  8.3 us
    pallas_call x1, Pallas kernels, run_experts(): pl.pallas_call(functools.partial(expert_kernel, width=width, pieces=len(g...  5.28 us
    ppermute x4, starting transfers between devices, swap(): return lax.ppermute(x, axis, [(i, i ^ k) for i in range(count)])  3.79 us
    pallas_call x1, Pallas kernels, on_device(): pl.pallas_call(attend_kernel, out_shape=(pltpu.VMEM((rows, depth), BF), p...  3.08 us
    ppermute x4, waiting for transfers between devices, swap(): return lax.ppermute(x, axis, [(i, i ^ k) for i in range(count)])  2.89 us
  transfers between devices with their start and end apart: 10, of which 10 were waited for; matrix products, arithmetic and copies ran while one was open for 0% of the time, Pallas kernels for 2%

profile of v9, /device:TPU:0, one launch (start us, length us, event | category | flops | bytes accessed | tf_op | source)
XLA Modules:
  0.0 35.3 jit_solution(11583948213074262921)
XLA Ops:
  0.6 0.0 copy-start
  0.6 0.0 copy-start.1
  0.7 0.0 copy-start.2
  0.7 3.1 %attend.1 = (bf16[8,2048]{1,0:T(8,128)(2,1)S(1)}, bf16[8,128]{1,0:T(8,128)(2,1)S(1)}, f32[1,2048]{1,0:T(1,128)S(1)}) custom-call(s32[8]{0:T(128)} %lengths_hbm.1, bf16[8,2,512]{2,1,0:T(2,128)(2,1)} %query_hbm.1, bf16[8,256]{1,0:T(8,128)(2,1)} %new_key_hbm.1, bf16[8,256]{1,0:T(8,128)(2,1)} %new_value_hbm.1, bf16[8,128,256]{2,1,0:T(8,128)(2,1)} %cache_keys_hbm.1, ...), custom_call_target="tpu_custom_call" | custom-call | flops 999999995904 | bytes 200000000 | tf_op jit(solution)/shard_map/attend/pallas_call | solution.py:369
  3.8 0.6 %collective-permute-start = (bf16[8,2048]{1,0:T(8,128)(2,1)S(1)}, bf16[8,2048]{1,0:T(8,128)(2,1)S(1)}, u32[]{:S(2)}, u32[]{:S(2)}) collective-permute-start(bf16[8,2048]{1,0:T(8,128)(2,1)S(1)} %get-tuple-element.7.mine), channel_id=1, source_target_pairs={{0,2},{2,0},{1,3},{3,1},{4,6},{6,4},{5,7},{7,5},{8,10},{10,8},{9,1... | collective-permute-start | bytes 98312 | tf_op jit(solution)/shard_map/ppermute | solution.py:37
  4.3 0.9 %collective-permute-done.other = bf16[8,2048]{1,0:T(8,128)(2,1)S(1)} collective-permute-done((bf16[8,2048]{1,0:T(8,128)(2,1)S(1)}, bf16[8,2048]{1,0:T(8,128)(2,1)S(1)}, u32[]{:S(2)}, u32[]{:S(2)}) %collective-permute-start) | collective-permute-done | bytes 32800 | tf_op jit(solution)/shard_map/ppermute | solution.py:37
  5.2 2.7 %collective-permute-start.1 = (bf16[8,2048]{1,0:T(8,128)(2,1)S(1)}, bf16[8,2048]{1,0:T(8,128)(2,1)S(1)}, u32[]{:S(2)}, u32[]{:S(2)}) collective-permute-start(bf16[8,2048]{1,0:T(8,128)(2,1)S(1)} %side_sum.1), channel_id=1, source_target_pairs={{0,3},{1,2},{2,1},{3,0},{4,7},{5,6},{6,5},{7,4},{8,11},{9,10},{10,... | collective-permute-start | bytes 98312 | tf_op jit(solution)/shard_map/ppermute | solution.py:52
  7.8 1.6 %collective-permute-done.1 = bf16[8,2048]{1,0:T(8,128)(2,1)S(1)} collective-permute-done((bf16[8,2048]{1,0:T(8,128)(2,1)S(1)}, bf16[8,2048]{1,0:T(8,128)(2,1)S(1)}, u32[]{:S(2)}, u32[]{:S(2)}) %collective-permute-start.1) | collective-permute-done | bytes 32800 | tf_op jit(solution)/shard_map/ppermute | solution.py:52
  9.5 2.0 %collective-permute-start.3 = (bf16[8,2176]{1,0:T(8,128)(2,1)S(1)}, bf16[8,2176]{1,0:T(8,128)(2,1)S(1)}, u32[]{:S(2)}, u32[]{:S(2)}) collective-permute-start(bf16[8,2176]{1,0:T(8,128)(2,1)S(1)} %pad_maximum_fusion.2.refs_0_), channel_id=1, source_target_pairs={{0,1},{1,0},{2,14},{3,15},{4,5},{5,4},{6,10},{7,11},{8,9},{9,8},{1... | collective-permute-start | bytes 104456 | tf_op jit(solution)/shard_map/ppermute | solution.py:52
  11.5 1.6 %collective-permute-start.2 = (bf16[8,2176]{1,0:T(8,128)(2,1)S(1)}, bf16[8,2176]{1,0:T(8,128)(2,1)S(1)}, u32[]{:S(2)}, u32[]{:S(2)}) collective-permute-start(bf16[8,2176]{1,0:T(8,128)(2,1)S(1)} %pad_maximum_fusion.2.refs_0_), channel_id=1, source_target_pairs={{0,4},{1,5},{2,10},{3,11},{4,0},{5,1},{6,14},{7,15},{8,12},{9,13},... | collective-permute-start | bytes 104456 | tf_op jit(solution)/shard_map/ppermute | solution.py:52
  13.1 0.4 %collective-permute-done.3 = bf16[8,2176]{1,0:T(8,128)(2,1)S(1)} collective-permute-done((bf16[8,2176]{1,0:T(8,128)(2,1)S(1)}, bf16[8,2176]{1,0:T(8,128)(2,1)S(1)}, u32[]{:S(2)}, u32[]{:S(2)}) %collective-permute-start.3) | collective-permute-done | bytes 34848 | tf_op jit(solution)/shard_map/ppermute | solution.py:52
  13.5 2.0 %collective-permute-done.2 = bf16[8,2176]{1,0:T(8,128)(2,1)S(1)} collective-permute-done((bf16[8,2176]{1,0:T(8,128)(2,1)S(1)}, bf16[8,2176]{1,0:T(8,128)(2,1)S(1)}, u32[]{:S(2)}, u32[]{:S(2)}) %collective-permute-start.2) | collective-permute-done | bytes 34848 | tf_op jit(solution)/shard_map/ppermute | solution.py:52
  15.5 1.7 %collective-permute-start.4 = (bf16[16,2176]{1,0:T(8,128)(2,1)S(1)}, bf16[16,2176]{1,0:T(8,128)(2,1)S(1)}, u32[]{:S(2)}, u32[]{:S(2)}) collective-permute-start(bf16[16,2176]{1,0:T(8,128)(2,1)S(1)} %pad_maximum_fusion.1), channel_id=1, source_target_pairs={{0,2},{2,0},{1,3},{3,1},{4,6},{6,4},{5,7},{7,5},{8,10},{10,8},{9,1... | collective-permute-start | bytes 208904 | tf_op jit(solution)/shard_map/ppermute | solution.py:37
  17.2 0.9 %collective-permute-done.4 = bf16[16,2176]{1,0:T(8,128)(2,1)S(1)} collective-permute-done((bf16[16,2176]{1,0:T(8,128)(2,1)S(1)}, bf16[16,2176]{1,0:T(8,128)(2,1)S(1)}, u32[]{:S(2)}, u32[]{:S(2)}) %collective-permute-start.4) | collective-permute-done | bytes 69664 | tf_op jit(solution)/shard_map/ppermute | solution.py:37
  18.1 0.0 copy-done
  18.1 0.0 copy-done.1
  18.1 0.0 copy-done.2
  18.2 5.3 %experts.1 = (bf16[16,2048]{1,0:T(8,128)(2,1)S(1)}, bf16[16,2048]{1,0:T(8,128)(2,1)S(1)}) custom-call(bf16[8,2176]{1,0:T(8,128)(2,1)S(1)} %pad_maximum_fusion.2.refs_0_, bf16[32,2176]{1,0:T(8,128)(2,1)S(1)} %pad_maximum_fusion.refs_1_, f32[1,2048]{1,0:T(1,128)S(1)} %get-tuple-element.9.refs_2_, bf16[8,2048,384]{2,1,0:T(8,128)(2,1)S(1)} %copy-done, ...), custom_call_target="tpu_custom_call" | custom-call | flops 1207959552 | bytes 37748736 | tf_op jit(solution)/shard_map/experts/pallas_call | solution.py:321
  23.4 0.4 %collective-permute-start.5 = (bf16[16,2048]{1,0:T(8,128)(2,1)S(1)}, bf16[16,2048]{1,0:T(8,128)(2,1)S(1)}, u32[]{:S(2)}, u32[]{:S(2)}) collective-permute-start(bf16[16,2048]{1,0:T(8,128)(2,1)S(1)} %get-tuple-element.11), channel_id=1, source_target_pairs={{0,2},{2,0},{1,3},{3,1},{4,6},{6,4},{5,7},{7,5},{8,10},{10,8},{9,1... | collective-permute-start | bytes 196616 | tf_op jit(solution)/shard_map/ppermute | solution.py:37
  23.9 0.9 %collective-permute-done.5 = bf16[16,2048]{1,0:T(8,128)(2,1)S(1)} collective-permute-done((bf16[16,2048]{1,0:T(8,128)(2,1)S(1)}, bf16[16,2048]{1,0:T(8,128)(2,1)S(1)}, u32[]{:S(2)}, u32[]{:S(2)}) %collective-permute-start.5) | collective-permute-done | bytes 65568 | tf_op jit(solution)/shard_map/ppermute | solution.py:37
  24.8 0.6 %collective-permute-start.6 = (bf16[8,2048]{1,0:T(8,128)(2,1)S(1)}, bf16[8,2048]{1,0:T(8,128)(2,1)S(1)}, u32[]{:S(2)}, u32[]{:S(2)}) collective-permute-start(bf16[8,2048]{1,0:T(8,128)(2,1)S(1)} %get-tuple-element.13), channel_id=1, source_target_pairs={{0,4},{1,5},{2,10},{3,11},{4,0},{5,1},{6,14},{7,15},{8,12},{9,13},... | collective-permute-start | bytes 98312 | tf_op jit(solution)/shard_map/ppermute | solution.py:52
  25.4 1.0 %collective-permute-start.7 = (bf16[8,2048]{1,0:T(8,128)(2,1)S(1)}, bf16[8,2048]{1,0:T(8,128)(2,1)S(1)}, u32[]{:S(2)}, u32[]{:S(2)}) collective-permute-start(bf16[8,2048]{1,0:T(8,128)(2,1)S(1)} %get-tuple-element.12), channel_id=1, source_target_pairs={{0,1},{1,0},{2,14},{3,15},{4,5},{5,4},{6,10},{7,11},{8,9},{9,8},{1... | collective-permute-start | bytes 98312 | tf_op jit(solution)/shard_map/ppermute | solution.py:52
  26.4 2.3 %collective-permute-done.6 = bf16[8,2048]{1,0:T(8,128)(2,1)S(1)} collective-permute-done((bf16[8,2048]{1,0:T(8,128)(2,1)S(1)}, bf16[8,2048]{1,0:T(8,128)(2,1)S(1)}, u32[]{:S(2)}, u32[]{:S(2)}) %collective-permute-start.6) | collective-permute-done | bytes 32800 | tf_op jit(solution)/shard_map/ppermute | solution.py:52
  28.8 0.6 %collective-permute-done.7 = bf16[8,2048]{1,0:T(8,128)(2,1)S(1)} collective-permute-done((bf16[8,2048]{1,0:T(8,128)(2,1)S(1)}, bf16[8,2048]{1,0:T(8,128)(2,1)S(1)}, u32[]{:S(2)}, u32[]{:S(2)}) %collective-permute-start.7) | collective-permute-done | bytes 32800 | tf_op jit(solution)/shard_map/ppermute | solution.py:52
  29.4 2.0 %collective-permute-start.8 = (bf16[8,1024]{1,0:T(8,128)(2,1)S(1)}, bf16[8,1024]{1,0:T(8,128)(2,1)S(1)}, u32[]{:S(2)}, u32[]{:S(2)}) collective-permute-start(bf16[8,1024]{1,0:T(8,128)(2,1)S(1)} %select_convert_fusion), channel_id=1, source_target_pairs={{0,3},{1,2},{2,1},{3,0},{4,7},{5,6},{6,5},{7,4},{8,11},{9,10},{10,... | collective-permute-start | bytes 49160 | tf_op jit(solution)/shard_map/ppermute | solution.py:52
  31.4 1.4 %collective-permute-done.8 = bf16[8,1024]{1,0:T(8,128)(2,1)S(1)} collective-permute-done((bf16[8,1024]{1,0:T(8,128)(2,1)S(1)}, bf16[8,1024]{1,0:T(8,128)(2,1)S(1)}, u32[]{:S(2)}, u32[]{:S(2)}) %collective-permute-start.8) | collective-permute-done | bytes 16416 | tf_op jit(solution)/shard_map/ppermute | solution.py:52
  32.8 1.1 %collective-permute-start.9 = (bf16[8,1024]{1,0:T(8,128)(2,1)S(1)}, bf16[8,1024]{1,0:T(8,128)(2,1)S(1)}, u32[]{:S(2)}, u32[]{:S(2)}) collective-permute-start(bf16[8,1024]{1,0:T(8,128)(2,1)S(1)} %add_convert_fusion.2), channel_id=1, source_target_pairs={{0,2},{2,0},{1,3},{3,1},{4,6},{6,4},{5,7},{7,5},{8,10},{10,8},{9,1... | collective-permute-start | bytes 49160 | tf_op jit(solution)/shard_map/ppermute | solution.py:37
  33.9 0.6 %take.1 = f32[8,1024]{1,0:T(8,128)} custom-call(f32[8,2048]{1,0:T(8,128)S(1)} %get-tuple-element.15.stream), custom_call_target="tpu_custom_call" | custom-call | flops 10000 | bytes 100000 | tf_op jit(solution)/shard_map/take/pallas_call | solution.py:421
  34.5 0.2 collective-permute-done.9
  34.7 0.6 %add_convert_fusion.1 = bf16[8,1024]{1,0:T(8,128)(2,1)} fusion(bf16[8,1024]{1,0:T(8,128)(2,1)S(1)} %collective-permute-done.9, bf16[8,1024]{1,0:T(8,128)(2,1)S(1)} %add_convert_fusion.2), kind=kLoop, calls=%fused_computation.6 | loop fusion | flops 32768 | bytes 49152 | tf_op jit(solution)/shard_map/convert_element_type | solution.py:440
  (10 shorter events, 0.1 us)
Async XLA Ops:
  0.6 17.5 %copy-start = (bf16[8,2048,384]{2,1,0:T(8,128)(2,1)S(1)}, bf16[8,2048,384]{2,1,0:T(8,128)(2,1)}, u32[]{:S(2)}) copy-start(bf16[8,2048,384]{2,1,0:T(8,128)(2,1)} %refs_3_.1) | copy-start | bytes 37748740
  0.6 17.5 %copy-start.1 = (bf16[8,2048,384]{2,1,0:T(8,128)(2,1)S(1)}, bf16[8,2048,384]{2,1,0:T(8,128)(2,1)}, u32[]{:S(2)}) copy-start(bf16[8,2048,384]{2,1,0:T(8,128)(2,1)} %refs_4_.1) | copy-start | bytes 37748740
  0.7 17.5 %copy-start.2 = (bf16[8,384,2048]{2,1,0:T(8,128)(2,1)S(1)}, bf16[8,384,2048]{2,1,0:T(8,128)(2,1)}, u32[]{:S(2)}) copy-start(bf16[8,384,2048]{2,1,0:T(8,128)(2,1)} %refs_5_.1) | copy-start | bytes 37748740
  3.8 1.4 %collective-permute-start = (bf16[8,2048]{1,0:T(8,128)(2,1)S(1)}, bf16[8,2048]{1,0:T(8,128)(2,1)S(1)}, u32[]{:S(2)}, u32[]{:S(2)}) collective-permute-start(bf16[8,2048]{1,0:T(8,128)(2,1)S(1)} %get-tuple-element.7.mine), channel_id=1, source_target_pairs={{0,2},{2,0},{1,3},{3,1},{4,6},{6,4},{5,7},{7,5},{8,10},{10,8},{9,1... | collective-permute-start | bytes 98312 | tf_op jit(solution)/shard_map/ppermute | solution.py:37
  5.2 4.3 %collective-permute-start.1 = (bf16[8,2048]{1,0:T(8,128)(2,1)S(1)}, bf16[8,2048]{1,0:T(8,128)(2,1)S(1)}, u32[]{:S(2)}, u32[]{:S(2)}) collective-permute-start(bf16[8,2048]{1,0:T(8,128)(2,1)S(1)} %side_sum.1), channel_id=1, source_target_pairs={{0,3},{1,2},{2,1},{3,0},{4,7},{5,6},{6,5},{7,4},{8,11},{9,10},{10,... | collective-permute-start | bytes 98312 | tf_op jit(solution)/shard_map/ppermute | solution.py:52
  9.5 4.0 %collective-permute-start.3 = (bf16[8,2176]{1,0:T(8,128)(2,1)S(1)}, bf16[8,2176]{1,0:T(8,128)(2,1)S(1)}, u32[]{:S(2)}, u32[]{:S(2)}) collective-permute-start(bf16[8,2176]{1,0:T(8,128)(2,1)S(1)} %pad_maximum_fusion.2.refs_0_), channel_id=1, source_target_pairs={{0,1},{1,0},{2,14},{3,15},{4,5},{5,4},{6,10},{7,11},{8,9},{9,8},{1... | collective-permute-start | bytes 104456 | tf_op jit(solution)/shard_map/ppermute | solution.py:52
  11.5 3.9 %collective-permute-start.2 = (bf16[8,2176]{1,0:T(8,128)(2,1)S(1)}, bf16[8,2176]{1,0:T(8,128)(2,1)S(1)}, u32[]{:S(2)}, u32[]{:S(2)}) collective-permute-start(bf16[8,2176]{1,0:T(8,128)(2,1)S(1)} %pad_maximum_fusion.2.refs_0_), channel_id=1, source_target_pairs={{0,4},{1,5},{2,10},{3,11},{4,0},{5,1},{6,14},{7,15},{8,12},{9,13},... | collective-permute-start | bytes 104456 | tf_op jit(solution)/shard_map/ppermute | solution.py:52
  15.5 2.7 %collective-permute-start.4 = (bf16[16,2176]{1,0:T(8,128)(2,1)S(1)}, bf16[16,2176]{1,0:T(8,128)(2,1)S(1)}, u32[]{:S(2)}, u32[]{:S(2)}) collective-permute-start(bf16[16,2176]{1,0:T(8,128)(2,1)S(1)} %pad_maximum_fusion.1), channel_id=1, source_target_pairs={{0,2},{2,0},{1,3},{3,1},{4,6},{6,4},{5,7},{7,5},{8,10},{10,8},{9,1... | collective-permute-start | bytes 208904 | tf_op jit(solution)/shard_map/ppermute | solution.py:37
  23.4 1.3 %collective-permute-start.5 = (bf16[16,2048]{1,0:T(8,128)(2,1)S(1)}, bf16[16,2048]{1,0:T(8,128)(2,1)S(1)}, u32[]{:S(2)}, u32[]{:S(2)}) collective-permute-start(bf16[16,2048]{1,0:T(8,128)(2,1)S(1)} %get-tuple-element.11), channel_id=1, source_target_pairs={{0,2},{2,0},{1,3},{3,1},{4,6},{6,4},{5,7},{7,5},{8,10},{10,8},{9,1... | collective-permute-start | bytes 196616 | tf_op jit(solution)/shard_map/ppermute | solution.py:37
  24.8 4.0 %collective-permute-start.6 = (bf16[8,2048]{1,0:T(8,128)(2,1)S(1)}, bf16[8,2048]{1,0:T(8,128)(2,1)S(1)}, u32[]{:S(2)}, u32[]{:S(2)}) collective-permute-start(bf16[8,2048]{1,0:T(8,128)(2,1)S(1)} %get-tuple-element.13), channel_id=1, source_target_pairs={{0,4},{1,5},{2,10},{3,11},{4,0},{5,1},{6,14},{7,15},{8,12},{9,13},... | collective-permute-start | bytes 98312 | tf_op jit(solution)/shard_map/ppermute | solution.py:52
  25.4 3.9 %collective-permute-start.7 = (bf16[8,2048]{1,0:T(8,128)(2,1)S(1)}, bf16[8,2048]{1,0:T(8,128)(2,1)S(1)}, u32[]{:S(2)}, u32[]{:S(2)}) collective-permute-start(bf16[8,2048]{1,0:T(8,128)(2,1)S(1)} %get-tuple-element.12), channel_id=1, source_target_pairs={{0,1},{1,0},{2,14},{3,15},{4,5},{5,4},{6,10},{7,11},{8,9},{9,8},{1... | collective-permute-start | bytes 98312 | tf_op jit(solution)/shard_map/ppermute | solution.py:52
  29.4 3.4 %collective-permute-start.8 = (bf16[8,1024]{1,0:T(8,128)(2,1)S(1)}, bf16[8,1024]{1,0:T(8,128)(2,1)S(1)}, u32[]{:S(2)}, u32[]{:S(2)}) collective-permute-start(bf16[8,1024]{1,0:T(8,128)(2,1)S(1)} %select_convert_fusion), channel_id=1, source_target_pairs={{0,3},{1,2},{2,1},{3,0},{4,7},{5,6},{6,5},{7,4},{8,11},{9,10},{10,... | collective-permute-start | bytes 49160 | tf_op jit(solution)/shard_map/ppermute | solution.py:52
  32.8 1.9 %collective-permute-start.9 = (bf16[8,1024]{1,0:T(8,128)(2,1)S(1)}, bf16[8,1024]{1,0:T(8,128)(2,1)S(1)}, u32[]{:S(2)}, u32[]{:S(2)}) collective-permute-start(bf16[8,1024]{1,0:T(8,128)(2,1)S(1)} %add_convert_fusion.2), channel_id=1, source_target_pairs={{0,2},{2,0},{1,3},{3,1},{4,6},{6,4},{5,7},{7,5},{8,10},{10,8},{9,1... | collective-permute-start | bytes 49160 | tf_op jit(solution)/shard_map/ppermute | solution.py:37
